TPU v7x, 32 devices: a whole 2x2x4 slice. The times are simulated.
32 devices in a mesh: row: 4 (over z), col: 4 (over x, core), tm: 2 (over y).
Axes of the slice: x: 2, y: 2, z: 4, core: 2. Of those that a mesh axis runs over, the one named last changes fastest.
Arguments:
- samples: bfloat16 [1024, 4, 2, 16384], P('row', None, 'tm', 'col'), may hold values from -6 to 6
- whitening: bfloat16 [1024, 1024], replicated, may hold values from -0.1875 to 0.1875
- ridge: float32 [2048], P('col'), may hold values from 2 to 20
- slab_start: int32 [1], replicated, may hold values from 0 to 63
- panels: int32 [4], replicated, may hold values from 0 to 3, as said below
Outputs:
- trailing: float32 [131072, 2048], P(('row', 'tm'), 'col')
- factor: bfloat16 [2, 131072, 512], P(None, ('row', 'tm'))
Inputs may be any that keep to these rules, and one draw needn't show every extreme that they name: `panels`: each panel index once.
All inputs are finite; a program needn't handle non-finite values.
Results may differ from a plain program's by a relative error of at most 0.012.
The roundings to bfloat16 on the way count: a program that leaves them out, or rounds other values in their place, can miss the bound.
Values may be sent and summed in bfloat16 or wider, within the bound.
A program may use at most 256 MiB of HBM per device.

v0:
```python
import functools
import math
import jax
import jax.numpy as jnp
from jax import lax
from jax.experimental import pallas as pl
from jax.experimental.pallas import tpu as pltpu
from jax.sharding import PartitionSpec as P

NB = 128
SUB = 8
HIGH = lax.Precision.HIGHEST
MESH = pl.DeviceIdType.MESH
NN = (((1,), (0,)), ((), ()))
NT = (((1,), (1,)), ((), ()))
TN = (((0,), (0,)), ((), ()))


def spread(x):
    return jnp.broadcast_to(x, (SUB, NB))


def block_inverse(a, held):
    n = NB // SUB
    rows = [a[s * SUB:(s + 1) * SUB, :] for s in range(n)]
    lane = lax.broadcasted_iota(jnp.int32, (SUB, NB), 1)
    sub = lax.broadcasted_iota(jnp.int32, (SUB, NB), 0)
    inv = [jnp.where(lane == sub + s * SUB, 1.0, 0.0).astype(jnp.float32) for s in range(n)]
    for p in range(n):
        for s in range(p, n):
            for c in range(SUB):
                held[p % 2, s, c] = spread(rows[s][:, p * SUB + c:p * SUB + c + 1])
        cols = {s: [held[p % 2, s, c] for c in range(SUB)] for s in range(p, n)}
        for c in range(SUB):
            over = 1.0 / spread(cols[p][c][c:c + 1, :])
            row, inverse = spread(rows[p][c:c + 1, :]), spread(inv[p][c:c + 1, :])
            heads = [spread(cols[p][d][c:c + 1, :]) for d in range(c + 1, SUB)]
            for s in range(p, n):
                m = cols[s][c] * over
                if s == p:
                    m = jnp.where(sub > c, m, 0.0)
                rows[s] = rows[s] - m * row
                inv[s] = inv[s] - m * inverse
                for d, head in zip(range(c + 1, SUB), heads):
                    cols[s][d] = cols[s][d] - m * head
    out = []
    for s in range(n):
        d = jnp.sum(jnp.where(lane == sub + s * SUB, rows[s], 0.0), axis=1, keepdims=True)
        out.append(inv[s] / jnp.sqrt(d))
    return jnp.concatenate(out, axis=0)


def invert(work, top, held):
    size = work.shape[0]
    blocks = size // NB

    def step(b, carry):
        at = pl.multiple_of(b * NB, NB)
        small = block_inverse(work[pl.ds(at, NB), pl.ds(at, NB)], held)
        top[...] = jnp.dot(small, work[pl.ds(at, NB), :], preferred_element_type=jnp.float32, precision=HIGH)
        work[pl.ds(at, NB), :] = top[...]

        def lower(c, carry):
            to = pl.multiple_of(c * NB, NB)
            work[pl.ds(to, NB), :] -= lax.dot_general(
                top[:, pl.ds(to, NB)], top[...], TN, preferred_element_type=jnp.float32, precision=HIGH)
            return carry

        return lax.fori_loop(b + 1, blocks, lower, carry)

    lax.fori_loop(0, blocks, step, 0)


def eye_mask(size):
    return lax.broadcasted_iota(jnp.int32, (size, size), 0) == lax.broadcasted_iota(jnp.int32, (size, size), 1)


def mm(a, b, dims=NN):
    return lax.dot_general(a, b, dims, preferred_element_type=jnp.float32)


def halves(a):
    hi = a.astype(jnp.bfloat16)
    return hi, (a - hi.astype(jnp.float32)).astype(jnp.bfloat16)


def mm2(a, b, dims=NN):
    hi, lo = halves(a)
    return mm(lo, b, dims) + mm(hi, b, dims)


def mm3(a, b, dims=NN):
    hi, lo = halves(a)
    bhi, blo = halves(b)
    return mm(lo, bhi, dims) + mm(hi, blo, dims) + mm(hi, bhi, dims)


def first_kernel(scale, info, s0_ref, r0_ref, i0_ref, work, top, held):
    size = s0_ref.shape[1]
    eye = eye_mask(size)
    work[:, :size] = mm(s0_ref[...], s0_ref[...], TN) * scale + jnp.where(eye, r0_ref[...], 0.0)
    work[:, size:] = jnp.where(eye, 1.0, 0.0)
    invert(work, top, held)
    i0_ref[...] = work[:, size:]


def second_kernel(scale, info, s0_ref, s1_ref, sj_ref, r0_ref, r1_ref, i0_ref, c01_ref, c0j_ref, i1_ref, work, top, held):
    size = s0_ref.shape[1]
    eye = eye_mask(size)
    i0 = i0_ref[...]
    c01 = mm3(i0, mm(s0_ref[...], s1_ref[...], TN) * scale).astype(jnp.bfloat16)
    c01_ref[...] = c01
    r0 = r0_ref[...] * (info[3] == 0).astype(jnp.float32)
    c0j_ref[...] = mm3(i0, mm(s0_ref[...], sj_ref[...], TN) * scale + jnp.where(eye, r0, 0.0)).astype(jnp.bfloat16)
    work[:, :size] = mm(s1_ref[...], s1_ref[...], TN) * scale + jnp.where(eye, r1_ref[...], 0.0) - mm(c01, c01, TN)
    work[:, size:] = jnp.where(eye, 1.0, 0.0)
    invert(work, top, held)
    i1_ref[...] = work[:, size:]


def third_kernel(
    scale, info, s0_ref, s1_ref, sj_ref, r0_ref, r1_ref, i0_ref, i1_ref, c01_ref, c0j_ref, w_ref, p_ref, d_ref
):
    size = s0_ref.shape[1]
    eye = eye_mask(size)
    live = (info[3] > 1).astype(jnp.float32)
    i0, i1, c01, c0j = i0_ref[...], i1_ref[...], c01_ref[...], c0j_ref[...]
    r1 = r1_ref[...]
    w = w_ref[...]
    p0 = mm3(mm(w, s0_ref[...], TN) * scale, i0, NT)
    p_ref[:, :size] = p0.astype(jnp.bfloat16)
    p1 = mm3(mm(w, s1_ref[...], TN) * scale - mm2(p0, c01), i1, NT)
    p_ref[:, size:2 * size] = p1.astype(jnp.bfloat16)
    own = r1 * (info[3] == 1).astype(jnp.float32)
    a1j = mm(s1_ref[...], sj_ref[...], TN) * scale + jnp.where(eye, own, 0.0) - mm(c01, c0j, TN)
    c1j = mm3(i1, a1j).astype(jnp.bfloat16)
    pn = mm(w, sj_ref[...], TN) * scale - mm2(p0, c0j) - mm2(p1, c1j)
    p_ref[:, 2 * size:] = (pn * live).astype(jnp.bfloat16)
    d00 = (i0 * r0_ref[...]).T
    d10 = mm3(-mm2(d00, c01), i1, NT)
    d11 = (i1 * r1).T
    d_ref[:size, :size] = d00
    d_ref[:size, size:2 * size] = d10
    d_ref[:size, 2 * size:] = (mm2(d00, c0j) + mm2(d10, c1j)) * -live
    d_ref[size:, :size] = jnp.zeros((size, size), jnp.float32)
    d_ref[size:, size:2 * size] = d11
    d_ref[size:, 2 * size:] = mm2(d11, c1j) * -live


def chain_call(kernel, info, operands, specs, outs, scratch, flops, name):
    def spec(x, pick, width):
        if pick is None:
            return pl.BlockSpec(x.shape, lambda i, info: (0, 0))
        return pl.BlockSpec((x.shape[0], width), lambda i, info: (0, info[pick]))

    width = outs[0].shape[-1] if name != "third" else outs[0].shape[-1] // 3
    return pl.pallas_call(
        kernel,
        grid_spec=pltpu.PrefetchScalarGridSpec(
            num_scalar_prefetch=1,
            grid=(1,),
            in_specs=[spec(x, p, width) for x, p in zip(operands, specs)],
            out_specs=[pl.BlockSpec(o.shape, lambda i, info: (0, 0)) for o in outs],
            scratch_shapes=scratch,
        ),
        out_shape=outs,
        compiler_params=pltpu.CompilerParams(vmem_limit_bytes=60 * 2**20),
        cost_estimate=pl.CostEstimate(flops=flops, bytes_accessed=8 * 2**20, transcendentals=0),
    )(info, *operands)


def gather_kernel(
    row_n, col_n, tm_n, part, ridge, w, out, ridges, summed, series,
    sum_send, sum_recv, row_send, row_recv, far_send, far_recv, near_send, near_recv, r_send, r_recv,
):
    row, col, tm = lax.axis_index("row"), lax.axis_index("col"), lax.axis_index("tm")
    plane = col_n * tm_n
    me = col * tm_n + tm
    times = part.shape[0]
    share = out.shape[1] // plane
    wide = share // 2

    def member(distance):
        other = lax.rem(me + distance, plane)
        return {"col": other // tm_n, "tm": lax.rem(other, tm_n)}

    def columns(owner, h):
        return pl.ds(pl.multiple_of(owner * share + h * wide, wide), wide)

    barrier = pltpu.get_barrier_semaphore()
    for d in range(1, plane):
        pl.semaphore_signal(barrier, inc=1, device_id=member(d), device_id_type=MESH)
    for d in range(1, row_n):
        pl.semaphore_signal(barrier, inc=1, device_id={"row": lax.rem(row + d, row_n)}, device_id_type=MESH)
    pl.semaphore_wait(barrier, plane + row_n - 2)

    def remote(src, dst, send, recv, to):
        return pltpu.make_async_remote_copy(
            src_ref=src, dst_ref=dst, send_sem=send, recv_sem=recv, device_id=to, device_id_type=MESH)

    def sum_copy(h, d):
        return remote(part.at[:, columns(lax.rem(me + d, plane), h)], summed.at[h, d - 1],
                      sum_send.at[h, d - 1], sum_recv.at[h, d - 1], member(d))

    def row_copy(h, d):
        return remote(series.at[h, pl.ds(0, times)], series.at[h, pl.ds(d * times, times)],
                      row_send.at[h, d - 1], row_recv.at[h, d - 1], {"row": lax.rem(row + d, row_n)})

    steps = [(a, b) for a in range(0, col_n, 2) for b in range(tm_n)]

    def origin(e):
        return lax.rem(col - steps[e][0] + col_n, col_n) * tm_n + lax.rem(tm - steps[e][1] + tm_n, tm_n)

    def far_copy(h, e):
        to = {"col": lax.rem(col + steps[e][0], col_n), "tm": lax.rem(tm + steps[e][1], tm_n)}
        at = columns(me, h)
        return remote(out.at[:, at], out.at[:, at], far_send.at[h, e - 1], far_recv.at[h, e - 1], to)

    def near_copy(h, e):
        at = columns(origin(e), h)
        return remote(out.at[:, at], out.at[:, at], near_send.at[h, e], near_recv.at[h, e],
                      {"col": col + 1 - 2 * lax.rem(col, 2)})

    def ridge_copy(d):
        return remote(ridge, ridges.at[col], r_send.at[d - 1], r_recv.at[d - 1], {"col": lax.rem(col + d, col_n)})

    started = []

    def start(copy):
        copy.start()
        started.append(copy)

    for h in range(2):
        for d in range(1, plane):
            start(sum_copy(h, d))
    for d in range(1, col_n):
        start(ridge_copy(d))
    ridges[col] = ridge[...]
    for h in range(2):
        total = part[:, columns(me, h)].astype(jnp.float32)
        for d in range(1, plane):
            sum_copy(h, d).wait_recv()
            total = total + summed[h, d - 1].astype(jnp.float32)
        series[h, pl.ds(0, times)] = total.astype(jnp.bfloat16)
        for d in range(1, row_n):
            start(row_copy(h, d))
    for h in range(2):
        for d in range(1, row_n):
            row_copy(h, d).wait_recv()
        out[:, columns(me, h)] = mm(w[...], series[h]).astype(jnp.bfloat16)
        for e in range(1, len(steps)):
            start(far_copy(h, e))
        start(near_copy(h, 0))
    for h in range(2):
        for e in range(1, len(steps)):
            far_copy(h, e).wait_recv()
            start(near_copy(h, e))
    for d in range(1, col_n):
        ridge_copy(d).wait_recv()
    for h in range(2):
        for e in range(len(steps)):
            near_copy(h, e).wait_recv()
    for copy in started:
        copy.wait_send()


def gather_slab(part, ridge, w, row_n, col_n, tm_n):
    times, slab = part.shape
    depth = w.shape[0]
    plane = col_n * tm_n
    wide = slab // plane // 2
    far = col_n // 2 * tm_n
    dma = pltpu.SemaphoreType.DMA
    vmem = pl.BlockSpec(memory_space=pltpu.VMEM)
    return pl.pallas_call(
        functools.partial(gather_kernel, row_n, col_n, tm_n),
        out_shape=[jax.ShapeDtypeStruct((depth, slab), jnp.bfloat16),
                   jax.ShapeDtypeStruct((col_n,) + ridge.shape, jnp.float32)],
        in_specs=[vmem] * 3,
        out_specs=[vmem] * 2,
        scratch_shapes=[
            pltpu.VMEM((2, plane - 1, times, wide), jnp.bfloat16),
            pltpu.VMEM((2, depth, wide), jnp.bfloat16),
            dma((2, plane - 1)), dma((2, plane - 1)), dma((2, row_n - 1)), dma((2, row_n - 1)),
            dma((2, far - 1)), dma((2, far - 1)), dma((2, far)), dma((2, far)),
            dma((col_n - 1,)), dma((col_n - 1,)),
        ],
        compiler_params=pltpu.CompilerParams(
            collective_id=1, has_side_effects=True, vmem_limit_bytes=40 * 2**20),
        cost_estimate=pl.CostEstimate(flops=40 * 10**9, bytes_accessed=2**20, transcendentals=0),
        name="gather_slab",
    )(part, ridge, w)


def split_kernel(rows, info, x_ref, *outs):
    for k in range(rows):
        @pl.when(info[0] == k)
        def _():
            for s, o in enumerate(outs):
                o[...] = x_ref[:, (k + s) % rows, :]


def split_blocks(row, x, first, w):
    times, rows, _ = x.shape
    bt = min(64, times)
    return pl.pallas_call(
        functools.partial(split_kernel, rows),
        grid_spec=pltpu.PrefetchScalarGridSpec(
            num_scalar_prefetch=1,
            grid=(times // bt,),
            in_specs=[pl.BlockSpec((bt, rows, w), lambda i, info: (i, 0, first // w))],
            out_specs=[pl.BlockSpec((bt, w), lambda i, info: (i, 0))] * rows,
        ),
        out_shape=[jax.ShapeDtypeStruct((times, w), x.dtype)] * rows,
        cost_estimate=pl.CostEstimate(flops=0, bytes_accessed=4 * times * rows * w * 2, transcendentals=0),
        name="split_blocks",
    )(row, x)


def final_body(chunk_base, info, own_ref, rest_ref, p_ref, d_ref, r_ref, *rest):
    t_ref, f_ref = rest[-2:]
    _, width = t_ref.shape
    times = own_ref.shape[1]
    acc = mm(own_ref[0], p_ref[:times, :], TN) + mm(rest_ref[0], p_ref[times:, :], TN)
    kind = kind_of(info, chunk_base(pl.program_id(0), pl.program_id(1)))

    def put(first, second, last):
        f_ref[0] = first.astype(f_ref.dtype)
        f_ref[1] = second.astype(f_ref.dtype)
        t_ref[...] = last

    @pl.when(kind < 2)
    def _():
        full = acc + d_ref[...]
        put(full[:, :width], full[:, width:2 * width], full[:, 2 * width:])

    @pl.when(kind == 2)
    def _():
        put(acc[:, :width], acc[:, width:2 * width],
            acc[:, 2 * width:] + jnp.where(eye_mask(width), r_ref[...], 0.0))

    @pl.when(kind > 2)
    def _():
        put(acc[:, :width], acc[:, width:2 * width], acc[:, 2 * width:])


def kind_of(info, block):
    at = block - info[4]
    inside = (at >= 0) & (at < info[5])
    kind = jnp.where(at == info[0], 0, jnp.where(at == info[1], 1, jnp.where(at == info[2], 2, 3)))
    return jnp.where(inside, kind, 3)


def final_chunk(info, own, others, weights, d, ridge, prior, chunk, chunks, width):
    cols, times, local = own.shape
    bm = width
    w = local // chunks
    per = w // bm
    rows = cols * local
    rest = others.shape[1]

    def base(c, i):
        return c * (local // bm) + chunk * per + i

    in_specs = [
        pl.BlockSpec((1, times, bm), lambda c, i, info: (c, 0, chunk * per + i)),
        pl.BlockSpec((1, rest, bm), lambda c, i, info: (c, 0, i)),
        pl.BlockSpec(weights.shape, lambda c, i, info: (0, 0)),
        pl.BlockSpec((bm, 3 * width), lambda c, i, info: (jnp.where(kind_of(info, base(c, i)) == 1, 1, 0), 0)),
        pl.BlockSpec((1, width), lambda c, i, info: (0, 0)),
    ]
    operands = [info, own, others, weights, d, ridge]
    aliases = {}
    if prior is not None:
        in_specs += [pl.BlockSpec(memory_space=pl.ANY)] * 2
        aliases = {len(operands): 0, len(operands) + 1: 1}
        operands += list(prior)
    return pl.pallas_call(
        functools.partial(final_body, base),
        grid_spec=pltpu.PrefetchScalarGridSpec(
            num_scalar_prefetch=1,
            grid=(cols, per),
            in_specs=in_specs,
            out_specs=[
                pl.BlockSpec((bm, width), lambda c, i, info: (base(c, i), 0)),
                pl.BlockSpec((2, bm, width), lambda c, i, info: (0, base(c, i), 0)),
            ],
        ),
        out_shape=[
            jax.ShapeDtypeStruct((rows, width), jnp.float32),
            jax.ShapeDtypeStruct((2, rows, width), jnp.bfloat16),
        ],
        input_output_aliases=aliases,
        compiler_params=pltpu.CompilerParams(
            vmem_limit_bytes=48 * 2**20, dimension_semantics=("arbitrary", "arbitrary")
        ),
        cost_estimate=pl.CostEstimate(
            flops=2 * cols * w * (times + rest) * 3 * width, bytes_accessed=cols * w * 6 * 2**10, transcendentals=0),
        name="final",
    )(*operands)


def on_device(samples, whitening, ridge, slab_start, panels):
    times, groups, _, local = samples.shape
    rows = lax.axis_size("row")
    cols = lax.axis_size("col")
    tms = lax.axis_size("tm")
    width = ridge.shape[0]
    slab = width * cols
    kd = local * cols
    depth = whitening.shape[0]
    scale = 1.0 / math.sqrt(depth)
    me_col = lax.axis_index("col")
    me_tm = lax.axis_index("tm")
    me_row = lax.axis_index("row")

    first = slab_start[0] * slab
    group = first // (tms * kd)
    tm_owner = (first % (tms * kd)) // kd
    offset = first % kd

    mine = lax.dynamic_index_in_dim(samples[:, :, 0], group, 1, keepdims=False)
    pieces = []
    for p in range(cols):
        at = offset + p * width
        have = (me_tm == tm_owner) & (me_col == at // local)
        part = lax.dynamic_slice_in_dim(mine, at % local, width, 1)
        pieces.append(jnp.where(have, part, jnp.zeros_like(part)))
    part = jnp.concatenate(pieces, axis=1)
    order = (me_row - jnp.arange(rows)) % rows
    turned = jnp.take(whitening.reshape(depth, rows, times), order, axis=1).reshape(depth, depth)
    sw, ridges = gather_slab(part, jnp.broadcast_to(ridge, (SUB, width)), turned, rows, cols, tms)
    ridges = ridges[:, 0].reshape(1, slab)

    chunks = 4 if local >= 4096 else 2
    w = local // chunks
    flat = samples.reshape(times, groups, local)
    row_info, sw = lax.optimization_barrier((me_row.reshape(1).astype(jnp.int32), sw))
    blocks = [split_blocks(row_info, flat, c * w, w) for c in range(chunks)]
    blocks, sw = lax.optimization_barrier((blocks, sw))
    moved = []
    for c in range(chunks):
        moved.append([
            lax.ppermute(blocks[c][s], "row", [(i, (i + s) % rows) for i in range(rows)]) for s in range(1, rows)
        ])
    own = lax.all_gather(jnp.concatenate([b[0] for b in blocks], axis=1), "col", axis=0)
    others = []
    for m in moved:
        others.append(lax.all_gather(jnp.concatenate(m, axis=0), "col", axis=0))

    q0, q1 = panels[0], panels[1]
    owner = (me_row == group) & (me_tm == tm_owner)
    kind = jnp.where(me_col == q0, 0, jnp.where(me_col == q1, 1, 2))
    info = jnp.stack([
        q0, q1, me_col, kind, offset // width, jnp.where(owner, cols, 0),
    ]).astype(jnp.int32)
    square = jax.ShapeDtypeStruct((width, width), jnp.float32)
    coarse = jax.ShapeDtypeStruct((width, width), jnp.bfloat16)
    scratch = [pltpu.VMEM((width, 2 * width), jnp.float32), pltpu.VMEM((NB, 2 * width), jnp.float32),
               pltpu.VMEM((2, NB // SUB, SUB, SUB, NB), jnp.float32)]
    i0, = chain_call(
        functools.partial(first_kernel, scale), info, [sw, ridges], [0, 0], [square], scratch, 20 * 10**9, "first")
    c01, c0j, i1 = chain_call(
        functools.partial(second_kernel, scale), info, [sw, sw, sw, ridges, ridges, i0], [0, 1, 2, 0, 1, None],
        [coarse, coarse, square], scratch, 24 * 10**9, "second")
    weights, d = chain_call(
        functools.partial(third_kernel, scale), info,
        [sw, sw, sw, ridges, ridges, i0, i1, c01, c0j, turned], [0, 1, 2, 0, 1, None, None, None, None, None],
        [jax.ShapeDtypeStruct((depth, 3 * width), jnp.bfloat16), jax.ShapeDtypeStruct((2 * width, 3 * width), jnp.float32)],
        [], 15 * 10**9, "third")
    own_ridge = ridge.reshape(1, width) * (kind == 2).astype(jnp.float32)

    prior = None
    for c in range(chunks):
        prior = final_chunk(info, own, others[c], weights, d, own_ridge, prior, c, chunks, width)
    return tuple(prior)


def solution(mesh):
    in_specs = (P("row", None, "tm", "col"), P(), P("col"), P(), P())
    out_specs = (P(("row", "tm"), "col"), P(None, ("row", "tm"), None))
    return jax.shard_map(on_device, mesh=mesh, in_specs=in_specs, out_specs=out_specs, check_vma=False)
```

profile of v0, /device:TPU:30, one launch (start us, length us, event | category | flops | bytes accessed | tf_op | source)
XLA Modules:
  0.0 476.9 jit_solution(11235660511288433743)
XLA Ops:
  7.2 0.0 all-gather.19.cloned.1.call-start
  8.2 3.9 copy.26
  12.2 2.8 copy.27
  15.0 2.0 gather_fusion
  17.0 1.9 copy.33
  18.9 0.1 broadcast_in_dim.18
  19.0 0.2 broadcast_select_fusion.w.w_ref
  19.2 7.2 %constant_dynamic-slice_fusion.3 = (bf16[256,1,1,512]{3,1,2,0:T(2,128)(2,1)S(1)}, bf16[256,1,1,512]{3,1,2,0:T(2,128)(2,1)S(1)}, bf16[256,1,1,512]{3,1,2,0:T(2,128)(2,1)S(1)}, bf16[256,1,1,512]{3,1,2,0:T(2,128)(2,1)S(1)}) fusion(bf16[256,4,1,4096]{3,1,2,0:T(4,128)(2,1)} %param.5, s32[]{:T(128)S(6)} %select_n.173, s32[]{:T(128)S(6)} %select_n.176, ...), kind=kLoop, calls=%fused_computation.30 | loop fusion | bytes 2097172 | tf_op jit(solution)/shard_map/dynamic_slice | solution.py:427
  26.4 0.1 fusion.2
  26.5 0.1 fusion
  26.6 0.1 pad_maximum_fusion.5.part
  26.7 0.5 copy-done.9
  27.2 42.3 %gather_slab.1 = (bf16[1024,2048]{1,0:T(8,128)(2,1)S(1)}, f32[4,8,512]{2,1,0:T(8,128)S(1)}) custom-call(bf16[256,2048]{1,0:T(8,128)(2,1)S(1)} %pad_maximum_fusion.5.part, f32[8,512]{1,0:T(8,128)S(1)} %broadcast_in_dim.17.ridge, bf16[1024,1024]{1,0:T(8,128)(2,1)S(1)} %broadcast_select_fusion.w.w_ref), custom_call_target="tpu_custom_call" | custom-call | flops 40000000000 | bytes 1048576 | tf_op jit(solution)/shard_map/gather_slab/pallas_call | solution.py:275
  69.5 2.0 copy-done.4
  71.5 6.2 %split_blocks.4 = (bf16[256,1024]{1,0:T(8,128)(2,1)}, bf16[256,1024]{1,0:T(8,128)(2,1)}, bf16[256,1024]{1,0:T(8,128)(2,1)}, bf16[256,1024]{1,0:T(8,128)(2,1)}) custom-call(s32[1]{0:T(128)} %bitcast.7.info, bf16[256,4,4096]{2,1,0:T(4,128)(2,1)} %bitcast.35), custom_call_target="tpu_custom_call" | custom-call | bytes 8388608 | tf_op jit(solution)/shard_map/split_blocks/pallas_call | solution.py:306
  77.7 6.5 %split_blocks.5 = (bf16[256,1024]{1,0:T(8,128)(2,1)}, bf16[256,1024]{1,0:T(8,128)(2,1)}, bf16[256,1024]{1,0:T(8,128)(2,1)}, bf16[256,1024]{1,0:T(8,128)(2,1)}) custom-call(s32[1]{0:T(128)} %bitcast.7.info, bf16[256,4,4096]{2,1,0:T(4,128)(2,1)} %bitcast.36), custom_call_target="tpu_custom_call" | custom-call | bytes 8388608 | tf_op jit(solution)/shard_map/split_blocks/pallas_call | solution.py:306
  84.2 6.2 %split_blocks.6 = (bf16[256,1024]{1,0:T(8,128)(2,1)}, bf16[256,1024]{1,0:T(8,128)(2,1)}, bf16[256,1024]{1,0:T(8,128)(2,1)}, bf16[256,1024]{1,0:T(8,128)(2,1)}) custom-call(s32[1]{0:T(128)} %bitcast.7.info, bf16[256,4,4096]{2,1,0:T(4,128)(2,1)} %bitcast.37), custom_call_target="tpu_custom_call" | custom-call | bytes 8388608 | tf_op jit(solution)/shard_map/split_blocks/pallas_call | solution.py:306
  90.4 6.2 %split_blocks.7 = (bf16[256,1024]{1,0:T(8,128)(2,1)}, bf16[256,1024]{1,0:T(8,128)(2,1)}, bf16[256,1024]{1,0:T(8,128)(2,1)}, bf16[256,1024]{1,0:T(8,128)(2,1)}) custom-call(s32[1]{0:T(128)} %bitcast.7.info, bf16[256,4,4096]{2,1,0:T(4,128)(2,1)} %bitcast.38), custom_call_target="tpu_custom_call" | custom-call | bytes 8388608 | tf_op jit(solution)/shard_map/split_blocks/pallas_call | solution.py:306
  96.6 1.6 collective-permute-start.10
  98.2 1.6 collective-permute-start.11
  99.8 2.3 collective-permute-start.9
  102.0 33.1 %collective-permute-done.10 = bf16[256,1024]{1,0:T(8,128)(2,1)S(1)} collective-permute-done((bf16[256,1024]{1,0:T(8,128)(2,1)}, bf16[256,1024]{1,0:T(8,128)(2,1)S(1)}, u32[]{:S(2)}, u32[]{:S(2)}) %collective-permute-start.10) | collective-permute-done | bytes 524320 | tf_op jit(solution)/shard_map/ppermute | solution.py:444
  135.1 0.3 collective-permute-done.9
  135.4 1.3 pad_maximum_fusion.4
  136.7 0.0 all-gather.19.cloned.1.call-update
  136.7 0.0 all-gather.11.cloned.1.call-start
  136.8 1.5 pad_maximum_fusion
  138.3 0.0 all-gather.11.cloned.1.call-update
  138.3 0.0 all-gather.17.cloned.1.call-start
  138.4 0.9 copy-done.19
  139.3 1.7 collective-permute-start.6
  141.0 21.6 %collective-permute-start.7 = (bf16[256,1024]{1,0:T(8,128)(2,1)S(1)}, bf16[256,1024]{1,0:T(8,128)(2,1)S(1)}, u32[]{:S(2)}, u32[]{:S(2)}) collective-permute-start(bf16[256,1024]{1,0:T(8,128)(2,1)S(1)} %copy-done.18), channel_id=1, source_target_pairs={{0,16},{8,24},{16,0},{24,8},{1,17},{9,25},{17,1},{25,9},{2,18},{10... | collective-permute-start | bytes 1572872 | tf_op jit(solution)/shard_map/ppermute | solution.py:444
  162.6 1.9 collective-permute-start.8
  164.5 8.2 %collective-permute-done.6 = bf16[256,1024]{1,0:T(8,128)(2,1)S(1)} collective-permute-done((bf16[256,1024]{1,0:T(8,128)(2,1)S(1)}, bf16[256,1024]{1,0:T(8,128)(2,1)S(1)}, u32[]{:S(2)}, u32[]{:S(2)}) %collective-permute-start.6) | collective-permute-done | bytes 524320 | tf_op jit(solution)/shard_map/ppermute | solution.py:444
  172.7 35.6 %collective-permute-done.7 = bf16[256,1024]{1,0:T(8,128)(2,1)S(1)} collective-permute-done((bf16[256,1024]{1,0:T(8,128)(2,1)S(1)}, bf16[256,1024]{1,0:T(8,128)(2,1)S(1)}, u32[]{:S(2)}, u32[]{:S(2)}) %collective-permute-start.7) | collective-permute-done | bytes 524320 | tf_op jit(solution)/shard_map/ppermute | solution.py:444
  208.3 1.3 pad_maximum_fusion.3
  209.6 0.0 all-gather.17.cloned.1.call-update
  209.6 0.0 all-gather.15.cloned.1.call-start
  209.7 0.1 collective-permute-start.3
  209.8 0.1 collective-permute-start.4
  209.9 2.0 collective-permute-start.5
  211.8 12.5 %collective-permute-done.3 = bf16[256,1024]{1,0:T(8,128)(2,1)S(1)} collective-permute-done((bf16[256,1024]{1,0:T(8,128)(2,1)S(1)}, bf16[256,1024]{1,0:T(8,128)(2,1)S(1)}, u32[]{:S(2)}, u32[]{:S(2)}) %collective-permute-start.3) | collective-permute-done | bytes 524320 | tf_op jit(solution)/shard_map/ppermute | solution.py:444
  224.3 30.2 %collective-permute-done.4 = bf16[256,1024]{1,0:T(8,128)(2,1)S(1)} collective-permute-done((bf16[256,1024]{1,0:T(8,128)(2,1)S(1)}, bf16[256,1024]{1,0:T(8,128)(2,1)S(1)}, u32[]{:S(2)}, u32[]{:S(2)}) %collective-permute-start.4) | collective-permute-done | bytes 524320 | tf_op jit(solution)/shard_map/ppermute | solution.py:444
  254.6 1.3 pad_maximum_fusion.2
  255.9 0.0 all-gather.15.cloned.1.call-update
  255.9 0.0 all-gather.13.cloned.1.call-start
  256.0 0.1 collective-permute-start
  256.0 3.5 collective-permute-start.1
  259.5 1.9 collective-permute-start.2
  261.5 0.6 slice.15
  262.1 7.6 %collective-permute-done = bf16[256,1024]{1,0:T(8,128)(2,1)S(1)} collective-permute-done((bf16[256,1024]{1,0:T(8,128)(2,1)S(1)}, bf16[256,1024]{1,0:T(8,128)(2,1)S(1)}, u32[]{:S(2)}, u32[]{:S(2)}) %collective-permute-start) | collective-permute-done | bytes 524320 | tf_op jit(solution)/shard_map/ppermute | solution.py:444
  269.6 35.7 %collective-permute-done.1 = bf16[256,1024]{1,0:T(8,128)(2,1)S(1)} collective-permute-done((bf16[256,1024]{1,0:T(8,128)(2,1)S(1)}, bf16[256,1024]{1,0:T(8,128)(2,1)S(1)}, u32[]{:S(2)}, u32[]{:S(2)}) %collective-permute-start.1) | collective-permute-done | bytes 524320 | tf_op jit(solution)/shard_map/ppermute | solution.py:444
  305.4 1.3 pad_maximum_fusion.1
  306.6 0.0 all-gather.13.cloned.1.call-update
  306.7 0.6 fusion.7
  308.5 0.7 stack.19.info
  309.1 25.2 %shard_map.68.i0_ref = f32[512,512]{1,0:T(8,128)} custom-call(s32[6]{0:T(128)} %stack.19.info, bf16[1024,2048]{1,0:T(8,128)(2,1)} %copy-done.4, f32[1,2048]{1,0:T(1,128)} %bitcast.49), custom_call_target="tpu_custom_call" | custom-call | flops 20000000000 | bytes 8388608 | tf_op jit(solution)/shard_map/pallas_call | solution.py:157
  334.3 29.4 %shard_map.69 = (bf16[512,512]{1,0:T(8,128)(2,1)}, bf16[512,512]{1,0:T(8,128)(2,1)}, f32[512,512]{1,0:T(8,128)}) custom-call(s32[6]{0:T(128)} %stack.19.info, bf16[1024,2048]{1,0:T(8,128)(2,1)} %copy-done.4, bf16[1024,2048]{1,0:T(8,128)(2,1)} %copy-done.4, bf16[1024,2048]{1,0:T(8,128)(2,1)} %copy-done.4, f32[1,2048]{1,0:T(1,128)} %bitcast.50, ...), custom_call_target="tpu_custom_call" | custom-call | flops 24000000000 | bytes 8388608 | tf_op jit(solution)/shard_map/pallas_call | solution.py:157
  363.7 21.6 %shard_map.70 = (bf16[1024,1536]{1,0:T(8,128)(2,1)}, f32[1024,1536]{1,0:T(8,128)}) custom-call(s32[6]{0:T(128)} %stack.19.info, bf16[1024,2048]{1,0:T(8,128)(2,1)} %copy-done.4, bf16[1024,2048]{1,0:T(8,128)(2,1)} %copy-done.4, bf16[1024,2048]{1,0:T(8,128)(2,1)} %copy-done.4, f32[1,2048]{1,0:T(1,128)} %bitcast.52, f32[1,2048]{1,0:T(1,128)} %bitcast.53, ...), custom_call_target="tpu_custom_call" | custom-call | flops 15000000512 | bytes 8388608 | tf_op jit(solution)/shard_map/pallas_call | solution.py:157
  385.4 1.9 copy-done
  387.3 20.9 %final.4 = (f32[16384,512]{1,0:T(8,128)}, bf16[2,16384,512]{2,1,0:T(8,128)(2,1)}) custom-call(s32[6]{0:T(128)S(1)} %copy-done.3, bf16[4,256,4096]{2,1,0:T(8,128)(2,1)} %bitcast.39, bf16[4,768,1024]{2,1,0:T(8,128)(2,1)} %bitcast.55, bf16[1024,1536]{1,0:T(8,128)(2,1)S(1)} %copy-done, f32[1024,1536]{1,0:T(8,128)} %get-tuple-element.82.d_ref, f32[1,512]{1,0:T(1,128)S(1)} %bitcast.31), custom_call_target="tpu_custom_call" | custom-call | flops 12884901888 | bytes 25165824 | tf_op jit(solution)/shard_map/final/pallas_call | solution.py:378
  408.2 20.6 %final.5 = (f32[16384,512]{1,0:T(8,128)}, bf16[2,16384,512]{2,1,0:T(8,128)(2,1)}) custom-call(s32[6]{0:T(128)S(1)} %copy-done.3, bf16[4,256,4096]{2,1,0:T(8,128)(2,1)} %bitcast.40, bf16[4,768,1024]{2,1,0:T(8,128)(2,1)} %bitcast.46, bf16[1024,1536]{1,0:T(8,128)(2,1)S(1)} %copy-done.1, ...), custom_call_target="tpu_custom_call", output_to_operand_aliasing={{0}: (6, {}), {1}: (7, {})} | custom-call | flops 12884901888 | bytes 25165824 | tf_op jit(solution)/shard_map/final/pallas_call | solution.py:378
  428.8 20.6 %final.6 = (f32[16384,512]{1,0:T(8,128)}, bf16[2,16384,512]{2,1,0:T(8,128)(2,1)}) custom-call(s32[6]{0:T(128)S(1)} %copy-done.3, bf16[4,256,4096]{2,1,0:T(8,128)(2,1)} %bitcast.41, bf16[4,768,1024]{2,1,0:T(8,128)(2,1)} %bitcast.47, bf16[1024,1536]{1,0:T(8,128)(2,1)S(1)} %copy-done.1, ...), custom_call_target="tpu_custom_call", output_to_operand_aliasing={{0}: (6, {}), {1}: (7, {})} | custom-call | flops 12884901888 | bytes 25165824 | tf_op jit(solution)/shard_map/final/pallas_call | solution.py:378
  449.4 20.6 %final.7 = (f32[16384,512]{1,0:T(8,128)}, bf16[2,16384,512]{2,1,0:T(8,128)(2,1)}) custom-call(s32[6]{0:T(128)S(1)} %copy-done.3, bf16[4,256,4096]{2,1,0:T(8,128)(2,1)} %bitcast.42, bf16[4,768,1024]{2,1,0:T(8,128)(2,1)} %bitcast.48, bf16[1024,1536]{1,0:T(8,128)(2,1)S(1)} %copy-done.1, ...), custom_call_target="tpu_custom_call", output_to_operand_aliasing={{0}: (6, {}), {1}: (7, {})} | custom-call | flops 12884901888 | bytes 25165824 | tf_op jit(solution)/shard_map/final/pallas_call | solution.py:378
  (55 shorter events, 0.2 us)
Async XLA Ops:
  7.2 378.2 %all-gather.19.cloned.1.call-start = ((), (), s32[]{:S(2)}) async-start(), calls=%async_computation.4 | async-start | bytes 7864320 | tf_op jit(solution)/shard_map/all_gather | solution.py:449
  19.2 8.0 %copy-start.2 = (bf16[1024,1024]{1,0:T(8,128)(2,1)}, bf16[1024,1024]{1,0:T(8,128)(2,1)S(1)}, u32[]{:S(2)}) copy-start(bf16[1024,1024]{1,0:T(8,128)(2,1)S(1)} %broadcast_select_fusion.w.w_ref) | copy-start | bytes 6291460
  26.5 0.7 copy-start.9
  69.5 2.0 copy-start.4
  90.4 7.8 %copy-start.21 = (bf16[256,1024]{1,0:T(8,128)(2,1)S(1)}, bf16[256,1024]{1,0:T(8,128)(2,1)}, u32[]{:S(2)}) copy-start(bf16[256,1024]{1,0:T(8,128)(2,1)} %get-tuple-element.91) | copy-start | bytes 1572868
  90.4 9.4 %copy-start.20 = (bf16[256,1024]{1,0:T(8,128)(2,1)S(1)}, bf16[256,1024]{1,0:T(8,128)(2,1)}, u32[]{:S(2)}) copy-start(bf16[256,1024]{1,0:T(8,128)(2,1)} %get-tuple-element.89) | copy-start | bytes 1572868
  96.6 40.2 %copy-start.5 = (bf16[256,1024]{1,0:T(8,128)(2,1)S(1)}, bf16[256,1024]{1,0:T(8,128)(2,1)}, u32[]{:S(2)}) copy-start(bf16[256,1024]{1,0:T(8,128)(2,1)} %get-tuple-element.69) | copy-start | bytes 1572868
  96.6 40.2 %copy-start.6 = (bf16[256,1024]{1,0:T(8,128)(2,1)S(1)}, bf16[256,1024]{1,0:T(8,128)(2,1)}, u32[]{:S(2)}) copy-start(bf16[256,1024]{1,0:T(8,128)(2,1)} %get-tuple-element.70) | copy-start | bytes 1572868
  96.6 40.2 %copy-start.7 = (bf16[256,1024]{1,0:T(8,128)(2,1)S(1)}, bf16[256,1024]{1,0:T(8,128)(2,1)}, u32[]{:S(2)}) copy-start(bf16[256,1024]{1,0:T(8,128)(2,1)} %get-tuple-element.71) | copy-start | bytes 1572868
  96.6 40.2 %copy-start.8 = (bf16[256,1024]{1,0:T(8,128)(2,1)S(1)}, bf16[256,1024]{1,0:T(8,128)(2,1)}, u32[]{:S(2)}) copy-start(bf16[256,1024]{1,0:T(8,128)(2,1)} %get-tuple-element.72) | copy-start | bytes 1572868
  96.6 38.5 %collective-permute-start.10 = (bf16[256,1024]{1,0:T(8,128)(2,1)}, bf16[256,1024]{1,0:T(8,128)(2,1)S(1)}, u32[]{:S(2)}, u32[]{:S(2)}) collective-permute-start(bf16[256,1024]{1,0:T(8,128)(2,1)} %get-tuple-element.90), channel_id=1, source_target_pairs={{0,16},{8,24},{16,0},{24,8},{1,17},{9,25},{17,1},{25,9},{2,18},{10... | collective-permute-start | bytes 1572872 | tf_op jit(solution)/shard_map/ppermute | solution.py:444
  98.2 36.9 %collective-permute-start.11 = (bf16[256,1024]{1,0:T(8,128)(2,1)S(1)}, bf16[256,1024]{1,0:T(8,128)(2,1)S(1)}, u32[]{:S(2)}, u32[]{:S(2)}) collective-permute-start(bf16[256,1024]{1,0:T(8,128)(2,1)S(1)} %copy-done.21), channel_id=1, source_target_pairs={{0,24},{8,0},{16,8},{24,16},{1,25},{9,1},{17,9},{25,17},{2,26},{10... | collective-permute-start | bytes 1572872 | tf_op jit(solution)/shard_map/ppermute | solution.py:444
  99.8 35.6 %collective-permute-start.9 = (bf16[256,1024]{1,0:T(8,128)(2,1)S(1)}, bf16[256,1024]{1,0:T(8,128)(2,1)S(1)}, u32[]{:S(2)}, u32[]{:S(2)}) collective-permute-start(bf16[256,1024]{1,0:T(8,128)(2,1)S(1)} %copy-done.20), channel_id=1, source_target_pairs={{0,8},{8,16},{16,24},{24,0},{1,9},{9,17},{17,25},{25,1},{2,10},{10... | collective-permute-start | bytes 1572872 | tf_op jit(solution)/shard_map/ppermute | solution.py:444
  136.7 248.6 %all-gather.11.cloned.1.call-start = ((), (), s32[]{:S(2)}) async-start(), calls=%async_computation | async-start | bytes 10485760 | tf_op jit(solution)/shard_map/all_gather | solution.py:446
  138.3 1.0 copy-start.19
  138.3 2.7 copy-start.18
  138.3 24.3 %copy-start.17 = (bf16[256,1024]{1,0:T(8,128)(2,1)S(1)}, bf16[256,1024]{1,0:T(8,128)(2,1)}, u32[]{:S(2)}) copy-start(bf16[256,1024]{1,0:T(8,128)(2,1)} %get-tuple-element.88) | copy-start | bytes 1572868
  138.3 71.4 %copy-start.16 = (bf16[256,1024]{1,0:T(8,128)(2,1)S(1)}, bf16[256,1024]{1,0:T(8,128)(2,1)}, u32[]{:S(2)}) copy-start(bf16[256,1024]{1,0:T(8,128)(2,1)} %get-tuple-element.83) | copy-start | bytes 1572868
  138.3 71.5 %copy-start.15 = (bf16[256,1024]{1,0:T(8,128)(2,1)S(1)}, bf16[256,1024]{1,0:T(8,128)(2,1)}, u32[]{:S(2)}) copy-start(bf16[256,1024]{1,0:T(8,128)(2,1)} %get-tuple-element.84) | copy-start | bytes 1572868
  138.3 71.5 %copy-start.14 = (bf16[256,1024]{1,0:T(8,128)(2,1)S(1)}, bf16[256,1024]{1,0:T(8,128)(2,1)}, u32[]{:S(2)}) copy-start(bf16[256,1024]{1,0:T(8,128)(2,1)} %get-tuple-element.85) | copy-start | bytes 1572868
  138.3 269.9 %all-gather.17.cloned.1.call-start = ((), (), s32[]{:S(2)}) async-start(), calls=%async_computation.3 | async-start | bytes 7864320 | tf_op jit(solution)/shard_map/all_gather | solution.py:449
  139.3 33.4 %collective-permute-start.6 = (bf16[256,1024]{1,0:T(8,128)(2,1)S(1)}, bf16[256,1024]{1,0:T(8,128)(2,1)S(1)}, u32[]{:S(2)}, u32[]{:S(2)}) collective-permute-start(bf16[256,1024]{1,0:T(8,128)(2,1)S(1)} %copy-done.19), channel_id=1, source_target_pairs={{0,8},{8,16},{16,24},{24,0},{1,9},{9,17},{17,25},{25,1},{2,10},{10... | collective-permute-start | bytes 1572872 | tf_op jit(solution)/shard_map/ppermute | solution.py:444
  141.0 67.3 %collective-permute-start.7 = (bf16[256,1024]{1,0:T(8,128)(2,1)S(1)}, bf16[256,1024]{1,0:T(8,128)(2,1)S(1)}, u32[]{:S(2)}, u32[]{:S(2)}) collective-permute-start(bf16[256,1024]{1,0:T(8,128)(2,1)S(1)} %copy-done.18), channel_id=1, source_target_pairs={{0,16},{8,24},{16,0},{24,8},{1,17},{9,25},{17,1},{25,9},{2,18},{10... | collective-permute-start | bytes 1572872 | tf_op jit(solution)/shard_map/ppermute | solution.py:444
  162.6 45.7 %collective-permute-start.8 = (bf16[256,1024]{1,0:T(8,128)(2,1)S(1)}, bf16[256,1024]{1,0:T(8,128)(2,1)S(1)}, u32[]{:S(2)}, u32[]{:S(2)}) collective-permute-start(bf16[256,1024]{1,0:T(8,128)(2,1)S(1)} %copy-done.17), channel_id=1, source_target_pairs={{0,24},{8,0},{16,8},{24,16},{1,25},{9,1},{17,9},{25,17},{2,26},{10... | collective-permute-start | bytes 1572872 | tf_op jit(solution)/shard_map/ppermute | solution.py:444
  209.6 46.3 %copy-start.13 = (bf16[256,1024]{1,0:T(8,128)(2,1)S(1)}, bf16[256,1024]{1,0:T(8,128)(2,1)}, u32[]{:S(2)}) copy-start(bf16[256,1024]{1,0:T(8,128)(2,1)} %get-tuple-element.73) | copy-start | bytes 1572868
  209.6 46.4 %copy-start.12 = (bf16[256,1024]{1,0:T(8,128)(2,1)S(1)}, bf16[256,1024]{1,0:T(8,128)(2,1)}, u32[]{:S(2)}) copy-start(bf16[256,1024]{1,0:T(8,128)(2,1)} %get-tuple-element.74) | copy-start | bytes 1572868
  209.6 49.9 %copy-start.11 = (bf16[256,1024]{1,0:T(8,128)(2,1)S(1)}, bf16[256,1024]{1,0:T(8,128)(2,1)}, u32[]{:S(2)}) copy-start(bf16[256,1024]{1,0:T(8,128)(2,1)} %get-tuple-element.75) | copy-start | bytes 1572868
  209.6 219.2 %all-gather.15.cloned.1.call-start = ((), (), s32[]{:S(2)}) async-start(), calls=%async_computation.2 | async-start | bytes 7864320 | tf_op jit(solution)/shard_map/all_gather | solution.py:449
  209.7 14.6 %collective-permute-start.3 = (bf16[256,1024]{1,0:T(8,128)(2,1)S(1)}, bf16[256,1024]{1,0:T(8,128)(2,1)S(1)}, u32[]{:S(2)}, u32[]{:S(2)}) collective-permute-start(bf16[256,1024]{1,0:T(8,128)(2,1)S(1)} %copy-done.16), channel_id=1, source_target_pairs={{0,8},{8,16},{16,24},{24,0},{1,9},{9,17},{17,25},{25,1},{2,10},{10... | collective-permute-start | bytes 1572872 | tf_op jit(solution)/shard_map/ppermute | solution.py:444
  209.8 44.8 %collective-permute-start.4 = (bf16[256,1024]{1,0:T(8,128)(2,1)S(1)}, bf16[256,1024]{1,0:T(8,128)(2,1)S(1)}, u32[]{:S(2)}, u32[]{:S(2)}) collective-permute-start(bf16[256,1024]{1,0:T(8,128)(2,1)S(1)} %copy-done.15), channel_id=1, source_target_pairs={{0,16},{8,24},{16,0},{24,8},{1,17},{9,25},{17,1},{25,9},{2,18},{10... | collective-permute-start | bytes 1572872 | tf_op jit(solution)/shard_map/ppermute | solution.py:444
  209.9 44.7 %collective-permute-start.5 = (bf16[256,1024]{1,0:T(8,128)(2,1)S(1)}, bf16[256,1024]{1,0:T(8,128)(2,1)S(1)}, u32[]{:S(2)}, u32[]{:S(2)}) collective-permute-start(bf16[256,1024]{1,0:T(8,128)(2,1)S(1)} %copy-done.14), channel_id=1, source_target_pairs={{0,24},{8,0},{16,8},{24,16},{1,25},{9,1},{17,9},{25,17},{2,26},{10... | collective-permute-start | bytes 1572872 | tf_op jit(solution)/shard_map/ppermute | solution.py:444
  255.9 193.5 %all-gather.13.cloned.1.call-start = ((), (), s32[]{:S(2)}) async-start(), calls=%async_computation.1 | async-start | bytes 7864320 | tf_op jit(solution)/shard_map/all_gather | solution.py:449
  256.0 13.7 %collective-permute-start = (bf16[256,1024]{1,0:T(8,128)(2,1)S(1)}, bf16[256,1024]{1,0:T(8,128)(2,1)S(1)}, u32[]{:S(2)}, u32[]{:S(2)}) collective-permute-start(bf16[256,1024]{1,0:T(8,128)(2,1)S(1)} %copy-done.13), channel_id=1, source_target_pairs={{0,8},{8,16},{16,24},{24,0},{1,9},{9,17},{17,25},{25,1},{2,10},{10... | collective-permute-start | bytes 1572872 | tf_op jit(solution)/shard_map/ppermute | solution.py:444
  256.0 49.3 %collective-permute-start.1 = (bf16[256,1024]{1,0:T(8,128)(2,1)S(1)}, bf16[256,1024]{1,0:T(8,128)(2,1)S(1)}, u32[]{:S(2)}, u32[]{:S(2)}) collective-permute-start(bf16[256,1024]{1,0:T(8,128)(2,1)S(1)} %copy-done.12), channel_id=1, source_target_pairs={{0,16},{8,24},{16,0},{24,8},{1,17},{9,25},{17,1},{25,9},{2,18},{10... | collective-permute-start | bytes 1572872 | tf_op jit(solution)/shard_map/ppermute | solution.py:444
  259.5 45.8 %collective-permute-start.2 = (bf16[256,1024]{1,0:T(8,128)(2,1)S(1)}, bf16[256,1024]{1,0:T(8,128)(2,1)S(1)}, u32[]{:S(2)}, u32[]{:S(2)}) collective-permute-start(bf16[256,1024]{1,0:T(8,128)(2,1)S(1)} %copy-done.11), channel_id=1, source_target_pairs={{0,24},{8,0},{16,8},{24,16},{1,25},{9,1},{17,9},{25,17},{2,26},{10... | collective-permute-start | bytes 1572872 | tf_op jit(solution)/shard_map/ppermute | solution.py:444
  262.1 44.6 %copy-start.10 = (s32[4]{0:T(128)S(1)}, s32[4]{0:T(128)}, u32[]{:S(2)}) copy-start(s32[4]{0:T(128)} %param.9) | copy-start | bytes 52
  363.7 21.7 %copy-start.3 = (s32[6]{0:T(128)S(1)}, s32[6]{0:T(128)}, u32[]{:S(2)}) copy-start(s32[6]{0:T(128)} %stack.19.info) | copy-start | bytes 76
  385.3 2.0 copy-start
  387.3 20.9 %copy-start.1 = (bf16[1024,1536]{1,0:T(8,128)(2,1)S(1)}, bf16[1024,1536]{1,0:T(8,128)(2,1)}, u32[]{:S(2)}) copy-start(bf16[1024,1536]{1,0:T(8,128)(2,1)} %get-tuple-element.81.p_ref) | copy-start | bytes 9437188
Sparse Core Ops, SparseCore 0:
  136.8 67.0 all-gather.18
  206.1 58.2 all-gather.10
  266.0 46.3 all-gather.16
  313.8 46.3 all-gather.14
  361.6 46.3 all-gather.12
where the time goes:
time: 486 us; the launch traced here: 477 us
  Pallas kernels  226 us (47%)
  waiting for transfers between devices  163 us (34%)
  starting transfers between devices  38.3 us (8%)
  local copies, waits for them, and re-layouts  25.2 us (5%)
  between operations  16.7 us (3%)
  other arithmetic  7.13 us (1%)
    ppermute x12, waiting for transfers between devices, on_device(): lax.ppermute(blocks[c][s], 'row', [(i, (i + s) % rows) for i in range(row...  163 us
    pallas_call x4, Pallas kernels, final_chunk(): pl.pallas_call(functools.partial(final_body, base), grid_spec=pltpu.Prefe...  82.6 us
    pallas_call x3, Pallas kernels, chain_call(): pl.pallas_call(kernel, grid_spec=pltpu.PrefetchScalarGridSpec(num_scalar_...  76.2 us
    pallas_call x1, Pallas kernels, gather_slab(): pl.pallas_call(functools.partial(gather_kernel, row_n, col_n, tm_n), out_...  42.3 us
    ppermute x12, starting transfers between devices, on_device(): lax.ppermute(blocks[c][s], 'row', [(i, (i + s) % rows) for i in range(row...  38.1 us
    pallas_call x4, Pallas kernels, split_blocks(): pl.pallas_call(functools.partial(split_kernel, rows), grid_spec=pltpu.Pre...  25.1 us
  transfers between devices with their start and end apart: 17, of which 8 were waited for; matrix products, arithmetic and copies ran while one was open for 2% of the time, Pallas kernels for 29%

commit v1 on v0

--- a/solution.py
+++ b/solution.py
@@ -119,7 +119,7 @@
 
 
 def third_kernel(
-    scale, info, s0_ref, s1_ref, sj_ref, r0_ref, r1_ref, i0_ref, i1_ref, c01_ref, c0j_ref, w_ref, p_ref, d_ref
+    scale, rows, info, s0_ref, s1_ref, sj_ref, r0_ref, r1_ref, i0_ref, i1_ref, c01_ref, c0j_ref, w_ref, p_ref, d_ref
 ):
     size = s0_ref.shape[1]
     eye = eye_mask(size)
@@ -127,15 +127,22 @@
     i0, i1, c01, c0j = i0_ref[...], i1_ref[...], c01_ref[...], c0j_ref[...]
     r1 = r1_ref[...]
     w = w_ref[...]
+    times = w.shape[0] // rows
+
+    def put(value, side):
+        for t in range(rows):
+            to = pl.multiple_of(lax.rem(info[6] - t + rows, rows) * times, times)
+            p_ref[pl.ds(to, times), side * size:(side + 1) * size] = value[t * times:(t + 1) * times].astype(jnp.bfloat16)
+
     p0 = mm3(mm(w, s0_ref[...], TN) * scale, i0, NT)
-    p_ref[:, :size] = p0.astype(jnp.bfloat16)
+    put(p0, 0)
     p1 = mm3(mm(w, s1_ref[...], TN) * scale - mm2(p0, c01), i1, NT)
-    p_ref[:, size:2 * size] = p1.astype(jnp.bfloat16)
+    put(p1, 1)
     own = r1 * (info[3] == 1).astype(jnp.float32)
     a1j = mm(s1_ref[...], sj_ref[...], TN) * scale + jnp.where(eye, own, 0.0) - mm(c01, c0j, TN)
     c1j = mm3(i1, a1j).astype(jnp.bfloat16)
     pn = mm(w, sj_ref[...], TN) * scale - mm2(p0, c0j) - mm2(p1, c1j)
-    p_ref[:, 2 * size:] = (pn * live).astype(jnp.bfloat16)
+    put(pn * live, 2)
     d00 = (i0 * r0_ref[...]).T
     d10 = mm3(-mm2(d00, c01), i1, NT)
     d11 = (i1 * r1).T
@@ -177,6 +184,7 @@
     plane = col_n * tm_n
     me = col * tm_n + tm
     times = part.shape[0]
+    here = pl.ds(pl.multiple_of(row * times, times), times)
     share = out.shape[1] // plane
     wide = share // 2
 
@@ -203,7 +211,7 @@
                       sum_send.at[h, d - 1], sum_recv.at[h, d - 1], member(d))
 
     def row_copy(h, d):
-        return remote(series.at[h, pl.ds(0, times)], series.at[h, pl.ds(d * times, times)],
+        return remote(series.at[h, here], series.at[h, here],
                       row_send.at[h, d - 1], row_recv.at[h, d - 1], {"row": lax.rem(row + d, row_n)})
 
     steps = [(a, b) for a in range(0, col_n, 2) for b in range(tm_n)]
@@ -241,7 +249,7 @@
         for d in range(1, plane):
             sum_copy(h, d).wait_recv()
             total = total + summed[h, d - 1].astype(jnp.float32)
-        series[h, pl.ds(0, times)] = total.astype(jnp.bfloat16)
+        series[h, here] = total.astype(jnp.bfloat16)
         for d in range(1, row_n):
             start(row_copy(h, d))
     for h in range(2):
@@ -297,7 +305,7 @@
         @pl.when(info[0] == k)
         def _():
             for s, o in enumerate(outs):
-                o[...] = x_ref[:, (k + s) % rows, :]
+                o[...] = x_ref[:, (k + s + 1) % rows, :]
 
 
 def split_blocks(row, x, first, w):
@@ -309,12 +317,42 @@
             num_scalar_prefetch=1,
             grid=(times // bt,),
             in_specs=[pl.BlockSpec((bt, rows, w), lambda i, info: (i, 0, first // w))],
-            out_specs=[pl.BlockSpec((bt, w), lambda i, info: (i, 0))] * rows,
+            out_specs=[pl.BlockSpec((bt, w), lambda i, info: (i, 0))] * (rows - 1),
         ),
-        out_shape=[jax.ShapeDtypeStruct((times, w), x.dtype)] * rows,
+        out_shape=[jax.ShapeDtypeStruct((times, w), x.dtype)] * (rows - 1),
         cost_estimate=pl.CostEstimate(flops=0, bytes_accessed=4 * times * rows * w * 2, transcendentals=0),
         name="split_blocks",
     )(row, x)
+
+
+def pick_kernel(rows, info, x_ref, o_ref):
+    keep = info[1 + pl.program_id(0)] > 0
+    for k in range(rows):
+        @pl.when(keep & (info[0] == k))
+        def _():
+            o_ref[...] = x_ref[:, k, :]
+
+    @pl.when(jnp.logical_not(keep))
+    def _():
+        o_ref[...] = jnp.zeros_like(o_ref)
+
+
+def pick_blocks(which, keep, at, x, wide):
+    times, rows, _ = x.shape
+    n = at.shape[0]
+    info = jnp.concatenate([which.reshape(1), keep, at]).astype(jnp.int32)
+    return pl.pallas_call(
+        functools.partial(pick_kernel, rows),
+        grid_spec=pltpu.PrefetchScalarGridSpec(
+            num_scalar_prefetch=1,
+            grid=(n,),
+            in_specs=[pl.BlockSpec((times, rows, wide), lambda p, info: (0, 0, info[1 + n + p]))],
+            out_specs=pl.BlockSpec((times, wide), lambda p, info: (0, p)),
+        ),
+        out_shape=jax.ShapeDtypeStruct((times, n * wide), x.dtype),
+        cost_estimate=pl.CostEstimate(flops=0, bytes_accessed=2 * times * rows * n * wide * 2, transcendentals=0),
+        name="pick_blocks",
+    )(info, x)
 
 
 def final_body(chunk_base, info, own_ref, rest_ref, p_ref, d_ref, r_ref, *rest):
@@ -351,19 +389,19 @@
     return jnp.where(inside, kind, 3)
 
 
-def final_chunk(info, own, others, weights, d, ridge, prior, chunk, chunks, width):
+def final_chunk(info, own, others, weights, d, ridge, prior, start, width):
     cols, times, local = own.shape
     bm = width
-    w = local // chunks
+    w = others.shape[2]
     per = w // bm
     rows = cols * local
     rest = others.shape[1]
 
     def base(c, i):
-        return c * (local // bm) + chunk * per + i
+        return c * (local // bm) + start // bm + i
 
     in_specs = [
-        pl.BlockSpec((1, times, bm), lambda c, i, info: (c, 0, chunk * per + i)),
+        pl.BlockSpec((1, times, bm), lambda c, i, info: (c, 0, start // bm + i)),
         pl.BlockSpec((1, rest, bm), lambda c, i, info: (c, 0, i)),
         pl.BlockSpec(weights.shape, lambda c, i, info: (0, 0)),
         pl.BlockSpec((bm, 3 * width), lambda c, i, info: (jnp.where(kind_of(info, base(c, i)) == 1, 1, 0), 0)),
@@ -419,40 +457,35 @@
     tm_owner = (first % (tms * kd)) // kd
     offset = first % kd
 
-    mine = lax.dynamic_index_in_dim(samples[:, :, 0], group, 1, keepdims=False)
-    pieces = []
-    for p in range(cols):
-        at = offset + p * width
-        have = (me_tm == tm_owner) & (me_col == at // local)
-        part = lax.dynamic_slice_in_dim(mine, at % local, width, 1)
-        pieces.append(jnp.where(have, part, jnp.zeros_like(part)))
-    part = jnp.concatenate(pieces, axis=1)
-    order = (me_row - jnp.arange(rows)) % rows
-    turned = jnp.take(whitening.reshape(depth, rows, times), order, axis=1).reshape(depth, depth)
-    sw, ridges = gather_slab(part, jnp.broadcast_to(ridge, (SUB, width)), turned, rows, cols, tms)
+    flat = samples.reshape(times, groups, local)
+    sizes = [local // 4] * 3 + [local // 8] * 2 if local >= 8 * width else [width] * (local // width)
+    starts = [sum(sizes[:c]) for c in range(len(sizes))]
+    row_info = me_row.reshape(1).astype(jnp.int32)
+    split = lambda row, c: split_blocks(row, flat, starts[c], sizes[c])
+    head = split(row_info, 0)
+    count = local // width
+    own = pick_blocks(me_row, jnp.ones((count,), jnp.int32), jnp.arange(count), flat, width)
+    at = offset + jnp.arange(cols) * width
+    have = (me_tm == tm_owner) & (me_col == at // local)
+    part = pick_blocks(group, have, at % local // width, flat, width)
+    part, head, own = lax.optimization_barrier((part, head, own))
+    own = lax.all_gather(own, "col", axis=0)
+    sw, ridges = gather_slab(part, jnp.broadcast_to(ridge, (SUB, width)), whitening, rows, cols, tms)
     ridges = ridges[:, 0].reshape(1, slab)
 
-    chunks = 4 if local >= 4096 else 2
-    w = local // chunks
-    flat = samples.reshape(times, groups, local)
-    row_info, sw = lax.optimization_barrier((me_row.reshape(1).astype(jnp.int32), sw))
-    blocks = [split_blocks(row_info, flat, c * w, w) for c in range(chunks)]
+    row_info, sw = lax.optimization_barrier((row_info, sw))
+    blocks = [split(row_info, c) for c in range(1, len(sizes))]
     blocks, sw = lax.optimization_barrier((blocks, sw))
-    moved = []
-    for c in range(chunks):
-        moved.append([
-            lax.ppermute(blocks[c][s], "row", [(i, (i + s) % rows) for i in range(rows)]) for s in range(1, rows)
-        ])
-    own = lax.all_gather(jnp.concatenate([b[0] for b in blocks], axis=1), "col", axis=0)
     others = []
-    for m in moved:
-        others.append(lax.all_gather(jnp.concatenate(m, axis=0), "col", axis=0))
+    for block in [head] + blocks:
+        moved = [lax.ppermute(block[s - 1], "row", [(i, (i + s) % rows) for i in range(rows)]) for s in range(1, rows)]
+        others.append(lax.all_gather(jnp.concatenate(moved, axis=0), "col", axis=0))
 
     q0, q1 = panels[0], panels[1]
     owner = (me_row == group) & (me_tm == tm_owner)
     kind = jnp.where(me_col == q0, 0, jnp.where(me_col == q1, 1, 2))
     info = jnp.stack([
-        q0, q1, me_col, kind, offset // width, jnp.where(owner, cols, 0),
+        q0, q1, me_col, kind, offset // width, jnp.where(owner, cols, 0), me_row,
     ]).astype(jnp.int32)
     square = jax.ShapeDtypeStruct((width, width), jnp.float32)
     coarse = jax.ShapeDtypeStruct((width, width), jnp.bfloat16)
@@ -464,15 +497,15 @@
         functools.partial(second_kernel, scale), info, [sw, sw, sw, ridges, ridges, i0], [0, 1, 2, 0, 1, None],
         [coarse, coarse, square], scratch, 24 * 10**9, "second")
     weights, d = chain_call(
-        functools.partial(third_kernel, scale), info,
-        [sw, sw, sw, ridges, ridges, i0, i1, c01, c0j, turned], [0, 1, 2, 0, 1, None, None, None, None, None],
+        functools.partial(third_kernel, scale, rows), info,
+        [sw, sw, sw, ridges, ridges, i0, i1, c01, c0j, whitening], [0, 1, 2, 0, 1, None, None, None, None, None],
         [jax.ShapeDtypeStruct((depth, 3 * width), jnp.bfloat16), jax.ShapeDtypeStruct((2 * width, 3 * width), jnp.float32)],
         [], 15 * 10**9, "third")
     own_ridge = ridge.reshape(1, width) * (kind == 2).astype(jnp.float32)
 
     prior = None
-    for c in range(chunks):
-        prior = final_chunk(info, own, others[c], weights, d, own_ridge, prior, c, chunks, width)
+    for c, start in enumerate(starts):
+        prior = final_chunk(info, own, others[c], weights, d, own_ridge, prior, start, width)
     return tuple(prior)
 
 

time: 486 us -> 508 us (1.045)
  the two profiles are of different devices: /device:TPU:30 before, /device:TPU:0 now
where the time goes in v1:
time: 508 us; the launch traced here: 501 us
  Pallas kernels  286 us (56%)
  waiting for transfers between devices  114 us (22%)
  starting transfers between devices  67.8 us (13%)
  between operations  16.6 us (3%)
  local copies, waits for them, and re-layouts  9.63 us (2%)
  other arithmetic  7.01 us (1%)
    ppermute x15, waiting for transfers between devices, on_device(): lax.ppermute(block[s - 1], 'row', [(i, (i + s) % rows) for i in range(row...  114 us
    pallas_call x5, Pallas kernels, final_chunk(): pl.pallas_call(functools.partial(final_body, base), grid_spec=pltpu.Prefe...  88.5 us
    pallas_call x1, Pallas kernels, gather_slab(): pl.pallas_call(functools.partial(gather_kernel, row_n, col_n, tm_n), out_...  82.1 us
    pallas_call x3, Pallas kernels, chain_call(): pl.pallas_call(kernel, grid_spec=pltpu.PrefetchScalarGridSpec(num_scalar_...  76.5 us
    ppermute x15, starting transfers between devices, on_device(): lax.ppermute(block[s - 1], 'row', [(i, (i + s) % rows) for i in range(row...  67.4 us
    pallas_call x5, Pallas kernels, split_blocks(): pl.pallas_call(functools.partial(split_kernel, rows), grid_spec=pltpu.Pre...  24.4 us
    pallas_call x2, Pallas kernels, pick_blocks(): pl.pallas_call(functools.partial(pick_kernel, rows), grid_spec=pltpu.Pref...  14.2 us
  transfers between devices with their start and end apart: 21, of which 9 were waited for; matrix products, arithmetic and copies ran while one was open for 1% of the time, Pallas kernels for 51%

profile of v1, /device:TPU:0, one launch (start us, length us, event | category | flops | bytes accessed | tf_op | source)
XLA Modules:
  0.0 501.0 jit_solution(7793478952184068213)
XLA Ops:
  7.2 0.0 all-gather.23.cloned.1.call-start
  8.0 0.6 pad_add_fusion.info
  8.6 4.6 pick_blocks.2.part
  13.2 5.3 %split_blocks.5 = (bf16[256,1024]{1,0:T(8,128)(2,1)}, bf16[256,1024]{1,0:T(8,128)(2,1)}, bf16[256,1024]{1,0:T(8,128)(2,1)}) custom-call(s32[1]{0:T(128)} %bitcast.7.info, bf16[256,4,4096]{2,1,0:T(4,128)(2,1)} %bitcast.27), custom_call_target="tpu_custom_call" | custom-call | bytes 8388608 | tf_op jit(solution)/shard_map/split_blocks/pallas_call | solution.py:314
  18.6 0.7 pad_add_fusion.1.info
  19.2 9.5 %pick_blocks.3 = bf16[256,4096]{1,0:T(8,128)(2,1)} custom-call(s32[17]{0:T(128)} %pad_add_fusion.1.info, bf16[256,4,4096]{2,1,0:T(4,128)(2,1)} %bitcast.28), custom_call_target="tpu_custom_call" | custom-call | bytes 16777216 | tf_op jit(solution)/shard_map/pick_blocks/pallas_call | solution.py:344
  28.8 3.1 collective-permute-start.12
  31.8 2.5 collective-permute-start.13
  34.3 1.4 collective-permute-start.14
  35.7 11.2 %collective-permute-done.12 = bf16[256,1024]{1,0:T(8,128)(2,1)S(1)} collective-permute-done((bf16[256,1024]{1,0:T(8,128)(2,1)}, bf16[256,1024]{1,0:T(8,128)(2,1)S(1)}, u32[]{:S(2)}, u32[]{:S(2)}) %collective-permute-start.12) | collective-permute-done | bytes 524320 | tf_op jit(solution)/shard_map/ppermute | solution.py:481
  46.9 21.6 %collective-permute-done.13 = bf16[256,1024]{1,0:T(8,128)(2,1)S(1)} collective-permute-done((bf16[256,1024]{1,0:T(8,128)(2,1)}, bf16[256,1024]{1,0:T(8,128)(2,1)S(1)}, u32[]{:S(2)}, u32[]{:S(2)}) %collective-permute-start.13) | collective-permute-done | bytes 524320 | tf_op jit(solution)/shard_map/ppermute | solution.py:481
  68.5 1.2 pad_maximum_fusion.2
  69.7 0.0 all-gather.23.cloned.1.call-update
  69.7 0.0 all-gather.13.cloned.1.call-start
  69.8 0.7 all-gather.13.cloned.1.call-update
  70.5 0.2 all-gather.21.cloned.1.call-start
  70.8 82.1 %gather_slab.1 = (bf16[1024,2048]{1,0:T(8,128)(2,1)S(1)}, f32[4,8,512]{2,1,0:T(8,128)S(1)}) custom-call(bf16[256,2048]{1,0:T(8,128)(2,1)S(1)} %copy-done.4, f32[8,512]{1,0:T(8,128)S(1)} %broadcast_in_dim.3.ridge, bf16[1024,1024]{1,0:T(8,128)(2,1)S(1)} %copy-done.6), custom_call_target="tpu_custom_call" | custom-call | flops 40000000000 | bytes 1048576 | tf_op jit(solution)/shard_map/gather_slab/pallas_call | solution.py:283
  152.8 2.0 copy-done.7
  154.9 5.3 %split_blocks.6 = (bf16[256,1024]{1,0:T(8,128)(2,1)}, bf16[256,1024]{1,0:T(8,128)(2,1)}, bf16[256,1024]{1,0:T(8,128)(2,1)}) custom-call(s32[1]{0:T(128)} %bitcast.7.info, bf16[256,4,4096]{2,1,0:T(4,128)(2,1)} %bitcast.29), custom_call_target="tpu_custom_call" | custom-call | bytes 8388608 | tf_op jit(solution)/shard_map/split_blocks/pallas_call | solution.py:314
  160.2 5.4 %split_blocks.7 = (bf16[256,1024]{1,0:T(8,128)(2,1)}, bf16[256,1024]{1,0:T(8,128)(2,1)}, bf16[256,1024]{1,0:T(8,128)(2,1)}) custom-call(s32[1]{0:T(128)} %bitcast.7.info, bf16[256,4,4096]{2,1,0:T(4,128)(2,1)} %bitcast.30), custom_call_target="tpu_custom_call" | custom-call | bytes 8388608 | tf_op jit(solution)/shard_map/split_blocks/pallas_call | solution.py:314
  165.6 4.1 split_blocks.8
  169.7 4.2 split_blocks.9
  173.9 0.1 collective-permute-start.10
  174.0 3.8 collective-permute-start.11
  177.8 0.2 collective-permute-start.9
  178.0 23.6 %collective-permute-done.10 = bf16[256,1024]{1,0:T(8,128)(2,1)S(1)} collective-permute-done((bf16[256,1024]{1,0:T(8,128)(2,1)S(1)}, bf16[256,1024]{1,0:T(8,128)(2,1)S(1)}, u32[]{:S(2)}, u32[]{:S(2)}) %collective-permute-start.10) | collective-permute-done | bytes 524320 | tf_op jit(solution)/shard_map/ppermute | solution.py:481
  201.7 10.7 %collective-permute-done.9 = bf16[256,1024]{1,0:T(8,128)(2,1)S(1)} collective-permute-done((bf16[256,1024]{1,0:T(8,128)(2,1)S(1)}, bf16[256,1024]{1,0:T(8,128)(2,1)S(1)}, u32[]{:S(2)}, u32[]{:S(2)}) %collective-permute-start.9) | collective-permute-done | bytes 524320 | tf_op jit(solution)/shard_map/ppermute | solution.py:481
  212.4 1.3 pad_maximum_fusion.1
  213.7 0.0 all-gather.21.cloned.1.call-update
  213.7 0.0 all-gather.19.cloned.1.call-start
  213.8 22.0 %collective-permute-start.6 = (bf16[256,1024]{1,0:T(8,128)(2,1)S(1)}, bf16[256,1024]{1,0:T(8,128)(2,1)S(1)}, u32[]{:S(2)}, u32[]{:S(2)}) collective-permute-start(bf16[256,1024]{1,0:T(8,128)(2,1)S(1)} %copy-done.12), channel_id=1, source_target_pairs={{0,8},{8,16},{16,24},{24,0},{1,9},{9,17},{17,25},{25,1},{2,10},{10... | collective-permute-start | bytes 1572872 | tf_op jit(solution)/shard_map/ppermute | solution.py:481
  235.8 2.4 collective-permute-start.8
  238.2 9.9 %collective-permute-done.6 = bf16[256,1024]{1,0:T(8,128)(2,1)S(1)} collective-permute-done((bf16[256,1024]{1,0:T(8,128)(2,1)S(1)}, bf16[256,1024]{1,0:T(8,128)(2,1)S(1)}, u32[]{:S(2)}, u32[]{:S(2)}) %collective-permute-start.6) | collective-permute-done | bytes 524320 | tf_op jit(solution)/shard_map/ppermute | solution.py:481
  248.1 12.5 %collective-permute-done.7 = bf16[256,1024]{1,0:T(8,128)(2,1)S(1)} collective-permute-done((bf16[256,1024]{1,0:T(8,128)(2,1)S(1)}, bf16[256,1024]{1,0:T(8,128)(2,1)S(1)}, u32[]{:S(2)}, u32[]{:S(2)}) %collective-permute-start.7) | collective-permute-done | bytes 524320 | tf_op jit(solution)/shard_map/ppermute | solution.py:481
  260.6 8.3 %collective-permute-done.8 = bf16[256,1024]{1,0:T(8,128)(2,1)S(1)} collective-permute-done((bf16[256,1024]{1,0:T(8,128)(2,1)S(1)}, bf16[256,1024]{1,0:T(8,128)(2,1)S(1)}, u32[]{:S(2)}, u32[]{:S(2)}) %collective-permute-start.8) | collective-permute-done | bytes 524320 | tf_op jit(solution)/shard_map/ppermute | solution.py:481
  268.9 1.3 pad_maximum_fusion
  270.1 0.0 all-gather.19.cloned.1.call-update
  270.2 0.0 all-gather.17.cloned.1.call-start
  270.2 11.5 %collective-permute-start.3 = (bf16[256,512]{1,0:T(8,128)(2,1)S(1)}, bf16[256,512]{1,0:T(8,128)(2,1)S(1)}, u32[]{:S(2)}, u32[]{:S(2)}) collective-permute-start(bf16[256,512]{1,0:T(8,128)(2,1)S(1)} %copy-done.21), channel_id=1, source_target_pairs={{0,8},{8,16},{16,24},{24,0},{1,9},{9,17},{17,25},{25,1},{2,10},{10... | collective-permute-start | bytes 786440 | tf_op jit(solution)/shard_map/ppermute | solution.py:481
  281.7 3.4 collective-permute-start.4
  285.1 6.7 %collective-permute-done.3 = bf16[256,512]{1,0:T(8,128)(2,1)S(1)} collective-permute-done((bf16[256,512]{1,0:T(8,128)(2,1)S(1)}, bf16[256,512]{1,0:T(8,128)(2,1)S(1)}, u32[]{:S(2)}, u32[]{:S(2)}) %collective-permute-start.3) | collective-permute-done | bytes 262176 | tf_op jit(solution)/shard_map/ppermute | solution.py:481
  291.8 9.2 %collective-permute-done.4 = bf16[256,512]{1,0:T(8,128)(2,1)S(1)} collective-permute-done((bf16[256,512]{1,0:T(8,128)(2,1)S(1)}, bf16[256,512]{1,0:T(8,128)(2,1)S(1)}, u32[]{:S(2)}, u32[]{:S(2)}) %collective-permute-start.4) | collective-permute-done | bytes 262176 | tf_op jit(solution)/shard_map/ppermute | solution.py:481
  301.0 1.0 pad_maximum_fusion.4
  302.0 0.0 all-gather.17.cloned.1.call-update
  302.0 0.0 all-gather.15.cloned.1.call-start
  302.1 14.6 %collective-permute-start = (bf16[256,512]{1,0:T(8,128)(2,1)S(1)}, bf16[256,512]{1,0:T(8,128)(2,1)S(1)}, u32[]{:S(2)}, u32[]{:S(2)}) collective-permute-start(bf16[256,512]{1,0:T(8,128)(2,1)S(1)} %copy-done.18), channel_id=1, source_target_pairs={{0,8},{8,16},{16,24},{24,0},{1,9},{9,17},{17,25},{25,1},{2,10},{10... | collective-permute-start | bytes 786440 | tf_op jit(solution)/shard_map/ppermute | solution.py:481
  316.7 2.4 collective-permute-start.2
  319.1 0.6 slice.15
  319.7 0.6 fusion
  321.6 0.7 stack.23.info
  322.3 25.1 %shard_map.68.i0_ref = f32[512,512]{1,0:T(8,128)} custom-call(s32[7]{0:T(128)} %stack.23.info, bf16[1024,2048]{1,0:T(8,128)(2,1)} %copy-done.7, f32[1,2048]{1,0:T(1,128)} %bitcast.40), custom_call_target="tpu_custom_call" | custom-call | flops 20000000000 | bytes 8388608 | tf_op jit(solution)/shard_map/pallas_call | solution.py:164
  347.4 29.6 %shard_map.69 = (bf16[512,512]{1,0:T(8,128)(2,1)}, bf16[512,512]{1,0:T(8,128)(2,1)}, f32[512,512]{1,0:T(8,128)}) custom-call(s32[7]{0:T(128)} %stack.23.info, bf16[1024,2048]{1,0:T(8,128)(2,1)} %copy-done.7, bf16[1024,2048]{1,0:T(8,128)(2,1)} %copy-done.7, bf16[1024,2048]{1,0:T(8,128)(2,1)} %copy-done.7, f32[1,2048]{1,0:T(1,128)} %bitcast.41, ...), custom_call_target="tpu_custom_call" | custom-call | flops 24000000000 | bytes 8388608 | tf_op jit(solution)/shard_map/pallas_call | solution.py:164
  377.0 1.0 pad_maximum_fusion.3
  378.0 0.0 all-gather.15.cloned.1.call-update
  378.0 21.8 %shard_map.70 = (bf16[1024,1536]{1,0:T(8,128)(2,1)}, f32[1024,1536]{1,0:T(8,128)}) custom-call(s32[7]{0:T(128)} %stack.23.info, bf16[1024,2048]{1,0:T(8,128)(2,1)} %copy-done.7, bf16[1024,2048]{1,0:T(8,128)(2,1)} %copy-done.7, bf16[1024,2048]{1,0:T(8,128)(2,1)} %copy-done.7, f32[1,2048]{1,0:T(1,128)} %bitcast.43, f32[1,2048]{1,0:T(1,128)} %bitcast.44, ...), custom_call_target="tpu_custom_call" | custom-call | flops 15000000512 | bytes 8388608 | tf_op jit(solution)/shard_map/pallas_call | solution.py:164
  399.8 0.0 all-gather.13.cloned.1.call-done
  399.8 1.9 copy-done
  401.7 21.1 %final.5 = (f32[16384,512]{1,0:T(8,128)}, bf16[2,16384,512]{2,1,0:T(8,128)(2,1)}) custom-call(s32[7]{0:T(128)S(1)} %copy-done.5, bf16[4,256,4096]{2,1,0:T(8,128)(2,1)} %bitcast.33, bf16[4,768,1024]{2,1,0:T(8,128)(2,1)} %bitcast.46, bf16[1024,1536]{1,0:T(8,128)(2,1)S(1)} %copy-done, f32[1024,1536]{1,0:T(8,128)} %get-tuple-element.81.d_ref, f32[1,512]{1,0:T(1,128)S(1)} %bitcast.21), custom_call_target="tpu_custom_call" | custom-call | flops 12884901888 | bytes 25165824 | tf_op jit(solution)/shard_map/final/pallas_call | solution.py:416
  422.8 20.7 %final.6 = (f32[16384,512]{1,0:T(8,128)}, bf16[2,16384,512]{2,1,0:T(8,128)(2,1)}) custom-call(s32[7]{0:T(128)S(1)} %copy-done.5, bf16[4,256,4096]{2,1,0:T(8,128)(2,1)} %bitcast.34, bf16[4,768,1024]{2,1,0:T(8,128)(2,1)} %bitcast.38, bf16[1024,1536]{1,0:T(8,128)(2,1)S(1)} %copy-done.1, ...), custom_call_target="tpu_custom_call", output_to_operand_aliasing={{0}: (6, {}), {1}: (7, {})} | custom-call | flops 12884901888 | bytes 25165824 | tf_op jit(solution)/shard_map/final/pallas_call | solution.py:416
  443.5 20.7 %final.7 = (f32[16384,512]{1,0:T(8,128)}, bf16[2,16384,512]{2,1,0:T(8,128)(2,1)}) custom-call(s32[7]{0:T(128)S(1)} %copy-done.5, bf16[4,256,4096]{2,1,0:T(8,128)(2,1)} %bitcast.35, bf16[4,768,1024]{2,1,0:T(8,128)(2,1)} %bitcast.39, bf16[1024,1536]{1,0:T(8,128)(2,1)S(1)} %copy-done.1, ...), custom_call_target="tpu_custom_call", output_to_operand_aliasing={{0}: (6, {}), {1}: (7, {})} | custom-call | flops 12884901888 | bytes 25165824 | tf_op jit(solution)/shard_map/final/pallas_call | solution.py:416
  464.2 1.9 copy-done.2
  466.0 13.0 %final.8 = (f32[16384,512]{1,0:T(8,128)}, bf16[2,16384,512]{2,1,0:T(8,128)(2,1)}) custom-call(s32[7]{0:T(128)S(1)} %copy-done.5, bf16[4,256,4096]{2,1,0:T(8,128)(2,1)} %bitcast.36, bf16[4,768,512]{2,1,0:T(8,128)(2,1)S(1)} %bitcast.19, bf16[1024,1536]{1,0:T(8,128)(2,1)} %get-tuple-element.80.p_ref, ...), custom_call_target="tpu_custom_call", output_to_operand_aliasing={{0}: (6, {}), {1}: (7, {})} | custom-call | flops 6442450944 | bytes 12582912 | tf_op jit(solution)/shard_map/final/pallas_call | solution.py:416
  479.1 1.9 copy-done.3
  481.0 13.0 %final.9 = (f32[16384,512]{1,0:T(8,128)}, bf16[2,16384,512]{2,1,0:T(8,128)(2,1)}) custom-call(s32[7]{0:T(128)S(1)} %copy-done.5, bf16[4,256,4096]{2,1,0:T(8,128)(2,1)} %bitcast.37, bf16[4,768,512]{2,1,0:T(8,128)(2,1)S(1)} %bitcast.20, bf16[1024,1536]{1,0:T(8,128)(2,1)} %get-tuple-element.80.p_ref, ...), custom_call_target="tpu_custom_call", output_to_operand_aliasing={{0}: (6, {}), {1}: (7, {})} | custom-call | flops 6442450944 | bytes 12582912 | tf_op jit(solution)/shard_map/final/pallas_call | solution.py:416
  (60 shorter events, 0.2 us)
Async XLA Ops:
  7.2 392.6 %all-gather.23.cloned.1.call-start = ((), (), s32[]{:S(2)}) async-start(), calls=%async_computation.5 | async-start | bytes 7864320 | tf_op jit(solution)/shard_map/all_gather | solution.py:482
  28.8 42.0 %copy-start.8 = (f32[512]{0:T(512)S(1)}, f32[512]{0:T(512)}, u32[]{:S(2)}) copy-start(f32[512]{0:T(512)} %param.7) | copy-start | bytes 6148
  28.8 42.0 %copy-start.4 = (bf16[256,2048]{1,0:T(8,128)(2,1)S(1)}, bf16[256,2048]{1,0:T(8,128)(2,1)}, u32[]{:S(2)}) copy-start(bf16[256,2048]{1,0:T(8,128)(2,1)} %pick_blocks.2.part) | copy-start | bytes 3145732
  28.8 42.0 %copy-start.6 = (bf16[1024,1024]{1,0:T(8,128)(2,1)S(1)}, bf16[1024,1024]{1,0:T(8,128)(2,1)}, u32[]{:S(2)}) copy-start(bf16[1024,1024]{1,0:T(8,128)(2,1)} %w_ref.1) | copy-start | bytes 6291460
  28.8 18.1 %collective-permute-start.12 = (bf16[256,1024]{1,0:T(8,128)(2,1)}, bf16[256,1024]{1,0:T(8,128)(2,1)S(1)}, u32[]{:S(2)}, u32[]{:S(2)}) collective-permute-start(bf16[256,1024]{1,0:T(8,128)(2,1)} %get-tuple-element.91), channel_id=1, source_target_pairs={{0,8},{8,16},{16,24},{24,0},{1,9},{9,17},{17,25},{25,1},{2,10},{10... | collective-permute-start | bytes 1572872 | tf_op jit(solution)/shard_map/ppermute | solution.py:481
  31.8 36.7 %collective-permute-start.13 = (bf16[256,1024]{1,0:T(8,128)(2,1)}, bf16[256,1024]{1,0:T(8,128)(2,1)S(1)}, u32[]{:S(2)}, u32[]{:S(2)}) collective-permute-start(bf16[256,1024]{1,0:T(8,128)(2,1)} %get-tuple-element.92), channel_id=1, source_target_pairs={{0,16},{8,24},{16,0},{24,8},{1,17},{9,25},{17,1},{25,9},{2,18},{10... | collective-permute-start | bytes 1572872 | tf_op jit(solution)/shard_map/ppermute | solution.py:481
  34.3 34.2 %collective-permute-start.14 = (bf16[256,1024]{1,0:T(8,128)(2,1)}, bf16[256,1024]{1,0:T(8,128)(2,1)S(1)}, u32[]{:S(2)}, u32[]{:S(2)}) collective-permute-start(bf16[256,1024]{1,0:T(8,128)(2,1)} %get-tuple-element.93), channel_id=1, source_target_pairs={{0,24},{8,0},{16,8},{24,16},{1,25},{9,1},{17,9},{25,17},{2,26},{10... | collective-permute-start | bytes 1572872 | tf_op jit(solution)/shard_map/ppermute | solution.py:481
  69.7 330.0 %all-gather.13.cloned.1.call-start = ((), (), s32[]{:S(2)}) async-start(), calls=%async_computation | async-start | bytes 10485760 | tf_op jit(solution)/shard_map/all_gather | solution.py:472
  70.5 352.2 %all-gather.21.cloned.1.call-start = ((), (), s32[]{:S(2)}) async-start(), calls=%async_computation.4 | async-start | bytes 7864320 | tf_op jit(solution)/shard_map/all_gather | solution.py:482
  152.8 2.0 copy-start.7
  169.7 4.2 copy-start.15
  169.7 4.3 copy-start.14
  169.7 8.1 %copy-start.13 = (bf16[256,1024]{1,0:T(8,128)(2,1)S(1)}, bf16[256,1024]{1,0:T(8,128)(2,1)}, u32[]{:S(2)}) copy-start(bf16[256,1024]{1,0:T(8,128)(2,1)} %get-tuple-element.88) | copy-start | bytes 1572868
  173.9 39.9 %copy-start.12 = (bf16[256,1024]{1,0:T(8,128)(2,1)S(1)}, bf16[256,1024]{1,0:T(8,128)(2,1)}, u32[]{:S(2)}) copy-start(bf16[256,1024]{1,0:T(8,128)(2,1)} %get-tuple-element.85) | copy-start | bytes 1572868
  173.9 61.9 %copy-start.11 = (bf16[256,1024]{1,0:T(8,128)(2,1)S(1)}, bf16[256,1024]{1,0:T(8,128)(2,1)}, u32[]{:S(2)}) copy-start(bf16[256,1024]{1,0:T(8,128)(2,1)} %get-tuple-element.86) | copy-start | bytes 1572868
  173.9 61.9 %copy-start.10 = (bf16[256,1024]{1,0:T(8,128)(2,1)S(1)}, bf16[256,1024]{1,0:T(8,128)(2,1)}, u32[]{:S(2)}) copy-start(bf16[256,1024]{1,0:T(8,128)(2,1)} %get-tuple-element.87) | copy-start | bytes 1572868
  173.9 27.7 %collective-permute-start.10 = (bf16[256,1024]{1,0:T(8,128)(2,1)S(1)}, bf16[256,1024]{1,0:T(8,128)(2,1)S(1)}, u32[]{:S(2)}, u32[]{:S(2)}) collective-permute-start(bf16[256,1024]{1,0:T(8,128)(2,1)S(1)} %copy-done.15), channel_id=1, source_target_pairs={{0,16},{8,24},{16,0},{24,8},{1,17},{9,25},{17,1},{25,9},{2,18},{10... | collective-permute-start | bytes 1572872 | tf_op jit(solution)/shard_map/ppermute | solution.py:481
  174.0 27.7 %collective-permute-start.11 = (bf16[256,1024]{1,0:T(8,128)(2,1)S(1)}, bf16[256,1024]{1,0:T(8,128)(2,1)S(1)}, u32[]{:S(2)}, u32[]{:S(2)}) collective-permute-start(bf16[256,1024]{1,0:T(8,128)(2,1)S(1)} %copy-done.14), channel_id=1, source_target_pairs={{0,24},{8,0},{16,8},{24,16},{1,25},{9,1},{17,9},{25,17},{2,26},{10... | collective-permute-start | bytes 1572872 | tf_op jit(solution)/shard_map/ppermute | solution.py:481
  177.8 34.5 %collective-permute-start.9 = (bf16[256,1024]{1,0:T(8,128)(2,1)S(1)}, bf16[256,1024]{1,0:T(8,128)(2,1)S(1)}, u32[]{:S(2)}, u32[]{:S(2)}) collective-permute-start(bf16[256,1024]{1,0:T(8,128)(2,1)S(1)} %copy-done.13), channel_id=1, source_target_pairs={{0,8},{8,16},{16,24},{24,0},{1,9},{9,17},{17,25},{25,1},{2,10},{10... | collective-permute-start | bytes 1572872 | tf_op jit(solution)/shard_map/ppermute | solution.py:481
  213.7 56.5 %copy-start.21 = (bf16[256,512]{1,0:T(8,128)(2,1)S(1)}, bf16[256,512]{1,0:T(8,128)(2,1)}, u32[]{:S(2)}) copy-start(bf16[256,512]{1,0:T(8,128)(2,1)} %get-tuple-element.82) | copy-start | bytes 786436
  213.7 68.1 %copy-start.20 = (bf16[256,512]{1,0:T(8,128)(2,1)S(1)}, bf16[256,512]{1,0:T(8,128)(2,1)}, u32[]{:S(2)}) copy-start(bf16[256,512]{1,0:T(8,128)(2,1)} %get-tuple-element.83) | copy-start | bytes 786436
  213.7 71.5 %copy-start.19 = (bf16[256,512]{1,0:T(8,128)(2,1)S(1)}, bf16[256,512]{1,0:T(8,128)(2,1)}, u32[]{:S(2)}) copy-start(bf16[256,512]{1,0:T(8,128)(2,1)} %get-tuple-element.84) | copy-start | bytes 786436
  213.7 88.4 %copy-start.18 = (bf16[256,512]{1,0:T(8,128)(2,1)S(1)}, bf16[256,512]{1,0:T(8,128)(2,1)}, u32[]{:S(2)}) copy-start(bf16[256,512]{1,0:T(8,128)(2,1)} %get-tuple-element.72) | copy-start | bytes 786436
  213.7 103.0 %copy-start.17 = (bf16[256,512]{1,0:T(8,128)(2,1)S(1)}, bf16[256,512]{1,0:T(8,128)(2,1)}, u32[]{:S(2)}) copy-start(bf16[256,512]{1,0:T(8,128)(2,1)} %get-tuple-element.73) | copy-start | bytes 786436
  213.7 103.0 %copy-start.16 = (bf16[256,512]{1,0:T(8,128)(2,1)S(1)}, bf16[256,512]{1,0:T(8,128)(2,1)}, u32[]{:S(2)}) copy-start(bf16[256,512]{1,0:T(8,128)(2,1)} %get-tuple-element.74) | copy-start | bytes 786436
  213.7 106.0 %copy-start.9 = (s32[4]{0:T(128)S(1)}, s32[4]{0:T(128)}, u32[]{:S(2)}) copy-start(s32[4]{0:T(128)} %param.9) | copy-start | bytes 52
  213.7 229.7 %all-gather.19.cloned.1.call-start = ((), (), s32[]{:S(2)}) async-start(), calls=%async_computation.3 | async-start | bytes 7864320 | tf_op jit(solution)/shard_map/all_gather | solution.py:482
  213.8 34.3 %collective-permute-start.6 = (bf16[256,1024]{1,0:T(8,128)(2,1)S(1)}, bf16[256,1024]{1,0:T(8,128)(2,1)S(1)}, u32[]{:S(2)}, u32[]{:S(2)}) collective-permute-start(bf16[256,1024]{1,0:T(8,128)(2,1)S(1)} %copy-done.12), channel_id=1, source_target_pairs={{0,8},{8,16},{16,24},{24,0},{1,9},{9,17},{17,25},{25,1},{2,10},{10... | collective-permute-start | bytes 1572872 | tf_op jit(solution)/shard_map/ppermute | solution.py:481
  235.8 24.8 %collective-permute-start.7 = (bf16[256,1024]{1,0:T(8,128)(2,1)S(1)}, bf16[256,1024]{1,0:T(8,128)(2,1)S(1)}, u32[]{:S(2)}, u32[]{:S(2)}) collective-permute-start(bf16[256,1024]{1,0:T(8,128)(2,1)S(1)} %copy-done.11), channel_id=1, source_target_pairs={{0,16},{8,24},{16,0},{24,8},{1,17},{9,25},{17,1},{25,9},{2,18},{10... | collective-permute-start | bytes 1572872 | tf_op jit(solution)/shard_map/ppermute | solution.py:481
  235.8 33.1 %collective-permute-start.8 = (bf16[256,1024]{1,0:T(8,128)(2,1)S(1)}, bf16[256,1024]{1,0:T(8,128)(2,1)S(1)}, u32[]{:S(2)}, u32[]{:S(2)}) collective-permute-start(bf16[256,1024]{1,0:T(8,128)(2,1)S(1)} %copy-done.10), channel_id=1, source_target_pairs={{0,24},{8,0},{16,8},{24,16},{1,25},{9,1},{17,9},{25,17},{2,26},{10... | collective-permute-start | bytes 1572872 | tf_op jit(solution)/shard_map/ppermute | solution.py:481
  270.2 194.0 %all-gather.17.cloned.1.call-start = ((), (), s32[]{:S(2)}) async-start(), calls=%async_computation.2 | async-start | bytes 3932160 | tf_op jit(solution)/shard_map/all_gather | solution.py:482
  270.2 21.6 %collective-permute-start.3 = (bf16[256,512]{1,0:T(8,128)(2,1)S(1)}, bf16[256,512]{1,0:T(8,128)(2,1)S(1)}, u32[]{:S(2)}, u32[]{:S(2)}) collective-permute-start(bf16[256,512]{1,0:T(8,128)(2,1)S(1)} %copy-done.21), channel_id=1, source_target_pairs={{0,8},{8,16},{16,24},{24,0},{1,9},{9,17},{17,25},{25,1},{2,10},{10... | collective-permute-start | bytes 786440 | tf_op jit(solution)/shard_map/ppermute | solution.py:481
  281.7 19.3 %collective-permute-start.4 = (bf16[256,512]{1,0:T(8,128)(2,1)S(1)}, bf16[256,512]{1,0:T(8,128)(2,1)S(1)}, u32[]{:S(2)}, u32[]{:S(2)}) collective-permute-start(bf16[256,512]{1,0:T(8,128)(2,1)S(1)} %copy-done.20), channel_id=1, source_target_pairs={{0,16},{8,24},{16,0},{24,8},{1,17},{9,25},{17,1},{25,9},{2,18},{10... | collective-permute-start | bytes 786440 | tf_op jit(solution)/shard_map/ppermute | solution.py:481
  285.1 15.9 %collective-permute-start.5 = (bf16[256,512]{1,0:T(8,128)(2,1)S(1)}, bf16[256,512]{1,0:T(8,128)(2,1)S(1)}, u32[]{:S(2)}, u32[]{:S(2)}) collective-permute-start(bf16[256,512]{1,0:T(8,128)(2,1)S(1)} %copy-done.19), channel_id=1, source_target_pairs={{0,24},{8,0},{16,8},{24,16},{1,25},{9,1},{17,9},{25,17},{2,26},{10... | collective-permute-start | bytes 786440 | tf_op jit(solution)/shard_map/ppermute | solution.py:481
  302.0 177.1 %all-gather.15.cloned.1.call-start = ((), (), s32[]{:S(2)}) async-start(), calls=%async_computation.1 | async-start | bytes 3932160 | tf_op jit(solution)/shard_map/all_gather | solution.py:482
  302.1 74.9 %collective-permute-start = (bf16[256,512]{1,0:T(8,128)(2,1)S(1)}, bf16[256,512]{1,0:T(8,128)(2,1)S(1)}, u32[]{:S(2)}, u32[]{:S(2)}) collective-permute-start(bf16[256,512]{1,0:T(8,128)(2,1)S(1)} %copy-done.18), channel_id=1, source_target_pairs={{0,8},{8,16},{16,24},{24,0},{1,9},{9,17},{17,25},{25,1},{2,10},{10... | collective-permute-start | bytes 786440 | tf_op jit(solution)/shard_map/ppermute | solution.py:481
  316.7 60.3 %collective-permute-start.1 = (bf16[256,512]{1,0:T(8,128)(2,1)S(1)}, bf16[256,512]{1,0:T(8,128)(2,1)S(1)}, u32[]{:S(2)}, u32[]{:S(2)}) collective-permute-start(bf16[256,512]{1,0:T(8,128)(2,1)S(1)} %copy-done.17), channel_id=1, source_target_pairs={{0,16},{8,24},{16,0},{24,8},{1,17},{9,25},{17,1},{25,9},{2,18},{10... | collective-permute-start | bytes 786440 | tf_op jit(solution)/shard_map/ppermute | solution.py:481
  316.7 60.3 %collective-permute-start.2 = (bf16[256,512]{1,0:T(8,128)(2,1)S(1)}, bf16[256,512]{1,0:T(8,128)(2,1)S(1)}, u32[]{:S(2)}, u32[]{:S(2)}) collective-permute-start(bf16[256,512]{1,0:T(8,128)(2,1)S(1)} %copy-done.16), channel_id=1, source_target_pairs={{0,24},{8,0},{16,8},{24,16},{1,25},{9,1},{17,9},{25,17},{2,26},{10... | collective-permute-start | bytes 786440 | tf_op jit(solution)/shard_map/ppermute | solution.py:481
  378.0 21.8 %copy-start.5 = (s32[7]{0:T(128)S(1)}, s32[7]{0:T(128)}, u32[]{:S(2)}) copy-start(s32[7]{0:T(128)} %stack.23.info) | copy-start | bytes 88
  399.8 1.9 copy-start
  401.7 21.1 %copy-start.1 = (bf16[1024,1536]{1,0:T(8,128)(2,1)S(1)}, bf16[1024,1536]{1,0:T(8,128)(2,1)}, u32[]{:S(2)}) copy-start(bf16[1024,1536]{1,0:T(8,128)(2,1)} %get-tuple-element.80.p_ref) | copy-start | bytes 9437188
  464.2 1.9 copy-start.2
  479.1 1.9 copy-start.3
Sparse Core Ops, SparseCore 0:
  69.9 84.7 all-gather.22
  156.7 57.7 all-gather.12
  216.1 62.3 all-gather.20
  279.9 48.1 all-gather.18
  329.6 28.5 all-gather.16
  378.1 26.1 all-gather.14

commit v2 on v1

--- a/solution.py
+++ b/solution.py
@@ -176,10 +176,11 @@
     )(info, *operands)
 
 
-def gather_kernel(
-    row_n, col_n, tm_n, part, ridge, w, out, ridges, summed, series,
-    sum_send, sum_recv, row_send, row_recv, far_send, far_recv, near_send, near_recv, r_send, r_recv,
-):
+def gather_kernel(row_n, col_n, tm_n, starts, sizes, part, ridge, w, flat, out, ridges, own, head, *rest):
+    count = len(sizes)
+    pieces = [rest[c * (row_n - 1):(c + 1) * (row_n - 1)] for c in range(count)]
+    (summed, series, source, sorted_, sum_send, sum_recv, row_send, row_recv, far_send, far_recv, near_send, near_recv,
+     r_send, r_recv, in_sem, out_sem, head_send, head_recv) = rest[count * (row_n - 1):]
     row, col, tm = lax.axis_index("row"), lax.axis_index("col"), lax.axis_index("tm")
     plane = col_n * tm_n
     me = col * tm_n + tm
@@ -232,18 +233,57 @@
     def ridge_copy(d):
         return remote(ridge, ridges.at[col], r_send.at[d - 1], r_recv.at[d - 1], {"col": lax.rem(col + d, col_n)})
 
+    def in_copy(c):
+        return pltpu.make_async_copy(
+            flat.at[:, :, pl.ds(starts[c], sizes[c])], source.at[c % 2, :, :, pl.ds(0, sizes[c])], in_sem.at[c % 2])
+
+    def out_copy(c, s):
+        to = pieces[c][s - 1] if s else own.at[:, pl.ds(starts[c], sizes[c])]
+        return pltpu.make_async_copy(sorted_.at[c % 2, s, :, pl.ds(0, sizes[c])], to, out_sem.at[c % 2, s])
+
+    def head_copy(s):
+        return remote(pieces[0][s - 1], head.at[pl.ds((s - 1) * times, times)], head_send.at[s - 1],
+                      head_recv.at[s - 1], {"row": lax.rem(row + s, row_n)})
+
+    def finish(c):
+        for s in range(row_n):
+            out_copy(c, s).wait()
+
+    def split(c):
+        if c >= count:
+            return
+        in_copy(c).wait()
+        if c + 1 < count:
+            in_copy(c + 1).start()
+        if c >= 2:
+            finish(c - 2)
+        for k in range(row_n):
+            @pl.when(row == k)
+            def _():
+                def strip(t, carry):
+                    at = pl.ds(pl.multiple_of(t * 16, 16), 16)
+                    for s in range(row_n):
+                        sorted_[c % 2, s, at, :sizes[c]] = source[c % 2, at, (k + s) % row_n, :sizes[c]]
+                    return carry
+
+                lax.fori_loop(0, times // 16, strip, 0)
+        for s in range(row_n):
+            out_copy(c, s).start()
+
     started = []
 
     def start(copy):
         copy.start()
         started.append(copy)
 
+    in_copy(0).start()
     for h in range(2):
         for d in range(1, plane):
             start(sum_copy(h, d))
     for d in range(1, col_n):
         start(ridge_copy(d))
     ridges[col] = ridge[...]
+    split(0)
     for h in range(2):
         total = part[:, columns(me, h)].astype(jnp.float32)
         for d in range(1, plane):
@@ -252,6 +292,8 @@
         series[h, here] = total.astype(jnp.bfloat16)
         for d in range(1, row_n):
             start(row_copy(h, d))
+    split(1)
+    split(2)
     for h in range(2):
         for d in range(1, row_n):
             row_copy(h, d).wait_recv()
@@ -259,6 +301,12 @@
         for e in range(1, len(steps)):
             start(far_copy(h, e))
         start(near_copy(h, 0))
+    if count < 3:
+        finish(0)
+    for s in range(1, row_n):
+        start(head_copy(s))
+    split(3)
+    split(4)
     for h in range(2):
         for e in range(1, len(steps)):
             far_copy(h, e).wait_recv()
@@ -268,11 +316,15 @@
     for h in range(2):
         for e in range(len(steps)):
             near_copy(h, e).wait_recv()
+    for c in range(max(count - 2, 1 if count < 3 else 0), count):
+        finish(c)
+    for s in range(1, row_n):
+        head_copy(s).wait_recv()
     for copy in started:
         copy.wait_send()
 
 
-def gather_slab(part, ridge, w, row_n, col_n, tm_n):
+def gather_slab(part, ridge, w, flat, starts, sizes, row_n, col_n, tm_n):
     times, slab = part.shape
     depth = w.shape[0]
     plane = col_n * tm_n
@@ -281,48 +333,29 @@
     dma = pltpu.SemaphoreType.DMA
     vmem = pl.BlockSpec(memory_space=pltpu.VMEM)
     return pl.pallas_call(
-        functools.partial(gather_kernel, row_n, col_n, tm_n),
+        functools.partial(gather_kernel, row_n, col_n, tm_n, starts, sizes),
         out_shape=[jax.ShapeDtypeStruct((depth, slab), jnp.bfloat16),
-                   jax.ShapeDtypeStruct((col_n,) + ridge.shape, jnp.float32)],
-        in_specs=[vmem] * 3,
-        out_specs=[vmem] * 2,
+                   jax.ShapeDtypeStruct((col_n,) + ridge.shape, jnp.float32),
+                   jax.ShapeDtypeStruct((times, flat.shape[2]), flat.dtype),
+                   jax.ShapeDtypeStruct(((row_n - 1) * times, sizes[0]), flat.dtype)]
+        + [jax.ShapeDtypeStruct((times, n), flat.dtype) for n in sizes for _ in range(row_n - 1)],
+        in_specs=[vmem] * 3 + [pl.BlockSpec(memory_space=pl.ANY)],
+        out_specs=[vmem] * 2 + [pl.BlockSpec(memory_space=pl.ANY)] * (2 + len(sizes) * (row_n - 1)),
         scratch_shapes=[
             pltpu.VMEM((2, plane - 1, times, wide), jnp.bfloat16),
             pltpu.VMEM((2, depth, wide), jnp.bfloat16),
+            pltpu.VMEM((2, times, row_n, max(sizes)), jnp.bfloat16),
+            pltpu.VMEM((2, row_n, times, max(sizes)), jnp.bfloat16),
             dma((2, plane - 1)), dma((2, plane - 1)), dma((2, row_n - 1)), dma((2, row_n - 1)),
             dma((2, far - 1)), dma((2, far - 1)), dma((2, far)), dma((2, far)),
             dma((col_n - 1,)), dma((col_n - 1,)),
+            dma((2,)), dma((2, row_n)), dma((row_n - 1,)), dma((row_n - 1,)),
         ],
         compiler_params=pltpu.CompilerParams(
-            collective_id=1, has_side_effects=True, vmem_limit_bytes=40 * 2**20),
+            collective_id=1, has_side_effects=True, vmem_limit_bytes=60 * 2**20),
         cost_estimate=pl.CostEstimate(flops=40 * 10**9, bytes_accessed=2**20, transcendentals=0),
         name="gather_slab",
-    )(part, ridge, w)
-
-
-def split_kernel(rows, info, x_ref, *outs):
-    for k in range(rows):
-        @pl.when(info[0] == k)
-        def _():
-            for s, o in enumerate(outs):
-                o[...] = x_ref[:, (k + s + 1) % rows, :]
-
-
-def split_blocks(row, x, first, w):
-    times, rows, _ = x.shape
-    bt = min(64, times)
-    return pl.pallas_call(
-        functools.partial(split_kernel, rows),
-        grid_spec=pltpu.PrefetchScalarGridSpec(
-            num_scalar_prefetch=1,
-            grid=(times // bt,),
-            in_specs=[pl.BlockSpec((bt, rows, w), lambda i, info: (i, 0, first // w))],
-            out_specs=[pl.BlockSpec((bt, w), lambda i, info: (i, 0))] * (rows - 1),
-        ),
-        out_shape=[jax.ShapeDtypeStruct((times, w), x.dtype)] * (rows - 1),
-        cost_estimate=pl.CostEstimate(flops=0, bytes_accessed=4 * times * rows * w * 2, transcendentals=0),
-        name="split_blocks",
-    )(row, x)
+    )(part, ridge, w, flat)
 
 
 def pick_kernel(rows, info, x_ref, o_ref):
@@ -330,7 +363,12 @@
     for k in range(rows):
         @pl.when(keep & (info[0] == k))
         def _():
-            o_ref[...] = x_ref[:, k, :]
+            def strip(t, carry):
+                at = pl.ds(pl.multiple_of(t * 16, 16), 16)
+                o_ref[at, :] = x_ref[at, k, :]
+                return carry
+
+            lax.fori_loop(0, o_ref.shape[0] // 16, strip, 0)
 
     @pl.when(jnp.logical_not(keep))
     def _():
@@ -458,28 +496,25 @@
     offset = first % kd
 
     flat = samples.reshape(times, groups, local)
-    sizes = [local // 4] * 3 + [local // 8] * 2 if local >= 8 * width else [width] * (local // width)
+    eighth = local // 8
+    sizes = [eighth, 2 * eighth, 2 * eighth, 2 * eighth, eighth] if eighth >= width else [width] * (local // width)
     starts = [sum(sizes[:c]) for c in range(len(sizes))]
-    row_info = me_row.reshape(1).astype(jnp.int32)
-    split = lambda row, c: split_blocks(row, flat, starts[c], sizes[c])
-    head = split(row_info, 0)
-    count = local // width
-    own = pick_blocks(me_row, jnp.ones((count,), jnp.int32), jnp.arange(count), flat, width)
     at = offset + jnp.arange(cols) * width
     have = (me_tm == tm_owner) & (me_col == at // local)
     part = pick_blocks(group, have, at % local // width, flat, width)
-    part, head, own = lax.optimization_barrier((part, head, own))
+    sw, ridges, own, head, *pieces = gather_slab(
+        part, jnp.broadcast_to(ridge, (SUB, width)), whitening, flat, starts, sizes, rows, cols, tms)
+    ridges = ridges[:, 0].reshape(1, slab)
     own = lax.all_gather(own, "col", axis=0)
-    sw, ridges = gather_slab(part, jnp.broadcast_to(ridge, (SUB, width)), whitening, rows, cols, tms)
-    ridges = ridges[:, 0].reshape(1, slab)
-
-    row_info, sw = lax.optimization_barrier((row_info, sw))
-    blocks = [split(row_info, c) for c in range(1, len(sizes))]
-    blocks, sw = lax.optimization_barrier((blocks, sw))
     others = []
-    for block in [head] + blocks:
-        moved = [lax.ppermute(block[s - 1], "row", [(i, (i + s) % rows) for i in range(rows)]) for s in range(1, rows)]
-        others.append(lax.all_gather(jnp.concatenate(moved, axis=0), "col", axis=0))
+    for c in range(len(sizes)):
+        block = pieces[c * (rows - 1):(c + 1) * (rows - 1)]
+        if c:
+            head = jnp.concatenate([
+                lax.ppermute(block[s - 1], "row", [(i, (i + s) % rows) for i in range(rows)])
+                for s in range(1, rows)
+            ], axis=0)
+        others.append(lax.all_gather(head, "col", axis=0))
 
     q0, q1 = panels[0], panels[1]
     owner = (me_row == group) & (me_tm == tm_owner)

time: 508 us -> 421 us (0.83)
  Pallas kernels: 286 us -> 227 us
  waiting for transfers between devices: 114 us -> 99.2 us
  starting transfers between devices: 67.8 us -> 57.9 us
    pallas_call x6 -> x1, Pallas kernels: 106 us -> 57.2 us  [gather_slab(): pl.pallas_call(functools.partial(gather_kernel, row_n, col_n, tm_n, start...]
    ppermute x15 -> x12, waiting for transfers between devices: 114 us -> 98.5 us  [on_device(): lax.ppermute(block[s - 1], 'row', [(i, (i + s) % rows) for i in range(row...]
    ppermute x15 -> x12, starting transfers between devices: 67.4 us -> 57.6 us  [on_device(): lax.ppermute(block[s - 1], 'row', [(i, (i + s) % rows) for i in range(row...]
    pallas_call x2 -> x1, Pallas kernels: 14.2 us -> 4.77 us  [pick_blocks(): pl.pallas_call(functools.partial(pick_kernel, rows), grid_spec=pltpu.Pref...]
  transfers between devices with their start and end apart: 21 -> 18, of which waited for: 9 -> 7; matrix products, arithmetic and copies ran while one was open for 1% -> 2% of each run, Pallas kernels for 51% -> 37%
where the time goes in v2:
time: 421 us; the launch traced here: 413 us
  Pallas kernels  227 us (54%)
  waiting for transfers between devices  99.2 us (24%)
  starting transfers between devices  57.9 us (14%)
  between operations  16.6 us (4%)
  local copies, waits for them, and re-layouts  7.12 us (2%)
  other arithmetic  5.41 us (1%)
    ppermute x12, waiting for transfers between devices, on_device(): lax.ppermute(block[s - 1], 'row', [(i, (i + s) % rows) for i in range(row...  98.5 us
    pallas_call x5, Pallas kernels, final_chunk(): pl.pallas_call(functools.partial(final_body, base), grid_spec=pltpu.Prefe...  88.2 us
    pallas_call x3, Pallas kernels, chain_call(): pl.pallas_call(kernel, grid_spec=pltpu.PrefetchScalarGridSpec(num_scalar_...  77 us
    ppermute x12, starting transfers between devices, on_device(): lax.ppermute(block[s - 1], 'row', [(i, (i + s) % rows) for i in range(row...  57.6 us
    pallas_call x1, Pallas kernels, gather_slab(): pl.pallas_call(functools.partial(gather_kernel, row_n, col_n, tm_n, start...  57.2 us
  transfers between devices with their start and end apart: 18, of which 7 were waited for; matrix products, arithmetic and copies ran while one was open for 2% of the time, Pallas kernels for 37%

profile of v2, /device:TPU:0, one launch (start us, length us, event | category | flops | bytes accessed | tf_op | source)
XLA Modules:
  0.0 413.4 jit_solution(1339080699222197211)
XLA Ops:
  7.2 0.0 all-gather.23.cloned.1.call-start
  8.0 0.6 pad_add_fusion.info
  8.6 4.8 %pick_blocks.1.part = bf16[256,2048]{1,0:T(8,128)(2,1)} custom-call(s32[9]{0:T(128)} %pad_add_fusion.info, bf16[256,4,4096]{2,1,0:T(4,128)(2,1)} %bitcast.31), custom_call_target="tpu_custom_call" | custom-call | bytes 8388608 | tf_op jit(solution)/shard_map/pick_blocks/pallas_call | solution.py:382
  13.4 0.0 copy-done.4
  13.4 0.6 broadcast_in_dim.3.ridge
  14.0 57.2 %gather_slab.1 = (bf16[1024,2048]{1,0:T(8,128)(2,1)}, f32[4,8,512]{2,1,0:T(8,128)}, bf16[256,4096]{1,0:T(8,128)(2,1)}, bf16[768,512]{1,0:T(8,128)(2,1)}, bf16[25...) custom-call(bf16[256,2048]{1,0:T(8,128)(2,1)} %pick_blocks.1.part, ...), custom_call_target="tpu_custom_call" | custom-call | flops 40000000000 | bytes 1048576 | tf_op jit(solution)/shard_map/gather_slab/pallas_call | solution.py:335
  71.2 0.0 all-gather.23.cloned.1.call-update
  71.2 0.0 all-gather.13.cloned.1.call-start
  71.2 0.0 copy-start.11
  71.2 0.0 copy-start.10
  71.2 0.0 copy-start.9
  71.3 0.7 all-gather.13.cloned.1.call-update
  71.9 0.0 all-gather.21.cloned.1.call-start
  72.0 1.4 collective-permute-start.10
  73.4 2.8 collective-permute-start.11
  76.1 0.0 collective-permute-start.9
  76.1 23.7 %collective-permute-done.10 = bf16[256,1024]{1,0:T(8,128)(2,1)S(1)} collective-permute-done((bf16[256,1024]{1,0:T(8,128)(2,1)}, bf16[256,1024]{1,0:T(8,128)(2,1)S(1)}, u32[]{:S(2)}, u32[]{:S(2)}) %collective-permute-start.10) | collective-permute-done | bytes 524320 | tf_op jit(solution)/shard_map/ppermute | solution.py:514
  99.9 0.0 collective-permute-done.11
  99.9 10.9 %collective-permute-done.9 = bf16[256,1024]{1,0:T(8,128)(2,1)S(1)} collective-permute-done((bf16[256,1024]{1,0:T(8,128)(2,1)}, bf16[256,1024]{1,0:T(8,128)(2,1)S(1)}, u32[]{:S(2)}, u32[]{:S(2)}) %collective-permute-start.9) | collective-permute-done | bytes 524320 | tf_op jit(solution)/shard_map/ppermute | solution.py:514
  110.8 1.3 pad_maximum_fusion.2
  112.1 0.0 all-gather.21.cloned.1.call-update
  112.1 0.0 all-gather.19.cloned.1.call-start
  112.1 0.0 copy-done.11
  112.2 21.9 %collective-permute-start.6 = (bf16[256,1024]{1,0:T(8,128)(2,1)S(1)}, bf16[256,1024]{1,0:T(8,128)(2,1)S(1)}, u32[]{:S(2)}, u32[]{:S(2)}) collective-permute-start(bf16[256,1024]{1,0:T(8,128)(2,1)S(1)} %copy-done.11), channel_id=1, source_target_pairs={{0,8},{8,16},{16,24},{24,0},{1,9},{9,17},{17,25},{25,1},{2,10},{10... | collective-permute-start | bytes 1572872 | tf_op jit(solution)/shard_map/ppermute | solution.py:514
  134.1 0.0 copy-done.10
  134.1 0.0 collective-permute-start.7
  134.1 2.4 collective-permute-start.8
  136.5 9.9 %collective-permute-done.6 = bf16[256,1024]{1,0:T(8,128)(2,1)S(1)} collective-permute-done((bf16[256,1024]{1,0:T(8,128)(2,1)S(1)}, bf16[256,1024]{1,0:T(8,128)(2,1)S(1)}, u32[]{:S(2)}, u32[]{:S(2)}) %collective-permute-start.6) | collective-permute-done | bytes 524320 | tf_op jit(solution)/shard_map/ppermute | solution.py:514
  146.4 12.7 %collective-permute-done.7 = bf16[256,1024]{1,0:T(8,128)(2,1)S(1)} collective-permute-done((bf16[256,1024]{1,0:T(8,128)(2,1)S(1)}, bf16[256,1024]{1,0:T(8,128)(2,1)S(1)}, u32[]{:S(2)}, u32[]{:S(2)}) %collective-permute-start.7) | collective-permute-done | bytes 524320 | tf_op jit(solution)/shard_map/ppermute | solution.py:514
  159.1 8.3 %collective-permute-done.8 = bf16[256,1024]{1,0:T(8,128)(2,1)S(1)} collective-permute-done((bf16[256,1024]{1,0:T(8,128)(2,1)S(1)}, bf16[256,1024]{1,0:T(8,128)(2,1)S(1)}, u32[]{:S(2)}, u32[]{:S(2)}) %collective-permute-start.8) | collective-permute-done | bytes 524320 | tf_op jit(solution)/shard_map/ppermute | solution.py:514
  167.4 1.3 pad_maximum_fusion.1
  168.6 0.0 all-gather.19.cloned.1.call-update
  168.7 0.0 all-gather.17.cloned.1.call-start
  168.7 11.5 %collective-permute-start.3 = (bf16[256,1024]{1,0:T(8,128)(2,1)S(1)}, bf16[256,1024]{1,0:T(8,128)(2,1)S(1)}, u32[]{:S(2)}, u32[]{:S(2)}) collective-permute-start(bf16[256,1024]{1,0:T(8,128)(2,1)S(1)} %copy-done.8), channel_id=1, source_target_pairs={{0,8},{8,16},{16,24},{24,0},{1,9},{9,17},{17,25},{25,1},{2,10},{10... | collective-permute-start | bytes 1572872 | tf_op jit(solution)/shard_map/ppermute | solution.py:514
  180.3 3.4 collective-permute-start.4
  183.6 0.0 collective-permute-start.5
  183.7 12.3 %collective-permute-done.3 = bf16[256,1024]{1,0:T(8,128)(2,1)S(1)} collective-permute-done((bf16[256,1024]{1,0:T(8,128)(2,1)S(1)}, bf16[256,1024]{1,0:T(8,128)(2,1)S(1)}, u32[]{:S(2)}, u32[]{:S(2)}) %collective-permute-start.3) | collective-permute-done | bytes 524320 | tf_op jit(solution)/shard_map/ppermute | solution.py:514
  196.0 20.6 %collective-permute-done.4 = bf16[256,1024]{1,0:T(8,128)(2,1)S(1)} collective-permute-done((bf16[256,1024]{1,0:T(8,128)(2,1)S(1)}, bf16[256,1024]{1,0:T(8,128)(2,1)S(1)}, u32[]{:S(2)}, u32[]{:S(2)}) %collective-permute-start.4) | collective-permute-done | bytes 524320 | tf_op jit(solution)/shard_map/ppermute | solution.py:514
  216.6 0.0 collective-permute-done.5
  216.6 1.3 pad_maximum_fusion
  217.9 0.0 all-gather.17.cloned.1.call-update
  218.0 0.0 all-gather.15.cloned.1.call-start
  218.0 11.8 %collective-permute-start = (bf16[256,512]{1,0:T(8,128)(2,1)S(1)}, bf16[256,512]{1,0:T(8,128)(2,1)S(1)}, u32[]{:S(2)}, u32[]{:S(2)}) collective-permute-start(bf16[256,512]{1,0:T(8,128)(2,1)S(1)} %copy-done.14), channel_id=1, source_target_pairs={{0,8},{8,16},{16,24},{24,0},{1,9},{9,17},{17,25},{25,1},{2,10},{10... | collective-permute-start | bytes 786440 | tf_op jit(solution)/shard_map/ppermute | solution.py:514
  229.8 0.0 collective-permute-start.1
  229.8 2.4 collective-permute-start.2
  232.2 1.4 slice.15
  233.7 0.6 fusion
  235.6 0.7 stack.23.info
  236.2 25.4 %shard_map.68.i0_ref = f32[512,512]{1,0:T(8,128)} custom-call(s32[7]{0:T(128)} %stack.23.info, bf16[1024,2048]{1,0:T(8,128)(2,1)} %get-tuple-element.35.s0_ref.s1_ref.sj_ref, f32[1,2048]{1,0:T(1,128)} %bitcast.36), custom_call_target="tpu_custom_call" | custom-call | flops 20000000000 | bytes 8388608 | tf_op jit(solution)/shard_map/pallas_call | solution.py:164
  261.7 29.9 %shard_map.69 = (bf16[512,512]{1,0:T(8,128)(2,1)}, bf16[512,512]{1,0:T(8,128)(2,1)}, f32[512,512]{1,0:T(8,128)}) custom-call(s32[7]{0:T(128)} %stack.23.info, bf16[1024,2048]{1,0:T(8,128)(2,1)} %get-tuple-element.35.s0_ref.s1_ref.sj_ref, bf16[1024,2048]{1,0:T(8,128)(2,1)} %get-tuple-element.35.s0_ref.s1_ref.sj_ref, ...), custom_call_target="tpu_custom_call" | custom-call | flops 24000000000 | bytes 8388608 | tf_op jit(solution)/shard_map/pallas_call | solution.py:164
  291.6 0.0 collective-permute-done
  291.6 0.0 collective-permute-done.1
  291.6 0.0 collective-permute-done.2
  291.6 0.9 pad_maximum_fusion.3
  292.5 0.0 all-gather.15.cloned.1.call-update
  292.6 21.7 %shard_map.70 = (bf16[1024,1536]{1,0:T(8,128)(2,1)}, f32[1024,1536]{1,0:T(8,128)}) custom-call(s32[7]{0:T(128)} %stack.23.info, bf16[1024,2048]{1,0:T(8,128)(2,1)} %get-tuple-element.35.s0_ref.s1_ref.sj_ref, bf16[1024,2048]{1,0:T(8,128)(2,1)} %get-tuple-element.35.s0_ref.s1_ref.sj_ref, bf16[1024,2048]{1,0:T(8,128)(2,1)} %get-tuple-element.35.s0_ref.s1_ref.sj_ref, ...), custom_call_target="tpu_custom_call" | custom-call | flops 15000000512 | bytes 8388608 | tf_op jit(solution)/shard_map/pallas_call | solution.py:164
  314.3 0.0 all-gather.13.cloned.1.call-done
  314.3 1.9 copy-done.3
  316.2 13.4 %final.5 = (f32[16384,512]{1,0:T(8,128)}, bf16[2,16384,512]{2,1,0:T(8,128)(2,1)}) custom-call(s32[7]{0:T(128)S(1)} %copy-done.2, bf16[4,256,4096]{2,1,0:T(8,128)(2,1)} %bitcast.26, bf16[4,768,512]{2,1,0:T(8,128)(2,1)S(1)} %bitcast.25, bf16[1024,1536]{1,0:T(8,128)(2,1)} %get-tuple-element.40.p_ref, f32[1024,1536]{1,0:T(8,128)} %get-tuple-element.41.d_ref, ...), custom_call_target="tpu_custom_call" | custom-call | flops 6442450944 | bytes 12582912 | tf_op jit(solution)/shard_map/final/pallas_call | solution.py:454
  329.6 20.7 %final.6 = (f32[16384,512]{1,0:T(8,128)}, bf16[2,16384,512]{2,1,0:T(8,128)(2,1)}) custom-call(s32[7]{0:T(128)S(1)} %copy-done.2, bf16[4,256,4096]{2,1,0:T(8,128)(2,1)} %bitcast.27, bf16[4,768,1024]{2,1,0:T(8,128)(2,1)} %bitcast.33, bf16[1024,1536]{1,0:T(8,128)(2,1)S(1)} %copy-done, ...), custom_call_target="tpu_custom_call", output_to_operand_aliasing={{0}: (6, {}), {1}: (7, {})} | custom-call | flops 12884901888 | bytes 25165824 | tf_op jit(solution)/shard_map/final/pallas_call | solution.py:454
  350.3 20.6 %final.7 = (f32[16384,512]{1,0:T(8,128)}, bf16[2,16384,512]{2,1,0:T(8,128)(2,1)}) custom-call(s32[7]{0:T(128)S(1)} %copy-done.2, bf16[4,256,4096]{2,1,0:T(8,128)(2,1)} %bitcast.28, bf16[4,768,1024]{2,1,0:T(8,128)(2,1)} %bitcast.34, bf16[1024,1536]{1,0:T(8,128)(2,1)S(1)} %copy-done, ...), custom_call_target="tpu_custom_call", output_to_operand_aliasing={{0}: (6, {}), {1}: (7, {})} | custom-call | flops 12884901888 | bytes 25165824 | tf_op jit(solution)/shard_map/final/pallas_call | solution.py:454
  370.8 20.6 %final.8 = (f32[16384,512]{1,0:T(8,128)}, bf16[2,16384,512]{2,1,0:T(8,128)(2,1)}) custom-call(s32[7]{0:T(128)S(1)} %copy-done.2, bf16[4,256,4096]{2,1,0:T(8,128)(2,1)} %bitcast.29, bf16[4,768,1024]{2,1,0:T(8,128)(2,1)} %bitcast.35, bf16[1024,1536]{1,0:T(8,128)(2,1)S(1)} %copy-done, ...), custom_call_target="tpu_custom_call", output_to_operand_aliasing={{0}: (6, {}), {1}: (7, {})} | custom-call | flops 12884901888 | bytes 25165824 | tf_op jit(solution)/shard_map/final/pallas_call | solution.py:454
  391.4 1.9 copy-done.1
  393.3 13.0 %final.9 = (f32[16384,512]{1,0:T(8,128)}, bf16[2,16384,512]{2,1,0:T(8,128)(2,1)}) custom-call(s32[7]{0:T(128)S(1)} %copy-done.2, bf16[4,256,4096]{2,1,0:T(8,128)(2,1)} %bitcast.30, bf16[4,768,512]{2,1,0:T(8,128)(2,1)S(1)} %bitcast.19, bf16[1024,1536]{1,0:T(8,128)(2,1)} %get-tuple-element.40.p_ref, ...), custom_call_target="tpu_custom_call", output_to_operand_aliasing={{0}: (6, {}), {1}: (7, {})} | custom-call | flops 6442450944 | bytes 12582912 | tf_op jit(solution)/shard_map/final/pallas_call | solution.py:454
  (30 shorter events, 0.1 us)
Async XLA Ops:
  7.2 307.1 %all-gather.23.cloned.1.call-start = ((), (), s32[]{:S(2)}) async-start(), calls=%async_computation.5 | async-start | bytes 3932160 | tf_op jit(solution)/shard_map/all_gather | solution.py:517
  8.6 4.8 %copy-start.4 = (f32[512]{0:T(512)S(1)}, f32[512]{0:T(512)}, u32[]{:S(2)}) copy-start(f32[512]{0:T(512)} %param.7) | copy-start | bytes 6148
  71.2 243.1 %all-gather.13.cloned.1.call-start = ((), (), s32[]{:S(2)}) async-start(), calls=%async_computation | async-start | bytes 10485760 | tf_op jit(solution)/shard_map/all_gather | solution.py:508
  71.2 40.9 %copy-start.11 = (bf16[256,1024]{1,0:T(8,128)(2,1)S(1)}, bf16[256,1024]{1,0:T(8,128)(2,1)}, u32[]{:S(2)}) copy-start(bf16[256,1024]{1,0:T(8,128)(2,1)} %get-tuple-element.45) | copy-start | bytes 1572868
  71.2 62.8 %copy-start.10 = (bf16[256,1024]{1,0:T(8,128)(2,1)S(1)}, bf16[256,1024]{1,0:T(8,128)(2,1)}, u32[]{:S(2)}) copy-start(bf16[256,1024]{1,0:T(8,128)(2,1)} %get-tuple-element.46) | copy-start | bytes 1572868
  71.2 62.8 %copy-start.9 = (bf16[256,1024]{1,0:T(8,128)(2,1)S(1)}, bf16[256,1024]{1,0:T(8,128)(2,1)}, u32[]{:S(2)}) copy-start(bf16[256,1024]{1,0:T(8,128)(2,1)} %get-tuple-element.47) | copy-start | bytes 1572868
  71.9 257.6 %all-gather.21.cloned.1.call-start = ((), (), s32[]{:S(2)}) async-start(), calls=%async_computation.4 | async-start | bytes 7864320 | tf_op jit(solution)/shard_map/all_gather | solution.py:517
  72.0 27.9 %collective-permute-start.10 = (bf16[256,1024]{1,0:T(8,128)(2,1)}, bf16[256,1024]{1,0:T(8,128)(2,1)S(1)}, u32[]{:S(2)}, u32[]{:S(2)}) collective-permute-start(bf16[256,1024]{1,0:T(8,128)(2,1)} %get-tuple-element.49), channel_id=1, source_target_pairs={{0,16},{8,24},{16,0},{24,8},{1,17},{9,25},{17,1},{25,9},{2,18},{10... | collective-permute-start | bytes 1572872 | tf_op jit(solution)/shard_map/ppermute | solution.py:514
  73.4 26.5 %collective-permute-start.11 = (bf16[256,1024]{1,0:T(8,128)(2,1)}, bf16[256,1024]{1,0:T(8,128)(2,1)S(1)}, u32[]{:S(2)}, u32[]{:S(2)}) collective-permute-start(bf16[256,1024]{1,0:T(8,128)(2,1)} %get-tuple-element.50), channel_id=1, source_target_pairs={{0,24},{8,0},{16,8},{24,16},{1,25},{9,1},{17,9},{25,17},{2,26},{10... | collective-permute-start | bytes 1572872 | tf_op jit(solution)/shard_map/ppermute | solution.py:514
  76.1 34.7 %collective-permute-start.9 = (bf16[256,1024]{1,0:T(8,128)(2,1)}, bf16[256,1024]{1,0:T(8,128)(2,1)S(1)}, u32[]{:S(2)}, u32[]{:S(2)}) collective-permute-start(bf16[256,1024]{1,0:T(8,128)(2,1)} %get-tuple-element.48), channel_id=1, source_target_pairs={{0,8},{8,16},{16,24},{24,0},{1,9},{9,17},{17,25},{25,1},{2,10},{10... | collective-permute-start | bytes 1572872 | tf_op jit(solution)/shard_map/ppermute | solution.py:514
  112.1 56.7 %copy-start.8 = (bf16[256,1024]{1,0:T(8,128)(2,1)S(1)}, bf16[256,1024]{1,0:T(8,128)(2,1)}, u32[]{:S(2)}) copy-start(bf16[256,1024]{1,0:T(8,128)(2,1)} %get-tuple-element.42) | copy-start | bytes 1572868
  112.1 68.2 %copy-start.7 = (bf16[256,1024]{1,0:T(8,128)(2,1)S(1)}, bf16[256,1024]{1,0:T(8,128)(2,1)}, u32[]{:S(2)}) copy-start(bf16[256,1024]{1,0:T(8,128)(2,1)} %get-tuple-element.43) | copy-start | bytes 1572868
  112.1 71.6 %copy-start.6 = (bf16[256,1024]{1,0:T(8,128)(2,1)S(1)}, bf16[256,1024]{1,0:T(8,128)(2,1)}, u32[]{:S(2)}) copy-start(bf16[256,1024]{1,0:T(8,128)(2,1)} %get-tuple-element.44) | copy-start | bytes 1572868
  112.1 238.2 %all-gather.19.cloned.1.call-start = ((), (), s32[]{:S(2)}) async-start(), calls=%async_computation.3 | async-start | bytes 7864320 | tf_op jit(solution)/shard_map/all_gather | solution.py:517
  112.2 34.2 %collective-permute-start.6 = (bf16[256,1024]{1,0:T(8,128)(2,1)S(1)}, bf16[256,1024]{1,0:T(8,128)(2,1)S(1)}, u32[]{:S(2)}, u32[]{:S(2)}) collective-permute-start(bf16[256,1024]{1,0:T(8,128)(2,1)S(1)} %copy-done.11), channel_id=1, source_target_pairs={{0,8},{8,16},{16,24},{24,0},{1,9},{9,17},{17,25},{25,1},{2,10},{10... | collective-permute-start | bytes 1572872 | tf_op jit(solution)/shard_map/ppermute | solution.py:514
  134.1 25.0 %collective-permute-start.7 = (bf16[256,1024]{1,0:T(8,128)(2,1)S(1)}, bf16[256,1024]{1,0:T(8,128)(2,1)S(1)}, u32[]{:S(2)}, u32[]{:S(2)}) collective-permute-start(bf16[256,1024]{1,0:T(8,128)(2,1)S(1)} %copy-done.10), channel_id=1, source_target_pairs={{0,16},{8,24},{16,0},{24,8},{1,17},{9,25},{17,1},{25,9},{2,18},{10... | collective-permute-start | bytes 1572872 | tf_op jit(solution)/shard_map/ppermute | solution.py:514
  134.1 33.3 %collective-permute-start.8 = (bf16[256,1024]{1,0:T(8,128)(2,1)S(1)}, bf16[256,1024]{1,0:T(8,128)(2,1)S(1)}, u32[]{:S(2)}, u32[]{:S(2)}) collective-permute-start(bf16[256,1024]{1,0:T(8,128)(2,1)S(1)} %copy-done.9), channel_id=1, source_target_pairs={{0,24},{8,0},{16,8},{24,16},{1,25},{9,1},{17,9},{25,17},{2,26},{10... | collective-permute-start | bytes 1572872 | tf_op jit(solution)/shard_map/ppermute | solution.py:514
  168.6 49.4 %copy-start.14 = (bf16[256,512]{1,0:T(8,128)(2,1)S(1)}, bf16[256,512]{1,0:T(8,128)(2,1)}, u32[]{:S(2)}) copy-start(bf16[256,512]{1,0:T(8,128)(2,1)} %get-tuple-element.32) | copy-start | bytes 786436
  168.6 61.1 %copy-start.13 = (bf16[256,512]{1,0:T(8,128)(2,1)S(1)}, bf16[256,512]{1,0:T(8,128)(2,1)}, u32[]{:S(2)}) copy-start(bf16[256,512]{1,0:T(8,128)(2,1)} %get-tuple-element.33) | copy-start | bytes 786436
  168.6 61.1 %copy-start.12 = (bf16[256,512]{1,0:T(8,128)(2,1)S(1)}, bf16[256,512]{1,0:T(8,128)(2,1)}, u32[]{:S(2)}) copy-start(bf16[256,512]{1,0:T(8,128)(2,1)} %get-tuple-element.34) | copy-start | bytes 786436
  168.6 65.0 %copy-start.5 = (s32[4]{0:T(128)S(1)}, s32[4]{0:T(128)}, u32[]{:S(2)}) copy-start(s32[4]{0:T(128)} %param.9) | copy-start | bytes 52
  168.7 202.2 %all-gather.17.cloned.1.call-start = ((), (), s32[]{:S(2)}) async-start(), calls=%async_computation.2 | async-start | bytes 7864320 | tf_op jit(solution)/shard_map/all_gather | solution.py:517
  168.7 27.3 %collective-permute-start.3 = (bf16[256,1024]{1,0:T(8,128)(2,1)S(1)}, bf16[256,1024]{1,0:T(8,128)(2,1)S(1)}, u32[]{:S(2)}, u32[]{:S(2)}) collective-permute-start(bf16[256,1024]{1,0:T(8,128)(2,1)S(1)} %copy-done.8), channel_id=1, source_target_pairs={{0,8},{8,16},{16,24},{24,0},{1,9},{9,17},{17,25},{25,1},{2,10},{10... | collective-permute-start | bytes 1572872 | tf_op jit(solution)/shard_map/ppermute | solution.py:514
  180.3 36.4 %collective-permute-start.4 = (bf16[256,1024]{1,0:T(8,128)(2,1)S(1)}, bf16[256,1024]{1,0:T(8,128)(2,1)S(1)}, u32[]{:S(2)}, u32[]{:S(2)}) collective-permute-start(bf16[256,1024]{1,0:T(8,128)(2,1)S(1)} %copy-done.7), channel_id=1, source_target_pairs={{0,16},{8,24},{16,0},{24,8},{1,17},{9,25},{17,1},{25,9},{2,18},{10... | collective-permute-start | bytes 1572872 | tf_op jit(solution)/shard_map/ppermute | solution.py:514
  183.6 33.0 %collective-permute-start.5 = (bf16[256,1024]{1,0:T(8,128)(2,1)S(1)}, bf16[256,1024]{1,0:T(8,128)(2,1)S(1)}, u32[]{:S(2)}, u32[]{:S(2)}) collective-permute-start(bf16[256,1024]{1,0:T(8,128)(2,1)S(1)} %copy-done.6), channel_id=1, source_target_pairs={{0,24},{8,0},{16,8},{24,16},{1,25},{9,1},{17,9},{25,17},{2,26},{10... | collective-permute-start | bytes 1572872 | tf_op jit(solution)/shard_map/ppermute | solution.py:514
  218.0 173.5 %all-gather.15.cloned.1.call-start = ((), (), s32[]{:S(2)}) async-start(), calls=%async_computation.1 | async-start | bytes 3932160 | tf_op jit(solution)/shard_map/all_gather | solution.py:517
  218.0 73.6 %collective-permute-start = (bf16[256,512]{1,0:T(8,128)(2,1)S(1)}, bf16[256,512]{1,0:T(8,128)(2,1)S(1)}, u32[]{:S(2)}, u32[]{:S(2)}) collective-permute-start(bf16[256,512]{1,0:T(8,128)(2,1)S(1)} %copy-done.14), channel_id=1, source_target_pairs={{0,8},{8,16},{16,24},{24,0},{1,9},{9,17},{17,25},{25,1},{2,10},{10... | collective-permute-start | bytes 786440 | tf_op jit(solution)/shard_map/ppermute | solution.py:514
  229.8 61.8 %collective-permute-start.1 = (bf16[256,512]{1,0:T(8,128)(2,1)S(1)}, bf16[256,512]{1,0:T(8,128)(2,1)S(1)}, u32[]{:S(2)}, u32[]{:S(2)}) collective-permute-start(bf16[256,512]{1,0:T(8,128)(2,1)S(1)} %copy-done.13), channel_id=1, source_target_pairs={{0,16},{8,24},{16,0},{24,8},{1,17},{9,25},{17,1},{25,9},{2,18},{10... | collective-permute-start | bytes 786440 | tf_op jit(solution)/shard_map/ppermute | solution.py:514
  229.8 61.8 %collective-permute-start.2 = (bf16[256,512]{1,0:T(8,128)(2,1)S(1)}, bf16[256,512]{1,0:T(8,128)(2,1)S(1)}, u32[]{:S(2)}, u32[]{:S(2)}) collective-permute-start(bf16[256,512]{1,0:T(8,128)(2,1)S(1)} %copy-done.12), channel_id=1, source_target_pairs={{0,24},{8,0},{16,8},{24,16},{1,25},{9,1},{17,9},{25,17},{2,26},{10... | collective-permute-start | bytes 786440 | tf_op jit(solution)/shard_map/ppermute | solution.py:514
  292.5 21.7 %copy-start.2 = (s32[7]{0:T(128)S(1)}, s32[7]{0:T(128)}, u32[]{:S(2)}) copy-start(s32[7]{0:T(128)} %stack.23.info) | copy-start | bytes 88
  314.3 1.9 copy-start.3
  316.2 13.4 %copy-start = (bf16[1024,1536]{1,0:T(8,128)(2,1)S(1)}, bf16[1024,1536]{1,0:T(8,128)(2,1)}, u32[]{:S(2)}) copy-start(bf16[1024,1536]{1,0:T(8,128)(2,1)} %get-tuple-element.40.p_ref) | copy-start | bytes 9437188
  391.4 1.9 copy-start.1
Sparse Core Ops, SparseCore 0:
  71.3 28.4 all-gather.22
  101.3 58.2 all-gather.12
  161.2 46.3 all-gather.20
  209.0 46.3 all-gather.18
  256.8 46.3 all-gather.16
  304.6 28.4 all-gather.14

commit v3 on v2

--- a/solution.py
+++ b/solution.py
@@ -9,6 +9,7 @@
 
 NB = 128
 SUB = 8
+HOPS = (1, 3)
 HIGH = lax.Precision.HIGHEST
 MESH = pl.DeviceIdType.MESH
 NN = (((1,), (0,)), ((), ()))
@@ -393,12 +394,21 @@
     )(info, x)
 
 
-def final_body(chunk_base, info, own_ref, rest_ref, p_ref, d_ref, r_ref, *rest):
-    t_ref, f_ref = rest[-2:]
+def final_body(chunk_base, units, info, own_ref, *refs):
+    p_ref, d_ref, r_ref = refs[units:units + 3]
+    rest_ref = refs[0]
+    if units > 1:
+        t_ref, f_ref, rest_ref = refs[-3:]
+        for u in range(units):
+            @pl.when(pl.program_id(0) == u)
+            def _():
+                rest_ref[0] = refs[u][...]
+    else:
+        t_ref, f_ref = refs[-2:]
     _, width = t_ref.shape
     times = own_ref.shape[1]
     acc = mm(own_ref[0], p_ref[:times, :], TN) + mm(rest_ref[0], p_ref[times:, :], TN)
-    kind = kind_of(info, chunk_base(pl.program_id(0), pl.program_id(1)))
+    kind = kind_of(info, chunk_base(pl.program_id(0), pl.program_id(1), info))
 
     def put(first, second, last):
         f_ref[0] = first.astype(f_ref.dtype)
@@ -430,37 +440,52 @@
 def final_chunk(info, own, others, weights, d, ridge, prior, start, width):
     cols, times, local = own.shape
     bm = width
-    w = others.shape[2]
+    units = len(others)
+    w = others[0].shape[-1]
+    rest = others[0].shape[-2]
     per = w // bm
     rows = cols * local
-    rest = others.shape[1]
-
-    def base(c, i):
-        return c * (local // bm) + start // bm + i
+
+    def column(c, info):
+        if units == 1:
+            return c
+        far, bits = 0, units.bit_length() - 1
+        for b in range(bits):
+            far = far + (((c >> b) & 1) << (bits - 1 - b))
+        return info[2] ^ far
+
+    def base(c, i, info):
+        return column(c, info) * (local // bm) + start // bm + i
+
+    def unit_spec(u):
+        if units == 1:
+            return pl.BlockSpec((1, rest, bm), lambda c, i, info: (c, 0, i))
+        return pl.BlockSpec((rest, bm), lambda c, i, info: (0, jnp.where(c == u, i, jnp.where(c > u, per - 1, 0))))
 
     in_specs = [
-        pl.BlockSpec((1, times, bm), lambda c, i, info: (c, 0, start // bm + i)),
-        pl.BlockSpec((1, rest, bm), lambda c, i, info: (c, 0, i)),
+        pl.BlockSpec((1, times, bm), lambda c, i, info: (column(c, info), 0, start // bm + i)),
+        *[unit_spec(u) for u in range(units)],
         pl.BlockSpec(weights.shape, lambda c, i, info: (0, 0)),
-        pl.BlockSpec((bm, 3 * width), lambda c, i, info: (jnp.where(kind_of(info, base(c, i)) == 1, 1, 0), 0)),
+        pl.BlockSpec((bm, 3 * width), lambda c, i, info: (jnp.where(kind_of(info, base(c, i, info)) == 1, 1, 0), 0)),
         pl.BlockSpec((1, width), lambda c, i, info: (0, 0)),
     ]
-    operands = [info, own, others, weights, d, ridge]
+    operands = [info, own, *others, weights, d, ridge]
     aliases = {}
     if prior is not None:
         in_specs += [pl.BlockSpec(memory_space=pl.ANY)] * 2
         aliases = {len(operands): 0, len(operands) + 1: 1}
         operands += list(prior)
     return pl.pallas_call(
-        functools.partial(final_body, base),
+        functools.partial(final_body, base, units),
         grid_spec=pltpu.PrefetchScalarGridSpec(
             num_scalar_prefetch=1,
             grid=(cols, per),
             in_specs=in_specs,
             out_specs=[
-                pl.BlockSpec((bm, width), lambda c, i, info: (base(c, i), 0)),
-                pl.BlockSpec((2, bm, width), lambda c, i, info: (0, base(c, i), 0)),
+                pl.BlockSpec((bm, width), lambda c, i, info: (base(c, i, info), 0)),
+                pl.BlockSpec((2, bm, width), lambda c, i, info: (0, base(c, i, info), 0)),
             ],
+            scratch_shapes=[pltpu.VMEM((1, rest, bm), jnp.bfloat16)] if units > 1 else [],
         ),
         out_shape=[
             jax.ShapeDtypeStruct((rows, width), jnp.float32),
@@ -476,6 +501,15 @@
     )(*operands)
 
 
+def hop_gather(block, cols):
+    held = [block]
+    bit = cols // 2
+    while bit:
+        held = held + [lax.ppermute(h, "col", [(i, i ^ bit) for i in range(cols)]) for h in held]
+        bit //= 2
+    return held
+
+
 def on_device(samples, whitening, ridge, slab_start, panels):
     times, groups, _, local = samples.shape
     rows = lax.axis_size("row")
@@ -507,6 +541,7 @@
     ridges = ridges[:, 0].reshape(1, slab)
     own = lax.all_gather(own, "col", axis=0)
     others = []
+    hops = HOPS if len(sizes) == 5 and cols & (cols - 1) == 0 else ()
     for c in range(len(sizes)):
         block = pieces[c * (rows - 1):(c + 1) * (rows - 1)]
         if c:
@@ -514,7 +549,10 @@
                 lax.ppermute(block[s - 1], "row", [(i, (i + s) % rows) for i in range(rows)])
                 for s in range(1, rows)
             ], axis=0)
-        others.append(lax.all_gather(head, "col", axis=0))
+        if c in hops:
+            others.append(hop_gather(head, cols))
+        else:
+            others.append([lax.all_gather(head, "col", axis=0)])
 
     q0, q1 = panels[0], panels[1]
     owner = (me_row == group) & (me_tm == tm_owner)

time: 421 us -> 438 us (1.040)
  the two profiles are of different devices: /device:TPU:0 before, /device:TPU:31 now
where the time goes in v3:
time: 438 us; the launch traced here: 431 us
  Pallas kernels  230 us (53%)
  starting transfers between devices  86.6 us (20%)
  waiting for transfers between devices  81 us (18%)
  between operations  16.2 us (4%)
  local copies, waits for them, and re-layouts  14.3 us (3%)
    pallas_call x5, Pallas kernels, final_chunk(): pl.pallas_call(functools.partial(final_body, base, units), grid_spec=pltp...  94 us
    ppermute x12, starting transfers between devices, on_device(): lax.ppermute(block[s - 1], 'row', [(i, (i + s) % rows) for i in range(row...  80.3 us
    pallas_call x3, Pallas kernels, chain_call(): pl.pallas_call(kernel, grid_spec=pltpu.PrefetchScalarGridSpec(num_scalar_...  76.8 us
    pallas_call x1, Pallas kernels, gather_slab(): pl.pallas_call(functools.partial(gather_kernel, row_n, col_n, tm_n, start...  54.8 us
    ppermute x12, waiting for transfers between devices, on_device(): lax.ppermute(block[s - 1], 'row', [(i, (i + s) % rows) for i in range(row...  50.3 us
    ppermute x6, waiting for transfers between devices, hop_gather(): lax.ppermute(h, 'col', [(i, i ^ bit) for i in range(cols)])  30 us
    unnamed x32, local copies, waits for them, and re-layouts  9.07 us
  transfers between devices with their start and end apart: 22, of which 4 were waited for; matrix products, arithmetic and copies ran while one was open for 2% of the time, Pallas kernels for 37%

profile of v3, /device:TPU:31, one launch (start us, length us, event | category | flops | bytes accessed | tf_op | source)
XLA Modules:
  0.0 431.4 jit_solution(7786661867562863157)
XLA Ops:
  7.2 0.0 all-gather.15.cloned.1.call-start
  8.0 0.6 pad_add_fusion.info
  8.6 4.8 %pick_blocks.1.part = bf16[256,2048]{1,0:T(8,128)(2,1)} custom-call(s32[9]{0:T(128)} %pad_add_fusion.info, bf16[256,4,4096]{2,1,0:T(4,128)(2,1)} %bitcast.29), custom_call_target="tpu_custom_call" | custom-call | bytes 8388608 | tf_op jit(solution)/shard_map/pick_blocks/pallas_call | solution.py:383
  13.4 0.6 broadcast_in_dim.3.ridge
  14.0 54.8 %gather_slab.1 = (bf16[1024,2048]{1,0:T(8,128)(2,1)}, f32[4,8,512]{2,1,0:T(8,128)}, bf16[256,4096]{1,0:T(8,128)(2,1)}, bf16[768,512]{1,0:T(8,128)(2,1)}, bf16[25...) custom-call(bf16[256,2048]{1,0:T(8,128)(2,1)} %pick_blocks.1.part, ...), custom_call_target="tpu_custom_call" | custom-call | flops 40000000000 | bytes 1048576 | tf_op jit(solution)/shard_map/gather_slab/pallas_call | solution.py:336
  68.8 0.0 all-gather.15.cloned.1.call-update
  68.9 0.0 all-gather.9.cloned.1.call-start
  68.9 0.7 all-gather.9.cloned.1.call-update
  69.6 0.0 all-gather.13.cloned.1.call-start
  69.7 0.2 copy-done.13
  69.8 0.0 collective-permute-start.10
  69.8 0.2 copy-done.12
  70.0 0.5 collective-permute-start.11
  70.5 2.8 collective-permute-start.9
  73.3 33.8 %collective-permute-done.10 = bf16[256,1024]{1,0:T(8,128)(2,1)S(1)} collective-permute-done((bf16[256,1024]{1,0:T(8,128)(2,1)S(1)}, bf16[256,1024]{1,0:T(8,128)(2,1)S(1)}, u32[]{:S(2)}, u32[]{:S(2)}) %collective-permute-start.10) | collective-permute-done | bytes 524320 | tf_op jit(solution)/shard_map/ppermute | solution.py:549
  107.0 0.0 collective-permute-done.11
  107.0 0.0 collective-permute-done.9
  107.0 1.3 pad_maximum_fusion
  108.3 0.0 all-gather.13.cloned.1.call-update
  108.3 0.0 all-gather.11.cloned.1.call-start
  108.4 1.1 copy-done.10
  109.5 0.4 collective-permute-start.12
  109.9 21.0 %collective-permute-start.13 = (bf16[256,1024]{1,0:T(8,128)(2,1)}, bf16[256,1024]{1,0:T(8,128)(2,1)S(1)}, u32[]{:S(2)}, u32[]{:S(2)}) collective-permute-start(bf16[256,1024]{1,0:T(8,128)(2,1)} %get-tuple-element.49), channel_id=1, source_target_pairs={{0,16},{8,24},{16,0},{24,8},{1,17},{9,25},{17,1},{25,9},{2,18},{10... | collective-permute-start | bytes 1572872 | tf_op jit(solution)/shard_map/ppermute | solution.py:549
  130.9 1.5 collective-permute-start.14
  132.4 1.8 collective-permute-start.3
  134.2 0.3 collective-permute-start
  134.5 1.4 slice.15
  135.9 0.6 fusion
  137.8 0.7 stack.23.info
  138.5 25.0 %shard_map.68.i0_ref = f32[512,512]{1,0:T(8,128)} custom-call(s32[7]{0:T(128)} %stack.23.info, bf16[1024,2048]{1,0:T(8,128)(2,1)} %get-tuple-element.35.s0_ref.s1_ref.sj_ref, f32[1,2048]{1,0:T(1,128)} %bitcast.32), custom_call_target="tpu_custom_call" | custom-call | flops 20000000000 | bytes 8388608 | tf_op jit(solution)/shard_map/pallas_call | solution.py:165
  163.4 0.0 collective-permute-done.12
  163.4 0.8 collective-permute-start.1
  164.3 11.7 %collective-permute-done.13 = bf16[256,1024]{1,0:T(8,128)(2,1)S(1)} collective-permute-done((bf16[256,1024]{1,0:T(8,128)(2,1)}, bf16[256,1024]{1,0:T(8,128)(2,1)S(1)}, u32[]{:S(2)}, u32[]{:S(2)}) %collective-permute-start.13) | collective-permute-done | bytes 524320 | tf_op jit(solution)/shard_map/ppermute | solution.py:549
  176.0 0.0 collective-permute-start.4
  176.0 0.0 collective-permute-done.14
  176.1 24.2 %collective-permute-start.5 = (bf16[256,1024]{1,0:T(8,128)(2,1)}, bf16[256,1024]{1,0:T(8,128)(2,1)}, u32[]{:S(2)}, u32[]{:S(2)}) collective-permute-start(bf16[256,1024]{1,0:T(8,128)(2,1)} %get-tuple-element.44), channel_id=1, source_target_pairs={{0,24},{8,0},{16,8},{24,16},{1,25},{9,1},{17,9},{25,17},{2,26},{10... | collective-permute-start | bytes 1572872 | tf_op jit(solution)/shard_map/ppermute | solution.py:549
  200.3 0.0 collective-permute-done
  200.3 27.1 %collective-permute-start.2 = (bf16[256,512]{1,0:T(8,128)(2,1)}, bf16[256,512]{1,0:T(8,128)(2,1)S(1)}, u32[]{:S(2)}, u32[]{:S(2)}) collective-permute-start(bf16[256,512]{1,0:T(8,128)(2,1)} %get-tuple-element.34), channel_id=1, source_target_pairs={{0,24},{8,0},{16,8},{24,16},{1,25},{9,1},{17,9},{25,17},{2,26},{10... | collective-permute-start | bytes 786440 | tf_op jit(solution)/shard_map/ppermute | solution.py:549
  227.3 4.8 %collective-permute-done.1 = bf16[256,512]{1,0:T(8,128)(2,1)S(1)} collective-permute-done((bf16[256,512]{1,0:T(8,128)(2,1)}, bf16[256,512]{1,0:T(8,128)(2,1)S(1)}, u32[]{:S(2)}, u32[]{:S(2)}) %collective-permute-start.1) | collective-permute-done | bytes 262176 | tf_op jit(solution)/shard_map/ppermute | solution.py:549
  232.2 2.4 collective-permute-start.15
  234.6 29.4 %shard_map.69 = (bf16[512,512]{1,0:T(8,128)(2,1)}, bf16[512,512]{1,0:T(8,128)(2,1)}, f32[512,512]{1,0:T(8,128)}) custom-call(s32[7]{0:T(128)} %stack.23.info, bf16[1024,2048]{1,0:T(8,128)(2,1)} %get-tuple-element.35.s0_ref.s1_ref.sj_ref, bf16[1024,2048]{1,0:T(8,128)(2,1)} %get-tuple-element.35.s0_ref.s1_ref.sj_ref, ...), custom_call_target="tpu_custom_call" | custom-call | flops 24000000000 | bytes 8388608 | tf_op jit(solution)/shard_map/pallas_call | solution.py:165
  263.9 0.0 collective-permute-done.2
  263.9 1.0 pad_maximum_fusion.1
  264.9 0.0 all-gather.11.cloned.1.call-update
  265.0 2.2 collective-permute-start.16
  267.2 0.0 collective-permute-done.3
  267.2 1.9 constant_dynamic-update-slice_fusion.2
  269.1 0.0 collective-permute-done.4
  269.1 1.9 constant_dynamic-update-slice_fusion.1
  271.0 0.0 collective-permute-done.5
  271.0 1.9 constant_dynamic-update-slice_fusion.refs_0_
  272.8 0.2 collective-permute-start.17
  273.0 22.5 %shard_map.70 = (bf16[1024,1536]{1,0:T(8,128)(2,1)}, f32[1024,1536]{1,0:T(8,128)}) custom-call(s32[7]{0:T(128)} %stack.23.info, bf16[1024,2048]{1,0:T(8,128)(2,1)} %get-tuple-element.35.s0_ref.s1_ref.sj_ref, bf16[1024,2048]{1,0:T(8,128)(2,1)} %get-tuple-element.35.s0_ref.s1_ref.sj_ref, bf16[1024,2048]{1,0:T(8,128)(2,1)} %get-tuple-element.35.s0_ref.s1_ref.sj_ref, ...), custom_call_target="tpu_custom_call" | custom-call | flops 15000000512 | bytes 8388608 | tf_op jit(solution)/shard_map/pallas_call | solution.py:165
  295.5 0.5 collective-permute-start.7
  296.0 30.0 %collective-permute-done.6.refs_1_ = bf16[768,1024]{1,0:T(8,128)(2,1)} collective-permute-done((bf16[768,1024]{1,0:T(8,128)(2,1)}, bf16[768,1024]{1,0:T(8,128)(2,1)}, u32[]{:S(2)}, u32[]{:S(2)}) %collective-permute-start.6) | collective-permute-done | bytes 1572896 | tf_op jit(solution)/shard_map/ppermute | solution.py:508
  325.9 0.9 collective-permute-start.8
  326.8 1.9 copy-done.7
  328.7 13.3 %final.5 = (f32[16384,512]{1,0:T(8,128)}, bf16[2,16384,512]{2,1,0:T(8,128)(2,1)}) custom-call(s32[7]{0:T(128)S(1)} %copy-done.6, bf16[4,256,4096]{2,1,0:T(8,128)(2,1)} %bitcast.24, bf16[4,768,512]{2,1,0:T(8,128)(2,1)S(1)} %bitcast.23, bf16[1024,1536]{1,0:T(8,128)(2,1)} %get-tuple-element.40.refs_1_.refs_4_, f32[1024,1536]{1,0:T(8,128)} %get-tuple-element.41.refs_2_.refs_5_, ...), custom_call_target="tpu_custom_call" | custom-call | flops 6442450944 | bytes 12582912 | tf_op jit(solution)/shard_map/final/pallas_call | solution.py:478
  342.0 0.0 collective-permute-done.16.refs_2_
  342.1 23.3 %final.6 = (f32[16384,512]{1,0:T(8,128)}, bf16[2,16384,512]{2,1,0:T(8,128)(2,1)}) custom-call(s32[7]{0:T(128)S(1)} %copy-done.6, bf16[4,256,4096]{2,1,0:T(8,128)(2,1)} %bitcast.25, bf16[768,1024]{1,0:T(8,128)(2,1)S(1)} %copy-done.3, bf16[768,1024]{1,0:T(8,128)(2,1)S(1)} %copy-done.5, ...), custom_call_target="tpu_custom_call", output_to_operand_aliasing={{0}: (9, {}), {1}: (10, {})} | custom-call | flops 12884901888 | bytes 25165824 | tf_op jit(solution)/shard_map/final/pallas_call | solution.py:478
  365.4 20.6 %final.7 = (f32[16384,512]{1,0:T(8,128)}, bf16[2,16384,512]{2,1,0:T(8,128)(2,1)}) custom-call(s32[7]{0:T(128)S(1)} %copy-done.6, bf16[4,256,4096]{2,1,0:T(8,128)(2,1)} %bitcast.26, bf16[4,768,1024]{2,1,0:T(8,128)(2,1)} %bitcast.31, bf16[1024,1536]{1,0:T(8,128)(2,1)S(1)} %copy-done, ...), custom_call_target="tpu_custom_call", output_to_operand_aliasing={{0}: (6, {}), {1}: (7, {})} | custom-call | flops 12884901888 | bytes 25165824 | tf_op jit(solution)/shard_map/final/pallas_call | solution.py:478
  386.0 23.8 %final.8 = (f32[16384,512]{1,0:T(8,128)}, bf16[2,16384,512]{2,1,0:T(8,128)(2,1)}) custom-call(s32[7]{0:T(128)S(1)} %copy-done.6, bf16[4,256,4096]{2,1,0:T(8,128)(2,1)} %bitcast.27, bf16[768,1024]{1,0:T(8,128)(2,1)} %constant_dynamic-update-slice_fusion.refs_0_, ...), custom_call_target="tpu_custom_call", output_to_operand_aliasing={{0}: (9, {}), {1}: (10, {})} | custom-call | flops 12884901888 | bytes 25165824 | tf_op jit(solution)/shard_map/final/pallas_call | solution.py:478
  409.8 1.9 copy-done.1
  411.7 13.0 %final.9 = (f32[16384,512]{1,0:T(8,128)}, bf16[2,16384,512]{2,1,0:T(8,128)(2,1)}) custom-call(s32[7]{0:T(128)S(1)} %copy-done.6, bf16[4,256,4096]{2,1,0:T(8,128)(2,1)} %bitcast.28, bf16[4,768,512]{2,1,0:T(8,128)(2,1)S(1)} %bitcast.17, bf16[1024,1536]{1,0:T(8,128)(2,1)} %get-tuple-element.40.refs_1_.refs_4_, ...), custom_call_target="tpu_custom_call", output_to_operand_aliasing={{0}: (6, {}), {1}: (7, {})} | custom-call | flops 6442450944 | bytes 12582912 | tf_op jit(solution)/shard_map/final/pallas_call | solution.py:478
  (38 shorter events, 0.2 us)
Async XLA Ops:
  7.2 319.6 %all-gather.15.cloned.1.call-start = ((), (), s32[]{:S(2)}) async-start(), calls=%async_computation.3 | async-start | bytes 3932160 | tf_op jit(solution)/shard_map/all_gather | solution.py:555
  8.6 4.8 %copy-start.8 = (f32[512]{0:T(512)S(1)}, f32[512]{0:T(512)}, u32[]{:S(2)}) copy-start(f32[512]{0:T(512)} %param.7) | copy-start | bytes 6148
  68.8 1.0 copy-start.13
  68.8 1.2 copy-start.12
  68.8 1.7 copy-start.11
  68.9 257.9 %all-gather.9.cloned.1.call-start = ((), (), s32[]{:S(2)}) async-start(), calls=%async_computation | async-start | bytes 10485760 | tf_op jit(solution)/shard_map/all_gather | solution.py:542
  69.6 295.8 %all-gather.13.cloned.1.call-start = ((), (), s32[]{:S(2)}) async-start(), calls=%async_computation.2 | async-start | bytes 7864320 | tf_op jit(solution)/shard_map/all_gather | solution.py:555
  69.8 37.2 %collective-permute-start.10 = (bf16[256,1024]{1,0:T(8,128)(2,1)S(1)}, bf16[256,1024]{1,0:T(8,128)(2,1)S(1)}, u32[]{:S(2)}, u32[]{:S(2)}) collective-permute-start(bf16[256,1024]{1,0:T(8,128)(2,1)S(1)} %copy-done.13), channel_id=1, source_target_pairs={{0,16},{8,24},{16,0},{24,8},{1,17},{9,25},{17,1},{25,9},{2,18},{10... | collective-permute-start | bytes 1572872 | tf_op jit(solution)/shard_map/ppermute | solution.py:549
  70.0 37.0 %collective-permute-start.11 = (bf16[256,1024]{1,0:T(8,128)(2,1)S(1)}, bf16[256,1024]{1,0:T(8,128)(2,1)S(1)}, u32[]{:S(2)}, u32[]{:S(2)}) collective-permute-start(bf16[256,1024]{1,0:T(8,128)(2,1)S(1)} %copy-done.12), channel_id=1, source_target_pairs={{0,24},{8,0},{16,8},{24,16},{1,25},{9,1},{17,9},{25,17},{2,26},{10... | collective-permute-start | bytes 1572872 | tf_op jit(solution)/shard_map/ppermute | solution.py:549
  70.5 36.6 %collective-permute-start.9 = (bf16[256,1024]{1,0:T(8,128)(2,1)S(1)}, bf16[256,1024]{1,0:T(8,128)(2,1)S(1)}, u32[]{:S(2)}, u32[]{:S(2)}) collective-permute-start(bf16[256,1024]{1,0:T(8,128)(2,1)S(1)} %copy-done.11), channel_id=1, source_target_pairs={{0,8},{8,16},{16,24},{24,0},{1,9},{9,17},{17,25},{25,1},{2,10},{10... | collective-permute-start | bytes 1572872 | tf_op jit(solution)/shard_map/ppermute | solution.py:549
  108.3 1.2 copy-start.10
  108.3 27.6 %copy-start.9 = (s32[4]{0:T(128)S(1)}, s32[4]{0:T(128)}, u32[]{:S(2)}) copy-start(s32[4]{0:T(128)} %param.9) | copy-start | bytes 52
  108.3 301.4 %all-gather.11.cloned.1.call-start = ((), (), s32[]{:S(2)}) async-start(), calls=%async_computation.1 | async-start | bytes 3932160 | tf_op jit(solution)/shard_map/all_gather | solution.py:555
  109.5 54.0 %collective-permute-start.12 = (bf16[256,1024]{1,0:T(8,128)(2,1)S(1)}, bf16[256,1024]{1,0:T(8,128)(2,1)S(1)}, u32[]{:S(2)}, u32[]{:S(2)}) collective-permute-start(bf16[256,1024]{1,0:T(8,128)(2,1)S(1)} %copy-done.10), channel_id=1, source_target_pairs={{0,8},{8,16},{16,24},{24,0},{1,9},{9,17},{17,25},{25,1},{2,10},{10... | collective-permute-start | bytes 1572872 | tf_op jit(solution)/shard_map/ppermute | solution.py:549
  109.9 66.1 %collective-permute-start.13 = (bf16[256,1024]{1,0:T(8,128)(2,1)}, bf16[256,1024]{1,0:T(8,128)(2,1)S(1)}, u32[]{:S(2)}, u32[]{:S(2)}) collective-permute-start(bf16[256,1024]{1,0:T(8,128)(2,1)} %get-tuple-element.49), channel_id=1, source_target_pairs={{0,16},{8,24},{16,0},{24,8},{1,17},{9,25},{17,1},{25,9},{2,18},{10... | collective-permute-start | bytes 1572872 | tf_op jit(solution)/shard_map/ppermute | solution.py:549
  130.9 45.1 %collective-permute-start.14 = (bf16[256,1024]{1,0:T(8,128)(2,1)}, bf16[256,1024]{1,0:T(8,128)(2,1)S(1)}, u32[]{:S(2)}, u32[]{:S(2)}) collective-permute-start(bf16[256,1024]{1,0:T(8,128)(2,1)} %get-tuple-element.50), channel_id=1, source_target_pairs={{0,24},{8,0},{16,8},{24,16},{1,25},{9,1},{17,9},{25,17},{2,26},{10... | collective-permute-start | bytes 1572872 | tf_op jit(solution)/shard_map/ppermute | solution.py:549
  132.4 134.8 %collective-permute-start.3 = (bf16[256,1024]{1,0:T(8,128)(2,1)}, bf16[256,1024]{1,0:T(8,128)(2,1)}, u32[]{:S(2)}, u32[]{:S(2)}) collective-permute-start(bf16[256,1024]{1,0:T(8,128)(2,1)} %get-tuple-element.42), channel_id=1, source_target_pairs={{0,8},{8,16},{16,24},{24,0},{1,9},{9,17},{17,25},{25,1},{2,10},{10... | collective-permute-start | bytes 1572872 | tf_op jit(solution)/shard_map/ppermute | solution.py:549
  134.2 66.1 %collective-permute-start = (bf16[256,512]{1,0:T(8,128)(2,1)}, bf16[256,512]{1,0:T(8,128)(2,1)S(1)}, u32[]{:S(2)}, u32[]{:S(2)}) collective-permute-start(bf16[256,512]{1,0:T(8,128)(2,1)} %get-tuple-element.32), channel_id=1, source_target_pairs={{0,8},{8,16},{16,24},{24,0},{1,9},{9,17},{17,25},{25,1},{2,10},{10... | collective-permute-start | bytes 786440 | tf_op jit(solution)/shard_map/ppermute | solution.py:549
  163.4 68.7 %collective-permute-start.1 = (bf16[256,512]{1,0:T(8,128)(2,1)}, bf16[256,512]{1,0:T(8,128)(2,1)S(1)}, u32[]{:S(2)}, u32[]{:S(2)}) collective-permute-start(bf16[256,512]{1,0:T(8,128)(2,1)} %get-tuple-element.33), channel_id=1, source_target_pairs={{0,16},{8,24},{16,0},{24,8},{1,17},{9,25},{17,1},{25,9},{2,18},{10... | collective-permute-start | bytes 786440 | tf_op jit(solution)/shard_map/ppermute | solution.py:549
  176.0 93.1 %collective-permute-start.4 = (bf16[256,1024]{1,0:T(8,128)(2,1)}, bf16[256,1024]{1,0:T(8,128)(2,1)}, u32[]{:S(2)}, u32[]{:S(2)}) collective-permute-start(bf16[256,1024]{1,0:T(8,128)(2,1)} %get-tuple-element.43), channel_id=1, source_target_pairs={{0,16},{8,24},{16,0},{24,8},{1,17},{9,25},{17,1},{25,9},{2,18},{10... | collective-permute-start | bytes 1572872 | tf_op jit(solution)/shard_map/ppermute | solution.py:549
  176.1 94.9 %collective-permute-start.5 = (bf16[256,1024]{1,0:T(8,128)(2,1)}, bf16[256,1024]{1,0:T(8,128)(2,1)}, u32[]{:S(2)}, u32[]{:S(2)}) collective-permute-start(bf16[256,1024]{1,0:T(8,128)(2,1)} %get-tuple-element.44), channel_id=1, source_target_pairs={{0,24},{8,0},{16,8},{24,16},{1,25},{9,1},{17,9},{25,17},{2,26},{10... | collective-permute-start | bytes 1572872 | tf_op jit(solution)/shard_map/ppermute | solution.py:549
  200.3 64.7 %copy-start.2 = (bf16[768,1024]{1,0:T(8,128)(2,1)}, bf16[768,1024]{1,0:T(8,128)(2,1)S(1)}, u32[]{:S(2)}) copy-start(bf16[768,1024]{1,0:T(8,128)(2,1)S(1)} %constant_dynamic-update-slice_fusion.3.refs_0_) | copy-start | bytes 4718596
  200.3 63.7 %collective-permute-start.2 = (bf16[256,512]{1,0:T(8,128)(2,1)}, bf16[256,512]{1,0:T(8,128)(2,1)S(1)}, u32[]{:S(2)}, u32[]{:S(2)}) collective-permute-start(bf16[256,512]{1,0:T(8,128)(2,1)} %get-tuple-element.34), channel_id=1, source_target_pairs={{0,24},{8,0},{16,8},{24,16},{1,25},{9,1},{17,9},{25,17},{2,26},{10... | collective-permute-start | bytes 786440 | tf_op jit(solution)/shard_map/ppermute | solution.py:549
  232.2 40.6 %collective-permute-start.15 = (bf16[768,1024]{1,0:T(8,128)(2,1)S(1)}, bf16[768,1024]{1,0:T(8,128)(2,1)S(1)}, u32[]{:S(2)}, u32[]{:S(2)}) collective-permute-start(bf16[768,1024]{1,0:T(8,128)(2,1)S(1)} %constant_dynamic-update-slice_fusion.3.refs_0_), channel_id=1, source_target_pairs={{0,4},{2,6},{4,0},{6,2},{1,5},{3,7},{5,1},{7,3},{8,12},{10,14},{12... | collective-permute-start | bytes 4718600 | tf_op jit(solution)/shard_map/ppermute | solution.py:508
  265.0 77.1 %collective-permute-start.16 = (bf16[768,1024]{1,0:T(8,128)(2,1)S(1)}, bf16[768,1024]{1,0:T(8,128)(2,1)}, u32[]{:S(2)}, u32[]{:S(2)}) collective-permute-start(bf16[768,1024]{1,0:T(8,128)(2,1)S(1)} %constant_dynamic-update-slice_fusion.3.refs_0_), channel_id=1, source_target_pairs={{0,2},{2,0},{4,6},{6,4},{1,3},{3,1},{5,7},{7,5},{8,10},{10,8},{12,... | collective-permute-start | bytes 4718600 | tf_op jit(solution)/shard_map/ppermute | solution.py:508
  272.8 53.1 %collective-permute-start.6 = (bf16[768,1024]{1,0:T(8,128)(2,1)}, bf16[768,1024]{1,0:T(8,128)(2,1)}, u32[]{:S(2)}, u32[]{:S(2)}) collective-permute-start(bf16[768,1024]{1,0:T(8,128)(2,1)} %constant_dynamic-update-slice_fusion.refs_0_), channel_id=1, source_target_pairs={{0,4},{2,6},{4,0},{6,2},{1,5},{3,7},{5,1},{7,3},{8,12},{10,14},{12... | collective-permute-start | bytes 4718600 | tf_op jit(solution)/shard_map/ppermute | solution.py:508
  272.8 22.7 %copy-start.4 = (bf16[768,1024]{1,0:T(8,128)(2,1)}, bf16[768,1024]{1,0:T(8,128)(2,1)S(1)}, u32[]{:S(2)}) copy-start(bf16[768,1024]{1,0:T(8,128)(2,1)S(1)} %collective-permute-done.15.refs_1_) | copy-start | bytes 4718596
  272.8 69.2 %collective-permute-start.17 = (bf16[768,1024]{1,0:T(8,128)(2,1)S(1)}, bf16[768,1024]{1,0:T(8,128)(2,1)}, u32[]{:S(2)}, u32[]{:S(2)}) collective-permute-start(bf16[768,1024]{1,0:T(8,128)(2,1)S(1)} %collective-permute-done.15.refs_1_), channel_id=1, source_target_pairs={{0,2},{2,0},{4,6},{6,4},{1,3},{3,1},{5,7},{7,5},{8,10},{10,8},{12,... | collective-permute-start | bytes 4718600 | tf_op jit(solution)/shard_map/ppermute | solution.py:508
  273.0 53.8 %copy-start.6 = (s32[7]{0:T(128)S(1)}, s32[7]{0:T(128)}, u32[]{:S(2)}) copy-start(s32[7]{0:T(128)} %stack.23.info) | copy-start | bytes 88
  295.5 90.5 %collective-permute-start.7 = (bf16[768,1024]{1,0:T(8,128)(2,1)}, bf16[768,1024]{1,0:T(8,128)(2,1)}, u32[]{:S(2)}, u32[]{:S(2)}) collective-permute-start(bf16[768,1024]{1,0:T(8,128)(2,1)} %constant_dynamic-update-slice_fusion.refs_0_), channel_id=1, source_target_pairs={{0,2},{2,0},{4,6},{6,4},{1,3},{3,1},{5,7},{7,5},{8,10},{10,8},{12,... | collective-permute-start | bytes 4718600 | tf_op jit(solution)/shard_map/ppermute | solution.py:508
  325.9 60.1 %collective-permute-start.8 = (bf16[768,1024]{1,0:T(8,128)(2,1)}, bf16[768,1024]{1,0:T(8,128)(2,1)}, u32[]{:S(2)}, u32[]{:S(2)}) collective-permute-start(bf16[768,1024]{1,0:T(8,128)(2,1)} %collective-permute-done.6.refs_1_), channel_id=1, source_target_pairs={{0,2},{2,0},{4,6},{6,4},{1,3},{3,1},{5,7},{7,5},{8,10},{10,8},{12,... | collective-permute-start | bytes 4718600 | tf_op jit(solution)/shard_map/ppermute | solution.py:508
  326.8 1.9 copy-start.7
  328.7 13.3 %copy-start.3 = (bf16[768,1024]{1,0:T(8,128)(2,1)S(1)}, bf16[768,1024]{1,0:T(8,128)(2,1)}, u32[]{:S(2)}) copy-start(bf16[768,1024]{1,0:T(8,128)(2,1)} %copy-done.2) | copy-start | bytes 4718596
  328.7 13.4 %copy-start.5 = (bf16[768,1024]{1,0:T(8,128)(2,1)S(1)}, bf16[768,1024]{1,0:T(8,128)(2,1)}, u32[]{:S(2)}) copy-start(bf16[768,1024]{1,0:T(8,128)(2,1)} %copy-done.4) | copy-start | bytes 4718596
  342.1 23.4 %copy-start = (bf16[1024,1536]{1,0:T(8,128)(2,1)S(1)}, bf16[1024,1536]{1,0:T(8,128)(2,1)}, u32[]{:S(2)}) copy-start(bf16[1024,1536]{1,0:T(8,128)(2,1)} %get-tuple-element.40.refs_1_.refs_4_) | copy-start | bytes 9437188
  409.8 1.9 copy-start.1
Sparse Core Ops, SparseCore 0:
  69.0 28.3 all-gather.14
  99.0 58.2 all-gather.8
  158.8 46.3 all-gather.12
  265.1 47.3 all-gather.10

commit v4 on v2

--- a/solution.py
+++ b/solution.py
@@ -104,54 +104,71 @@
     i0_ref[...] = work[:, size:]
 
 
-def second_kernel(scale, info, s0_ref, s1_ref, sj_ref, r0_ref, r1_ref, i0_ref, c01_ref, c0j_ref, i1_ref, work, top, held):
+def second_kernel(
+    scale, info, s0_ref, s1_ref, sj_ref, r0_ref, r1_ref, i0_ref, c01_ref, c0j_ref, i1_ref, work, top, held
+):
     size = s0_ref.shape[1]
     eye = eye_mask(size)
-    i0 = i0_ref[...]
-    c01 = mm3(i0, mm(s0_ref[...], s1_ref[...], TN) * scale).astype(jnp.bfloat16)
-    c01_ref[...] = c01
     r0 = r0_ref[...] * (info[3] == 0).astype(jnp.float32)
-    c0j_ref[...] = mm3(i0, mm(s0_ref[...], sj_ref[...], TN) * scale + jnp.where(eye, r0, 0.0)).astype(jnp.bfloat16)
-    work[:, :size] = mm(s1_ref[...], s1_ref[...], TN) * scale + jnp.where(eye, r1_ref[...], 0.0) - mm(c01, c01, TN)
+    work[:, :size] = mm(s0_ref[...], s1_ref[...], TN) * scale
+    work[:, size:] = mm(s0_ref[...], sj_ref[...], TN) * scale + jnp.where(eye, r0, 0.0)
+
+    def couple(b, carry):
+        at = pl.ds(pl.multiple_of(b * NB, NB), NB)
+        c01_ref[at, :] = mm3(i0_ref[at, :], work[:, :size]).astype(jnp.bfloat16)
+        c0j_ref[at, :] = mm3(i0_ref[at, :], work[:, size:]).astype(jnp.bfloat16)
+        return carry
+
+    lax.fori_loop(0, size // NB, couple, 0)
+    work[:, :size] = (mm(s1_ref[...], s1_ref[...], TN) * scale + jnp.where(eye, r1_ref[...], 0.0)
+                      - mm(c01_ref[...], c01_ref[...], TN))
     work[:, size:] = jnp.where(eye, 1.0, 0.0)
     invert(work, top, held)
     i1_ref[...] = work[:, size:]
 
 
 def third_kernel(
-    scale, rows, info, s0_ref, s1_ref, sj_ref, r0_ref, r1_ref, i0_ref, i1_ref, c01_ref, c0j_ref, w_ref, p_ref, d_ref
+    scale, rows, info, s0_ref, s1_ref, sj_ref, r0_ref, r1_ref, i0_ref, i1_ref, c01_ref, c0j_ref, w_ref, p_ref, d_ref,
+    c1j_ref
 ):
     size = s0_ref.shape[1]
+    depth = w_ref.shape[0]
+    times = depth // rows
+    strip = max(times, size // 2)
     eye = eye_mask(size)
     live = (info[3] > 1).astype(jnp.float32)
-    i0, i1, c01, c0j = i0_ref[...], i1_ref[...], c01_ref[...], c0j_ref[...]
-    r1 = r1_ref[...]
-    w = w_ref[...]
-    times = w.shape[0] // rows
-
-    def put(value, side):
-        for t in range(rows):
-            to = pl.multiple_of(lax.rem(info[6] - t + rows, rows) * times, times)
-            p_ref[pl.ds(to, times), side * size:(side + 1) * size] = value[t * times:(t + 1) * times].astype(jnp.bfloat16)
-
-    p0 = mm3(mm(w, s0_ref[...], TN) * scale, i0, NT)
-    put(p0, 0)
-    p1 = mm3(mm(w, s1_ref[...], TN) * scale - mm2(p0, c01), i1, NT)
-    put(p1, 1)
-    own = r1 * (info[3] == 1).astype(jnp.float32)
-    a1j = mm(s1_ref[...], sj_ref[...], TN) * scale + jnp.where(eye, own, 0.0) - mm(c01, c0j, TN)
-    c1j = mm3(i1, a1j).astype(jnp.bfloat16)
-    pn = mm(w, sj_ref[...], TN) * scale - mm2(p0, c0j) - mm2(p1, c1j)
-    put(pn * live, 2)
-    d00 = (i0 * r0_ref[...]).T
-    d10 = mm3(-mm2(d00, c01), i1, NT)
-    d11 = (i1 * r1).T
-    d_ref[:size, :size] = d00
-    d_ref[:size, size:2 * size] = d10
-    d_ref[:size, 2 * size:] = (mm2(d00, c0j) + mm2(d10, c1j)) * -live
+    own = r1_ref[...] * (info[3] == 1).astype(jnp.float32)
+    a1j = mm(s1_ref[...], sj_ref[...], TN) * scale + jnp.where(eye, own, 0.0) - mm(c01_ref[...], c0j_ref[...], TN)
+    c1j_ref[...] = mm3(i1_ref[...], a1j).astype(jnp.bfloat16)
+
+    def weights(b, carry):
+        w = w_ref[:, pl.ds(pl.multiple_of(b * strip, strip), strip)]
+        p0 = mm3(mm(w, s0_ref[...], TN) * scale, i0_ref[...], NT)
+        p1 = mm3(mm(w, s1_ref[...], TN) * scale - mm2(p0, c01_ref[...]), i1_ref[...], NT)
+        pn = (mm(w, sj_ref[...], TN) * scale - mm2(p0, c0j_ref[...]) - mm2(p1, c1j_ref[...])) * live
+        for t in range(strip // times):
+            place = lax.rem(info[6] - (b * (strip // times) + t) + rows, rows)
+            to = pl.ds(pl.multiple_of(place * times, times), times)
+            for side, value in enumerate((p0, p1, pn)):
+                p_ref[to, side * size:(side + 1) * size] = value[t * times:(t + 1) * times].astype(jnp.bfloat16)
+        return carry
+
+    lax.fori_loop(0, depth // strip, weights, 0)
+    d_ref[:size, :size] = (i0_ref[...] * r0_ref[...]).T
     d_ref[size:, :size] = jnp.zeros((size, size), jnp.float32)
-    d_ref[size:, size:2 * size] = d11
-    d_ref[size:, 2 * size:] = mm2(d11, c1j) * -live
+    d_ref[size:, size:2 * size] = (i1_ref[...] * r1_ref[...]).T
+
+    def ridges(b, carry):
+        at = pl.ds(pl.multiple_of(b * NB, NB), NB)
+        low = pl.ds(pl.multiple_of(size + b * NB, NB), NB)
+        d00 = d_ref[at, :size]
+        d10 = mm3(-mm2(d00, c01_ref[...]), i1_ref[...], NT)
+        d_ref[at, size:2 * size] = d10
+        d_ref[at, 2 * size:] = (mm2(d00, c0j_ref[...]) + mm2(d10, c1j_ref[...])) * -live
+        d_ref[low, 2 * size:] = mm2(d_ref[low, size:2 * size], c1j_ref[...]) * -live
+        return carry
+
+    lax.fori_loop(0, size // NB, ridges, 0)
 
 
 def chain_call(kernel, info, operands, specs, outs, scratch, flops, name):
@@ -393,12 +410,44 @@
     )(info, x)
 
 
-def final_body(chunk_base, info, own_ref, rest_ref, p_ref, d_ref, r_ref, *rest):
-    t_ref, f_ref = rest[-2:]
-    _, width = t_ref.shape
-    times = own_ref.shape[1]
-    acc = mm(own_ref[0], p_ref[:times, :], TN) + mm(rest_ref[0], p_ref[times:, :], TN)
-    kind = kind_of(info, chunk_base(pl.program_id(0), pl.program_id(1)))
+def final_body(chunk_base, units, per, start, info, *refs):
+    owns, others = refs[:units], refs[units:2 * units]
+    p_ref, d_ref, r_ref = refs[2 * units:2 * units + 3]
+    t_ref, f_ref, held, arrived = refs[-4:]
+    bm, width = t_ref.shape
+    times = owns[0].shape[0]
+    step = pl.program_id(0) * per + pl.program_id(1)
+    slot = step % 2
+
+    def copies(u, i, slot):
+        return (
+            pltpu.make_async_copy(
+                owns[u].at[:, pl.ds(pl.multiple_of(start + i * bm, bm), bm)], held.at[slot, pl.ds(0, times)],
+                arrived.at[slot, 0]),
+            pltpu.make_async_copy(
+                others[u].at[:, pl.ds(pl.multiple_of(i * bm, bm), bm)],
+                held.at[slot, pl.ds(times, held.shape[1] - times)], arrived.at[slot, 1]),
+        )
+
+    def fetch(n):
+        for u in range(units):
+            @pl.when(n // per == u)
+            def _():
+                for copy in copies(u, n % per, n % 2):
+                    copy.start()
+
+    @pl.when(step == 0)
+    def _():
+        fetch(step)
+
+    @pl.when(step + 1 < units * per)
+    def _():
+        fetch(step + 1)
+
+    for copy in copies(0, 0, slot):
+        copy.wait()
+    acc = mm(held[slot], p_ref[...], TN)
+    kind = kind_of(info, chunk_base(pl.program_id(0), pl.program_id(1), info))
 
     def put(first, second, last):
         f_ref[0] = first.astype(f_ref.dtype)
@@ -428,39 +477,41 @@
 
 
 def final_chunk(info, own, others, weights, d, ridge, prior, start, width):
-    cols, times, local = own.shape
+    units = len(others)
+    times, local = own[0].shape
+    rest, w = others[0].shape
     bm = width
-    w = others.shape[2]
     per = w // bm
-    rows = cols * local
-    rest = others.shape[1]
-
-    def base(c, i):
-        return c * (local // bm) + start // bm + i
-
-    in_specs = [
-        pl.BlockSpec((1, times, bm), lambda c, i, info: (c, 0, start // bm + i)),
-        pl.BlockSpec((1, rest, bm), lambda c, i, info: (c, 0, i)),
+    rows = units * local
+
+    def base(c, i, info):
+        far, bits = 0, units.bit_length() - 1
+        for b in range(bits):
+            far = far + (((c >> b) & 1) << (bits - 1 - b))
+        return (info[2] ^ far) * (local // bm) + start // bm + i
+
+    in_specs = [pl.BlockSpec(memory_space=pl.ANY)] * (2 * units) + [
         pl.BlockSpec(weights.shape, lambda c, i, info: (0, 0)),
-        pl.BlockSpec((bm, 3 * width), lambda c, i, info: (jnp.where(kind_of(info, base(c, i)) == 1, 1, 0), 0)),
+        pl.BlockSpec((bm, 3 * width), lambda c, i, info: (jnp.where(kind_of(info, base(c, i, info)) == 1, 1, 0), 0)),
         pl.BlockSpec((1, width), lambda c, i, info: (0, 0)),
     ]
-    operands = [info, own, others, weights, d, ridge]
+    operands = [info, *own, *others, weights, d, ridge]
     aliases = {}
     if prior is not None:
         in_specs += [pl.BlockSpec(memory_space=pl.ANY)] * 2
         aliases = {len(operands): 0, len(operands) + 1: 1}
         operands += list(prior)
     return pl.pallas_call(
-        functools.partial(final_body, base),
+        functools.partial(final_body, base, units, per, start),
         grid_spec=pltpu.PrefetchScalarGridSpec(
             num_scalar_prefetch=1,
-            grid=(cols, per),
+            grid=(units, per),
             in_specs=in_specs,
             out_specs=[
-                pl.BlockSpec((bm, width), lambda c, i, info: (base(c, i), 0)),
-                pl.BlockSpec((2, bm, width), lambda c, i, info: (0, base(c, i), 0)),
+                pl.BlockSpec((bm, width), lambda c, i, info: (base(c, i, info), 0)),
+                pl.BlockSpec((2, bm, width), lambda c, i, info: (0, base(c, i, info), 0)),
             ],
+            scratch_shapes=[pltpu.VMEM((2, times + rest, bm), jnp.bfloat16), pltpu.SemaphoreType.DMA((2, 2))],
         ),
         out_shape=[
             jax.ShapeDtypeStruct((rows, width), jnp.float32),
@@ -471,9 +522,21 @@
             vmem_limit_bytes=48 * 2**20, dimension_semantics=("arbitrary", "arbitrary")
         ),
         cost_estimate=pl.CostEstimate(
-            flops=2 * cols * w * (times + rest) * 3 * width, bytes_accessed=cols * w * 6 * 2**10, transcendentals=0),
+            flops=2 * units * w * (times + rest) * 3 * width, bytes_accessed=units * w * 6 * 2**10, transcendentals=0),
         name="final",
     )(*operands)
+
+
+def hop_gather(block, cols):
+    held = [block]
+    bit = cols // 2
+    while bit:
+        moved = []
+        for h in held:
+            moved.append(lax.ppermute(h, "col", [(i, i ^ bit) for i in range(cols)]))
+        held = held + moved
+        bit //= 2
+    return held
 
 
 def on_device(samples, whitening, ridge, slab_start, panels):
@@ -505,7 +568,7 @@
     sw, ridges, own, head, *pieces = gather_slab(
         part, jnp.broadcast_to(ridge, (SUB, width)), whitening, flat, starts, sizes, rows, cols, tms)
     ridges = ridges[:, 0].reshape(1, slab)
-    own = lax.all_gather(own, "col", axis=0)
+    own = hop_gather(own, cols)
     others = []
     for c in range(len(sizes)):
         block = pieces[c * (rows - 1):(c + 1) * (rows - 1)]
@@ -514,7 +577,7 @@
                 lax.ppermute(block[s - 1], "row", [(i, (i + s) % rows) for i in range(rows)])
                 for s in range(1, rows)
             ], axis=0)
-        others.append(lax.all_gather(head, "col", axis=0))
+        others.append(hop_gather(head, cols))
 
     q0, q1 = panels[0], panels[1]
     owner = (me_row == group) & (me_tm == tm_owner)
@@ -535,7 +598,7 @@
         functools.partial(third_kernel, scale, rows), info,
         [sw, sw, sw, ridges, ridges, i0, i1, c01, c0j, whitening], [0, 1, 2, 0, 1, None, None, None, None, None],
         [jax.ShapeDtypeStruct((depth, 3 * width), jnp.bfloat16), jax.ShapeDtypeStruct((2 * width, 3 * width), jnp.float32)],
-        [], 15 * 10**9, "third")
+        [pltpu.VMEM((width, width), jnp.bfloat16)], 15 * 10**9, "third")
     own_ridge = ridge.reshape(1, width) * (kind == 2).astype(jnp.float32)
 
     prior = None

time: 421 us -> 462 us (1.097); the launches traced: 413 us -> 461 us
  waiting for transfers between devices: 99.2 us -> 127 us
  local copies, waits for them, and re-layouts: 7.12 us -> 22.2 us
  between operations: 16.6 us -> 3.12 us
  Pallas kernels: 227 us -> 240 us
  starting transfers between devices: 57.9 us -> 68.5 us
  other arithmetic: 5.41 us -> 0.62 us
    ppermute x0 -> x18, waiting for transfers between devices: none -> 62 us  [hop_gather(): moved.append(lax.ppermute(h, 'col', [(i, i ^ bit) for i in range(cols)]))]
    ppermute x12, waiting for transfers between devices: 98.5 us -> 64.6 us  [on_device(): lax.ppermute(block[s - 1], 'row', [(i, (i + s) % rows) for i in range(row...]
    unnamed x30 -> x42, local copies, waits for them, and re-layouts: 3.82 us -> 13.4 us
    ppermute x0 -> x18, starting transfers between devices: none -> 8.71 us  [hop_gather(): moved.append(lax.ppermute(h, 'col', [(i, i ^ bit) for i in range(cols)]))]
    pallas_call x5, Pallas kernels: 88.2 us -> 95.4 us  [final_chunk(): pl.pallas_call(functools.partial(final_body, base, units, per, start), gr...]
    concatenate x0 -> x4, local copies, waits for them, and re-layouts: none -> 5.57 us  [on_device(): jnp.concatenate([lax.ppermute(block[s - 1], 'row', [(i, (i + s) % rows) f...]
    pallas_call x3, Pallas kernels: 77 us -> 82.5 us  [chain_call(): pl.pallas_call(kernel, grid_spec=pltpu.PrefetchScalarGridSpec(num_scalar_...]
    concatenate x4 -> x0, other arithmetic: 4.78 us -> none  [on_device(): jnp.concatenate([lax.ppermute(block[s - 1], 'row', [(i, (i + s) % rows) f...]
  transfers between devices with their start and end apart: 18 -> 30, of which waited for: 7 -> 8; matrix products, arithmetic and copies ran while one was open for 2% -> 4% of each run, Pallas kernels for 37% -> 36%
where the time goes in v4:
time: 462 us; the launch traced here: 461 us
  Pallas kernels  240 us (52%)
  waiting for transfers between devices  127 us (27%)
  starting transfers between devices  68.5 us (15%)
  local copies, waits for them, and re-layouts  22.2 us (5%)
    pallas_call x5, Pallas kernels, final_chunk(): pl.pallas_call(functools.partial(final_body, base, units, per, start), gr...  95.4 us
    pallas_call x3, Pallas kernels, chain_call(): pl.pallas_call(kernel, grid_spec=pltpu.PrefetchScalarGridSpec(num_scalar_...  82.5 us
    ppermute x12, waiting for transfers between devices, on_device(): lax.ppermute(block[s - 1], 'row', [(i, (i + s) % rows) for i in range(row...  64.6 us
    ppermute x18, waiting for transfers between devices, hop_gather(): moved.append(lax.ppermute(h, 'col', [(i, i ^ bit) for i in range(cols)]))  62 us
    ppermute x12, starting transfers between devices, on_device(): lax.ppermute(block[s - 1], 'row', [(i, (i + s) % rows) for i in range(row...  59.7 us
    pallas_call x1, Pallas kernels, gather_slab(): pl.pallas_call(functools.partial(gather_kernel, row_n, col_n, tm_n, start...  57.2 us
    unnamed x42, local copies, waits for them, and re-layouts  13.4 us
  transfers between devices with their start and end apart: 30, of which 8 were waited for; matrix products, arithmetic and copies ran while one was open for 4% of the time, Pallas kernels for 36%

profile of v4, /device:TPU:0, one launch (start us, length us, event | category | flops | bytes accessed | tf_op | source)
XLA Modules:
  0.0 460.8 jit_solution(16869513103148148088)
XLA Ops:
  1.4 0.6 pad_add_fusion.info
  2.0 4.8 %pick_blocks.1.part = bf16[256,2048]{1,0:T(8,128)(2,1)} custom-call(s32[9]{0:T(128)} %pad_add_fusion.info, bf16[256,4,4096]{2,1,0:T(4,128)(2,1)} %bitcast.18), custom_call_target="tpu_custom_call" | custom-call | bytes 8388608 | tf_op jit(solution)/shard_map/pick_blocks/pallas_call | solution.py:399
  6.8 0.6 broadcast_in_dim.3.ridge
  7.4 57.2 %gather_slab.1 = (bf16[1024,2048]{1,0:T(8,128)(2,1)}, f32[4,8,512]{2,1,0:T(8,128)}, bf16[256,4096]{1,0:T(8,128)(2,1)}, bf16[768,512]{1,0:T(8,128)(2,1)}, bf16[25...) custom-call(bf16[256,2048]{1,0:T(8,128)(2,1)} %pick_blocks.1.part, ...), custom_call_target="tpu_custom_call" | custom-call | flops 40000000000 | bytes 1048576 | tf_op jit(solution)/shard_map/gather_slab/pallas_call | solution.py:352
  64.6 1.8 collective-permute-start.3
  66.4 1.9 collective-permute-start.4
  68.2 0.7 collective-permute-start.5
  68.9 1.4 collective-permute-start.21
  70.2 1.1 collective-permute-start.22
  71.3 4.6 %collective-permute-done.3 = bf16[256,512]{1,0:T(8,128)(2,1)S(1)} collective-permute-done((bf16[256,512]{1,0:T(8,128)(2,1)}, bf16[256,512]{1,0:T(8,128)(2,1)S(1)}, u32[]{:S(2)}, u32[]{:S(2)}) %collective-permute-start.3) | collective-permute-done | bytes 262176 | tf_op jit(solution)/shard_map/ppermute | solution.py:577
  76.0 2.4 collective-permute-start.23
  78.3 8.9 %collective-permute-done.4 = bf16[256,512]{1,0:T(8,128)(2,1)S(1)} collective-permute-done((bf16[256,512]{1,0:T(8,128)(2,1)}, bf16[256,512]{1,0:T(8,128)(2,1)S(1)}, u32[]{:S(2)}, u32[]{:S(2)}) %collective-permute-start.4) | collective-permute-done | bytes 262176 | tf_op jit(solution)/shard_map/ppermute | solution.py:577
  87.2 3.2 collective-permute-start.15
  90.4 0.0 collective-permute-done.5
  90.4 0.7 copy-done.14
  91.1 23.7 %collective-permute-start.16 = (bf16[256,1024]{1,0:T(8,128)(2,1)}, bf16[256,1024]{1,0:T(8,128)(2,1)S(1)}, u32[]{:S(2)}, u32[]{:S(2)}) collective-permute-start(bf16[256,1024]{1,0:T(8,128)(2,1)} %get-tuple-element.46), channel_id=1, source_target_pairs={{0,16},{8,24},{16,0},{24,8},{1,17},{9,25},{17,1},{25,9},{2,18},{10... | collective-permute-start | bytes 1572872 | tf_op jit(solution)/shard_map/ppermute | solution.py:577
  114.9 1.4 slice.15
  116.3 0.6 fusion
  118.2 0.6 stack.23.info
  118.8 0.8 collective-permute-start.27
  119.6 28.7 %collective-permute-done.22 = bf16[256,1024]{1,0:T(8,128)(2,1)S(1)} collective-permute-done((bf16[256,1024]{1,0:T(8,128)(2,1)}, bf16[256,1024]{1,0:T(8,128)(2,1)S(1)}, u32[]{:S(2)}, u32[]{:S(2)}) %collective-permute-start.22) | collective-permute-done | bytes 524320 | tf_op jit(solution)/shard_map/ppermute | solution.py:577
  148.2 1.1 collective-permute-start.17
  149.3 10.7 %collective-permute-start.9 = (bf16[256,1024]{1,0:T(8,128)(2,1)}, bf16[256,1024]{1,0:T(8,128)(2,1)}, u32[]{:S(2)}, u32[]{:S(2)}) collective-permute-start(bf16[256,1024]{1,0:T(8,128)(2,1)} %get-tuple-element.42), channel_id=1, source_target_pairs={{0,8},{8,16},{16,24},{24,0},{1,9},{9,17},{17,25},{25,1},{2,10},{10... | collective-permute-start | bytes 1572872 | tf_op jit(solution)/shard_map/ppermute | solution.py:577
  160.0 0.0 collective-permute-done.15
  160.0 10.9 %collective-permute-start.10 = (bf16[256,1024]{1,0:T(8,128)(2,1)}, bf16[256,1024]{1,0:T(8,128)(2,1)}, u32[]{:S(2)}, u32[]{:S(2)}) collective-permute-start(bf16[256,1024]{1,0:T(8,128)(2,1)} %get-tuple-element.43), channel_id=1, source_target_pairs={{0,16},{8,24},{16,0},{24,8},{1,17},{9,25},{17,1},{25,9},{2,18},{10... | collective-permute-start | bytes 1572872 | tf_op jit(solution)/shard_map/ppermute | solution.py:577
  170.9 22.3 %collective-permute-done.16 = bf16[256,1024]{1,0:T(8,128)(2,1)S(1)} collective-permute-done((bf16[256,1024]{1,0:T(8,128)(2,1)}, bf16[256,1024]{1,0:T(8,128)(2,1)S(1)}, u32[]{:S(2)}, u32[]{:S(2)}) %collective-permute-start.16) | collective-permute-done | bytes 524320 | tf_op jit(solution)/shard_map/ppermute | solution.py:577
  193.2 1.1 collective-permute-start.11
  194.3 25.0 %shard_map.68.i0_ref = f32[512,512]{1,0:T(8,128)} custom-call(s32[7]{0:T(128)} %stack.23.info, bf16[1024,2048]{1,0:T(8,128)(2,1)} %get-tuple-element.35.s0_ref.s1_ref.sj_ref, f32[1,2048]{1,0:T(1,128)} %bitcast.20), custom_call_target="tpu_custom_call" | custom-call | flops 20000000000 | bytes 8388608 | tf_op jit(solution)/shard_map/pallas_call | solution.py:181
  219.3 2.0 constant_dynamic-update-slice_fusion.11
  221.3 1.9 constant_dynamic-update-slice_fusion.10
  223.2 1.9 constant_dynamic-update-slice_fusion.9.refs_4_
  225.1 1.2 collective-permute-start
  226.3 0.5 collective-permute-start.28
  226.8 0.8 collective-permute-start.24
  227.6 30.6 %shard_map.69 = (bf16[512,512]{1,0:T(8,128)(2,1)}, bf16[512,512]{1,0:T(8,128)(2,1)}, f32[512,512]{1,0:T(8,128)}) custom-call(s32[7]{0:T(128)} %stack.23.info, bf16[1024,2048]{1,0:T(8,128)(2,1)} %get-tuple-element.35.s0_ref.s1_ref.sj_ref, bf16[1024,2048]{1,0:T(8,128)(2,1)} %get-tuple-element.35.s0_ref.s1_ref.sj_ref, ...), custom_call_target="tpu_custom_call" | custom-call | flops 24000000000 | bytes 8388608 | tf_op jit(solution)/shard_map/pallas_call | solution.py:181
  258.3 0.8 constant_dynamic-update-slice_fusion.8
  259.1 1.9 constant_dynamic-update-slice_fusion.5
  261.0 0.8 constant_dynamic-update-slice_fusion.7
  261.8 0.8 constant_dynamic-update-slice_fusion.6.refs_4_
  262.7 1.9 constant_dynamic-update-slice_fusion.4
  264.6 9.1 %collective-permute-done.refs_1_ = bf16[256,4096]{1,0:T(8,128)(2,1)} collective-permute-done((bf16[256,4096]{1,0:T(8,128)(2,1)S(1)}, bf16[256,4096]{1,0:T(8,128)(2,1)}, u32[]{:S(2)}, u32[]{:S(2)}) %collective-permute-start) | collective-permute-done | bytes 2097184 | tf_op jit(solution)/shard_map/ppermute | solution.py:536
  273.7 0.0 collective-permute-start.2
  273.7 1.9 constant_dynamic-update-slice_fusion.3.refs_4_
  275.6 0.5 collective-permute-start.25
  276.1 1.2 collective-permute-start.18
  277.3 0.8 collective-permute-start.12
  278.1 29.3 %collective-permute-done.24.refs_5_ = bf16[768,1024]{1,0:T(8,128)(2,1)} collective-permute-done((bf16[768,1024]{1,0:T(8,128)(2,1)}, bf16[768,1024]{1,0:T(8,128)(2,1)}, u32[]{:S(2)}, u32[]{:S(2)}) %collective-permute-start.24) | collective-permute-done | bytes 1572896 | tf_op jit(solution)/shard_map/ppermute | solution.py:536
  307.4 26.9 %shard_map.70 = (bf16[1024,1536]{1,0:T(8,128)(2,1)}, f32[1024,1536]{1,0:T(8,128)}) custom-call(s32[7]{0:T(128)} %stack.23.info, bf16[1024,2048]{1,0:T(8,128)(2,1)} %get-tuple-element.35.s0_ref.s1_ref.sj_ref, bf16[1024,2048]{1,0:T(8,128)(2,1)} %get-tuple-element.35.s0_ref.s1_ref.sj_ref, bf16[1024,2048]{1,0:T(8,128)(2,1)} %get-tuple-element.35.s0_ref.s1_ref.sj_ref, ...), custom_call_target="tpu_custom_call" | custom-call | flops 15000000512 | bytes 8388608 | tf_op jit(solution)/shard_map/pallas_call | solution.py:181
  334.3 1.0 constant_dynamic-update-slice_fusion.1
  335.3 1.0 constant_dynamic-update-slice_fusion.refs_4_
  336.3 4.8 %collective-permute-done.18.refs_5_ = bf16[768,1024]{1,0:T(8,128)(2,1)} collective-permute-done((bf16[768,1024]{1,0:T(8,128)(2,1)}, bf16[768,1024]{1,0:T(8,128)(2,1)}, u32[]{:S(2)}, u32[]{:S(2)}) %collective-permute-start.18) | collective-permute-done | bytes 1572896 | tf_op jit(solution)/shard_map/ppermute | solution.py:536
  341.1 0.5 collective-permute-start.20
  341.6 13.1 %final.5 = (f32[16384,512]{1,0:T(8,128)}, bf16[2,16384,512]{2,1,0:T(8,128)(2,1)}) custom-call(s32[7]{0:T(128)S(1)} %copy-done.2, bf16[256,4096]{1,0:T(8,128)(2,1)S(1)} %copy-done, bf16[256,4096]{1,0:T(8,128)(2,1)} %collective-permute-done.refs_1_, bf16[256,4096]{1,0:T(8,128)(2,1)} %collective-permute-done.1.refs_2_, ...), custom_call_target="tpu_custom_call" | custom-call | flops 6442450944 | bytes 12582912 | tf_op jit(solution)/shard_map/final/pallas_call | solution.py:504
  354.8 1.3 collective-permute-start.6
  356.1 18.7 %collective-permute-done.12.refs_5_ = bf16[768,1024]{1,0:T(8,128)(2,1)} collective-permute-done((bf16[768,1024]{1,0:T(8,128)(2,1)}, bf16[768,1024]{1,0:T(8,128)(2,1)}, u32[]{:S(2)}, u32[]{:S(2)}) %collective-permute-start.12) | collective-permute-done | bytes 1572896 | tf_op jit(solution)/shard_map/ppermute | solution.py:536
  374.8 0.5 collective-permute-start.14
  375.3 22.8 %final.6 = (f32[16384,512]{1,0:T(8,128)}, bf16[2,16384,512]{2,1,0:T(8,128)(2,1)}) custom-call(s32[7]{0:T(128)S(1)} %copy-done.2, bf16[256,4096]{1,0:T(8,128)(2,1)} %get-tuple-element.31.refs_0_, bf16[256,4096]{1,0:T(8,128)(2,1)} %collective-permute-done.refs_1_, ...), custom_call_target="tpu_custom_call", output_to_operand_aliasing={{0}: (12, {}), {1}: (13, {})} | custom-call | flops 12884901888 | bytes 25165824 | tf_op jit(solution)/shard_map/final/pallas_call | solution.py:504
  398.1 0.1 collective-permute-start.7
  398.2 0.5 collective-permute-start.8
  398.7 1.2 copy-done.4
  399.9 23.2 %final.7 = (f32[16384,512]{1,0:T(8,128)}, bf16[2,16384,512]{2,1,0:T(8,128)(2,1)}) custom-call(s32[7]{0:T(128)S(1)} %copy-done.2, bf16[256,4096]{1,0:T(8,128)(2,1)} %get-tuple-element.31.refs_0_, bf16[256,4096]{1,0:T(8,128)(2,1)} %collective-permute-done.refs_1_, ...), custom_call_target="tpu_custom_call", output_to_operand_aliasing={{0}: (12, {}), {1}: (13, {})} | custom-call | flops 12884901888 | bytes 25165824 | tf_op jit(solution)/shard_map/final/pallas_call | solution.py:504
  423.1 1.2 copy-done.5
  424.3 23.0 %final.8 = (f32[16384,512]{1,0:T(8,128)}, bf16[2,16384,512]{2,1,0:T(8,128)(2,1)}) custom-call(s32[7]{0:T(128)S(1)} %copy-done.2, bf16[256,4096]{1,0:T(8,128)(2,1)} %get-tuple-element.31.refs_0_, bf16[256,4096]{1,0:T(8,128)(2,1)} %collective-permute-done.refs_1_, ...), custom_call_target="tpu_custom_call", output_to_operand_aliasing={{0}: (12, {}), {1}: (13, {})} | custom-call | flops 12884901888 | bytes 25165824 | tf_op jit(solution)/shard_map/final/pallas_call | solution.py:504
  447.3 13.3 %final.9 = (f32[16384,512]{1,0:T(8,128)}, bf16[2,16384,512]{2,1,0:T(8,128)(2,1)}) custom-call(s32[7]{0:T(128)S(1)} %copy-done.2, bf16[256,4096]{1,0:T(8,128)(2,1)S(1)} %copy-done.1, bf16[256,4096]{1,0:T(8,128)(2,1)} %collective-permute-done.refs_1_, ...), custom_call_target="tpu_custom_call", output_to_operand_aliasing={{0}: (12, {}), {1}: (13, {})} | custom-call | flops 6442450944 | bytes 12582912 | tf_op jit(solution)/shard_map/final/pallas_call | solution.py:504
  (60 shorter events, 0.2 us)
Async XLA Ops:
  2.0 4.8 %copy-start.15 = (f32[512]{0:T(512)S(1)}, f32[512]{0:T(512)}, u32[]{:S(2)}) copy-start(f32[512]{0:T(512)} %param.7) | copy-start | bytes 6148
  7.4 108.9 %copy-start.16 = (s32[4]{0:T(128)S(1)}, s32[4]{0:T(128)}, u32[]{:S(2)}) copy-start(s32[4]{0:T(128)} %param.9) | copy-start | bytes 52
  64.6 11.4 %collective-permute-start.3 = (bf16[256,512]{1,0:T(8,128)(2,1)}, bf16[256,512]{1,0:T(8,128)(2,1)S(1)}, u32[]{:S(2)}, u32[]{:S(2)}) collective-permute-start(bf16[256,512]{1,0:T(8,128)(2,1)} %get-tuple-element.32), channel_id=1, source_target_pairs={{0,8},{8,16},{16,24},{24,0},{1,9},{9,17},{17,25},{25,1},{2,10},{10... | collective-permute-start | bytes 786440 | tf_op jit(solution)/shard_map/ppermute | solution.py:577
  66.4 20.9 %collective-permute-start.4 = (bf16[256,512]{1,0:T(8,128)(2,1)}, bf16[256,512]{1,0:T(8,128)(2,1)S(1)}, u32[]{:S(2)}, u32[]{:S(2)}) collective-permute-start(bf16[256,512]{1,0:T(8,128)(2,1)} %get-tuple-element.33), channel_id=1, source_target_pairs={{0,16},{8,24},{16,0},{24,8},{1,17},{9,25},{17,1},{25,9},{2,18},{10... | collective-permute-start | bytes 786440 | tf_op jit(solution)/shard_map/ppermute | solution.py:577
  68.2 22.2 %collective-permute-start.5 = (bf16[256,512]{1,0:T(8,128)(2,1)}, bf16[256,512]{1,0:T(8,128)(2,1)S(1)}, u32[]{:S(2)}, u32[]{:S(2)}) collective-permute-start(bf16[256,512]{1,0:T(8,128)(2,1)} %get-tuple-element.34), channel_id=1, source_target_pairs={{0,24},{8,0},{16,8},{24,16},{1,25},{9,1},{17,9},{25,17},{2,26},{10... | collective-permute-start | bytes 786440 | tf_op jit(solution)/shard_map/ppermute | solution.py:577
  68.9 49.9 %collective-permute-start.21 = (bf16[256,1024]{1,0:T(8,128)(2,1)}, bf16[256,1024]{1,0:T(8,128)(2,1)S(1)}, u32[]{:S(2)}, u32[]{:S(2)}) collective-permute-start(bf16[256,1024]{1,0:T(8,128)(2,1)} %get-tuple-element.48), channel_id=1, source_target_pairs={{0,8},{8,16},{16,24},{24,0},{1,9},{9,17},{17,25},{25,1},{2,10},{10... | collective-permute-start | bytes 1572872 | tf_op jit(solution)/shard_map/ppermute | solution.py:577
  70.2 78.0 %collective-permute-start.22 = (bf16[256,1024]{1,0:T(8,128)(2,1)}, bf16[256,1024]{1,0:T(8,128)(2,1)S(1)}, u32[]{:S(2)}, u32[]{:S(2)}) collective-permute-start(bf16[256,1024]{1,0:T(8,128)(2,1)} %get-tuple-element.49), channel_id=1, source_target_pairs={{0,16},{8,24},{16,0},{24,8},{1,17},{9,25},{17,1},{25,9},{2,18},{10... | collective-permute-start | bytes 1572872 | tf_op jit(solution)/shard_map/ppermute | solution.py:577
  75.9 14.5 %copy-start.11 = (bf16[256,512]{1,0:T(8,128)(2,1)}, bf16[256,512]{1,0:T(8,128)(2,1)S(1)}, u32[]{:S(2)}) copy-start(bf16[256,512]{1,0:T(8,128)(2,1)S(1)} %collective-permute-done.3) | copy-start | bytes 786436
  76.0 73.4 %collective-permute-start.23 = (bf16[256,1024]{1,0:T(8,128)(2,1)}, bf16[256,1024]{1,0:T(8,128)(2,1)S(1)}, u32[]{:S(2)}, u32[]{:S(2)}) collective-permute-start(bf16[256,1024]{1,0:T(8,128)(2,1)} %get-tuple-element.50), channel_id=1, source_target_pairs={{0,24},{8,0},{16,8},{24,16},{1,25},{9,1},{17,9},{25,17},{2,26},{10... | collective-permute-start | bytes 1572872 | tf_op jit(solution)/shard_map/ppermute | solution.py:577
  87.2 3.2 copy-start.13
  87.2 72.8 %collective-permute-start.15 = (bf16[256,1024]{1,0:T(8,128)(2,1)}, bf16[256,1024]{1,0:T(8,128)(2,1)S(1)}, u32[]{:S(2)}, u32[]{:S(2)}) collective-permute-start(bf16[256,1024]{1,0:T(8,128)(2,1)} %get-tuple-element.45), channel_id=1, source_target_pairs={{0,8},{8,16},{16,24},{24,0},{1,9},{9,17},{17,25},{25,1},{2,10},{10... | collective-permute-start | bytes 1572872 | tf_op jit(solution)/shard_map/ppermute | solution.py:577
  90.4 0.7 copy-start.14
  91.1 102.1 %collective-permute-start.16 = (bf16[256,1024]{1,0:T(8,128)(2,1)}, bf16[256,1024]{1,0:T(8,128)(2,1)S(1)}, u32[]{:S(2)}, u32[]{:S(2)}) collective-permute-start(bf16[256,1024]{1,0:T(8,128)(2,1)} %get-tuple-element.46), channel_id=1, source_target_pairs={{0,16},{8,24},{16,0},{24,8},{1,17},{9,25},{17,1},{25,9},{2,18},{10... | collective-permute-start | bytes 1572872 | tf_op jit(solution)/shard_map/ppermute | solution.py:577
  118.8 75.5 %copy-start.8 = (bf16[256,1024]{1,0:T(8,128)(2,1)}, bf16[256,1024]{1,0:T(8,128)(2,1)S(1)}, u32[]{:S(2)}) copy-start(bf16[256,1024]{1,0:T(8,128)(2,1)S(1)} %collective-permute-done.21) | copy-start | bytes 1572868
  118.8 108.8 %collective-permute-start.27 = (bf16[768,512]{1,0:T(8,128)(2,1)}, bf16[768,512]{1,0:T(8,128)(2,1)}, u32[]{:S(2)}, u32[]{:S(2)}) collective-permute-start(bf16[768,512]{1,0:T(8,128)(2,1)} %get-tuple-element.51.refs_4_), channel_id=1, source_target_pairs={{0,4},{2,6},{4,0},{6,2},{1,5},{3,7},{5,1},{7,3},{8,12},{10,14},{12... | collective-permute-start | bytes 2359304 | tf_op jit(solution)/shard_map/ppermute | solution.py:536
  148.2 46.1 %copy-start.9 = (bf16[256,1024]{1,0:T(8,128)(2,1)}, bf16[256,1024]{1,0:T(8,128)(2,1)S(1)}, u32[]{:S(2)}) copy-start(bf16[256,1024]{1,0:T(8,128)(2,1)S(1)} %collective-permute-done.22) | copy-start | bytes 1572868
  148.2 76.9 %collective-permute-start.17 = (bf16[256,1024]{1,0:T(8,128)(2,1)}, bf16[256,1024]{1,0:T(8,128)(2,1)S(1)}, u32[]{:S(2)}, u32[]{:S(2)}) collective-permute-start(bf16[256,1024]{1,0:T(8,128)(2,1)} %get-tuple-element.47), channel_id=1, source_target_pairs={{0,24},{8,0},{16,8},{24,16},{1,25},{9,1},{17,9},{25,17},{2,26},{10... | collective-permute-start | bytes 1572872 | tf_op jit(solution)/shard_map/ppermute | solution.py:577
  149.3 45.0 %copy-start.10 = (bf16[256,1024]{1,0:T(8,128)(2,1)}, bf16[256,1024]{1,0:T(8,128)(2,1)S(1)}, u32[]{:S(2)}) copy-start(bf16[256,1024]{1,0:T(8,128)(2,1)S(1)} %collective-permute-done.23) | copy-start | bytes 1572868
  149.3 77.0 %collective-permute-start.9 = (bf16[256,1024]{1,0:T(8,128)(2,1)}, bf16[256,1024]{1,0:T(8,128)(2,1)}, u32[]{:S(2)}, u32[]{:S(2)}) collective-permute-start(bf16[256,1024]{1,0:T(8,128)(2,1)} %get-tuple-element.42), channel_id=1, source_target_pairs={{0,8},{8,16},{16,24},{24,0},{1,9},{9,17},{17,25},{25,1},{2,10},{10... | collective-permute-start | bytes 1572872 | tf_op jit(solution)/shard_map/ppermute | solution.py:577
  160.0 66.3 %collective-permute-start.10 = (bf16[256,1024]{1,0:T(8,128)(2,1)}, bf16[256,1024]{1,0:T(8,128)(2,1)}, u32[]{:S(2)}, u32[]{:S(2)}) collective-permute-start(bf16[256,1024]{1,0:T(8,128)(2,1)} %get-tuple-element.43), channel_id=1, source_target_pairs={{0,16},{8,24},{16,0},{24,8},{1,17},{9,25},{17,1},{25,9},{2,18},{10... | collective-permute-start | bytes 1572872 | tf_op jit(solution)/shard_map/ppermute | solution.py:577
  193.2 1.1 copy-start.6
  193.2 33.6 %collective-permute-start.11 = (bf16[256,1024]{1,0:T(8,128)(2,1)}, bf16[256,1024]{1,0:T(8,128)(2,1)}, u32[]{:S(2)}, u32[]{:S(2)}) collective-permute-start(bf16[256,1024]{1,0:T(8,128)(2,1)} %get-tuple-element.44), channel_id=1, source_target_pairs={{0,24},{8,0},{16,8},{24,16},{1,25},{9,1},{17,9},{25,17},{2,26},{10... | collective-permute-start | bytes 1572872 | tf_op jit(solution)/shard_map/ppermute | solution.py:577
  219.3 5.8 %copy-start = (bf16[256,4096]{1,0:T(8,128)(2,1)S(1)}, bf16[256,4096]{1,0:T(8,128)(2,1)}, u32[]{:S(2)}) copy-start(bf16[256,4096]{1,0:T(8,128)(2,1)} %get-tuple-element.31.refs_0_) | copy-start | bytes 6291460
  219.3 7.0 %copy-start.3 = (bf16[768,512]{1,0:T(8,128)(2,1)S(1)}, bf16[768,512]{1,0:T(8,128)(2,1)}, u32[]{:S(2)}) copy-start(bf16[768,512]{1,0:T(8,128)(2,1)} %get-tuple-element.51.refs_4_) | copy-start | bytes 2359300
  225.1 48.6 %collective-permute-start = (bf16[256,4096]{1,0:T(8,128)(2,1)S(1)}, bf16[256,4096]{1,0:T(8,128)(2,1)}, u32[]{:S(2)}, u32[]{:S(2)}) collective-permute-start(bf16[256,4096]{1,0:T(8,128)(2,1)S(1)} %copy-done), channel_id=1, source_target_pairs={{0,4},{2,6},{4,0},{6,2},{1,5},{3,7},{5,1},{7,3},{8,12},{10,14},{12... | collective-permute-start | bytes 6291464 | tf_op jit(solution)/shard_map/ppermute | solution.py:536
  226.3 51.0 %collective-permute-start.1 = (bf16[256,4096]{1,0:T(8,128)(2,1)S(1)}, bf16[256,4096]{1,0:T(8,128)(2,1)}, u32[]{:S(2)}, u32[]{:S(2)}) collective-permute-start(bf16[256,4096]{1,0:T(8,128)(2,1)S(1)} %copy-done), channel_id=1, source_target_pairs={{0,2},{2,0},{4,6},{6,4},{1,3},{3,1},{5,7},{7,5},{8,10},{10,8},{12,... | collective-permute-start | bytes 6291464 | tf_op jit(solution)/shard_map/ppermute | solution.py:536
  226.3 49.2 %collective-permute-start.28 = (bf16[768,512]{1,0:T(8,128)(2,1)S(1)}, bf16[768,512]{1,0:T(8,128)(2,1)}, u32[]{:S(2)}, u32[]{:S(2)}) collective-permute-start(bf16[768,512]{1,0:T(8,128)(2,1)S(1)} %copy-done.3), channel_id=1, source_target_pairs={{0,2},{2,0},{4,6},{6,4},{1,3},{3,1},{5,7},{7,5},{8,10},{10,8},{12,... | collective-permute-start | bytes 2359304 | tf_op jit(solution)/shard_map/ppermute | solution.py:536
  226.8 80.6 %collective-permute-start.24 = (bf16[768,1024]{1,0:T(8,128)(2,1)}, bf16[768,1024]{1,0:T(8,128)(2,1)}, u32[]{:S(2)}, u32[]{:S(2)}) collective-permute-start(bf16[768,1024]{1,0:T(8,128)(2,1)} %constant_dynamic-update-slice_fusion.9.refs_4_), channel_id=1, source_target_pairs={{0,4},{2,6},{4,0},{6,2},{1,5},{3,7},{5,1},{7,3},{8,12},{10,14},{12... | collective-permute-start | bytes 4718600 | tf_op jit(solution)/shard_map/ppermute | solution.py:536
  227.6 48.4 %collective-permute-start.29 = (bf16[768,512]{1,0:T(8,128)(2,1)}, bf16[768,512]{1,0:T(8,128)(2,1)}, u32[]{:S(2)}, u32[]{:S(2)}) collective-permute-start(bf16[768,512]{1,0:T(8,128)(2,1)} %collective-permute-done.27.refs_5_), channel_id=1, source_target_pairs={{0,2},{2,0},{4,6},{6,4},{1,3},{3,1},{5,7},{7,5},{8,10},{10,8},{12,... | collective-permute-start | bytes 2359304 | tf_op jit(solution)/shard_map/ppermute | solution.py:536
  258.3 2.7 copy-start.7
  273.7 67.4 %collective-permute-start.2 = (bf16[256,4096]{1,0:T(8,128)(2,1)}, bf16[256,4096]{1,0:T(8,128)(2,1)}, u32[]{:S(2)}, u32[]{:S(2)}) collective-permute-start(bf16[256,4096]{1,0:T(8,128)(2,1)} %collective-permute-done.refs_1_), channel_id=1, source_target_pairs={{0,2},{2,0},{4,6},{6,4},{1,3},{3,1},{5,7},{7,5},{8,10},{10,8},{12,... | collective-permute-start | bytes 6291464 | tf_op jit(solution)/shard_map/ppermute | solution.py:536
  275.6 79.2 %collective-permute-start.25 = (bf16[768,1024]{1,0:T(8,128)(2,1)}, bf16[768,1024]{1,0:T(8,128)(2,1)}, u32[]{:S(2)}, u32[]{:S(2)}) collective-permute-start(bf16[768,1024]{1,0:T(8,128)(2,1)} %constant_dynamic-update-slice_fusion.9.refs_4_), channel_id=1, source_target_pairs={{0,2},{2,0},{4,6},{6,4},{1,3},{3,1},{5,7},{7,5},{8,10},{10,8},{12,... | collective-permute-start | bytes 4718600 | tf_op jit(solution)/shard_map/ppermute | solution.py:536
  276.1 65.0 %collective-permute-start.18 = (bf16[768,1024]{1,0:T(8,128)(2,1)}, bf16[768,1024]{1,0:T(8,128)(2,1)}, u32[]{:S(2)}, u32[]{:S(2)}) collective-permute-start(bf16[768,1024]{1,0:T(8,128)(2,1)} %constant_dynamic-update-slice_fusion.6.refs_4_), channel_id=1, source_target_pairs={{0,4},{2,6},{4,0},{6,2},{1,5},{3,7},{5,1},{7,3},{8,12},{10,14},{12... | collective-permute-start | bytes 4718600 | tf_op jit(solution)/shard_map/ppermute | solution.py:536
  277.3 97.5 %collective-permute-start.12 = (bf16[768,1024]{1,0:T(8,128)(2,1)}, bf16[768,1024]{1,0:T(8,128)(2,1)}, u32[]{:S(2)}, u32[]{:S(2)}) collective-permute-start(bf16[768,1024]{1,0:T(8,128)(2,1)} %constant_dynamic-update-slice_fusion.3.refs_4_), channel_id=1, source_target_pairs={{0,4},{2,6},{4,0},{6,2},{1,5},{3,7},{5,1},{7,3},{8,12},{10,14},{12... | collective-permute-start | bytes 4718600 | tf_op jit(solution)/shard_map/ppermute | solution.py:536
  307.4 67.4 %collective-permute-start.26 = (bf16[768,1024]{1,0:T(8,128)(2,1)}, bf16[768,1024]{1,0:T(8,128)(2,1)}, u32[]{:S(2)}, u32[]{:S(2)}) collective-permute-start(bf16[768,1024]{1,0:T(8,128)(2,1)} %collective-permute-done.24.refs_5_), channel_id=1, source_target_pairs={{0,2},{2,0},{4,6},{6,4},{1,3},{3,1},{5,7},{7,5},{8,10},{10,8},{12,... | collective-permute-start | bytes 4718600 | tf_op jit(solution)/shard_map/ppermute | solution.py:536
  307.4 26.9 %copy-start.12 = (bf16[256,512]{1,0:T(8,128)(2,1)S(1)}, bf16[256,512]{1,0:T(8,128)(2,1)}, u32[]{:S(2)}) copy-start(bf16[256,512]{1,0:T(8,128)(2,1)} %copy-done.11) | copy-start | bytes 786436
  334.3 7.3 %copy-start.2 = (s32[7]{0:T(128)S(1)}, s32[7]{0:T(128)}, u32[]{:S(2)}) copy-start(s32[7]{0:T(128)} %stack.23.info) | copy-start | bytes 88
  341.1 57.1 %collective-permute-start.19 = (bf16[768,1024]{1,0:T(8,128)(2,1)}, bf16[768,1024]{1,0:T(8,128)(2,1)S(1)}, u32[]{:S(2)}, u32[]{:S(2)}) collective-permute-start(bf16[768,1024]{1,0:T(8,128)(2,1)} %constant_dynamic-update-slice_fusion.6.refs_4_), channel_id=1, source_target_pairs={{0,2},{2,0},{4,6},{6,4},{1,3},{3,1},{5,7},{7,5},{8,10},{10,8},{12,... | collective-permute-start | bytes 4718600 | tf_op jit(solution)/shard_map/ppermute | solution.py:536
  341.1 57.6 %collective-permute-start.20 = (bf16[768,1024]{1,0:T(8,128)(2,1)}, bf16[768,1024]{1,0:T(8,128)(2,1)S(1)}, u32[]{:S(2)}, u32[]{:S(2)}) collective-permute-start(bf16[768,1024]{1,0:T(8,128)(2,1)} %collective-permute-done.18.refs_5_), channel_id=1, source_target_pairs={{0,2},{2,0},{4,6},{6,4},{1,3},{3,1},{5,7},{7,5},{8,10},{10,8},{12,... | collective-permute-start | bytes 4718600 | tf_op jit(solution)/shard_map/ppermute | solution.py:536
  354.8 43.3 %collective-permute-start.6 = (bf16[768,512]{1,0:T(8,128)(2,1)S(1)}, bf16[768,512]{1,0:T(8,128)(2,1)S(1)}, u32[]{:S(2)}, u32[]{:S(2)}) collective-permute-start(bf16[768,512]{1,0:T(8,128)(2,1)S(1)} %constant_dynamic-update-slice_fusion.refs_4_), channel_id=1, source_target_pairs={{0,4},{2,6},{4,0},{6,2},{1,5},{3,7},{5,1},{7,3},{8,12},{10,14},{12... | collective-permute-start | bytes 2359304 | tf_op jit(solution)/shard_map/ppermute | solution.py:536
  374.8 48.3 %collective-permute-start.13 = (bf16[768,1024]{1,0:T(8,128)(2,1)}, bf16[768,1024]{1,0:T(8,128)(2,1)S(1)}, u32[]{:S(2)}, u32[]{:S(2)}) collective-permute-start(bf16[768,1024]{1,0:T(8,128)(2,1)} %constant_dynamic-update-slice_fusion.3.refs_4_), channel_id=1, source_target_pairs={{0,2},{2,0},{4,6},{6,4},{1,3},{3,1},{5,7},{7,5},{8,10},{10,8},{12,... | collective-permute-start | bytes 4718600 | tf_op jit(solution)/shard_map/ppermute | solution.py:536
  374.8 48.3 %collective-permute-start.14 = (bf16[768,1024]{1,0:T(8,128)(2,1)}, bf16[768,1024]{1,0:T(8,128)(2,1)S(1)}, u32[]{:S(2)}, u32[]{:S(2)}) collective-permute-start(bf16[768,1024]{1,0:T(8,128)(2,1)} %collective-permute-done.12.refs_5_), channel_id=1, source_target_pairs={{0,2},{2,0},{4,6},{6,4},{1,3},{3,1},{5,7},{7,5},{8,10},{10,8},{12,... | collective-permute-start | bytes 4718600 | tf_op jit(solution)/shard_map/ppermute | solution.py:536
  398.1 49.1 %collective-permute-start.7 = (bf16[768,512]{1,0:T(8,128)(2,1)S(1)}, bf16[768,512]{1,0:T(8,128)(2,1)S(1)}, u32[]{:S(2)}, u32[]{:S(2)}) collective-permute-start(bf16[768,512]{1,0:T(8,128)(2,1)S(1)} %constant_dynamic-update-slice_fusion.refs_4_), channel_id=1, source_target_pairs={{0,2},{2,0},{4,6},{6,4},{1,3},{3,1},{5,7},{7,5},{8,10},{10,8},{12,... | collective-permute-start | bytes 2359304 | tf_op jit(solution)/shard_map/ppermute | solution.py:536
  398.2 49.0 %collective-permute-start.8 = (bf16[768,512]{1,0:T(8,128)(2,1)S(1)}, bf16[768,512]{1,0:T(8,128)(2,1)S(1)}, u32[]{:S(2)}, u32[]{:S(2)}) collective-permute-start(bf16[768,512]{1,0:T(8,128)(2,1)S(1)} %collective-permute-done.6.refs_5_), channel_id=1, source_target_pairs={{0,2},{2,0},{4,6},{6,4},{1,3},{3,1},{5,7},{7,5},{8,10},{10,8},{12,... | collective-permute-start | bytes 2359304 | tf_op jit(solution)/shard_map/ppermute | solution.py:536
  398.7 1.2 copy-start.4
  423.1 1.2 copy-start.5
  424.3 23.0 %copy-start.1 = (bf16[256,4096]{1,0:T(8,128)(2,1)S(1)}, bf16[256,4096]{1,0:T(8,128)(2,1)}, u32[]{:S(2)}) copy-start(bf16[256,4096]{1,0:T(8,128)(2,1)} %get-tuple-element.31.refs_0_) | copy-start | bytes 6291460

commit v5 on v4

--- a/solution.py
+++ b/solution.py
@@ -278,12 +278,13 @@
             @pl.when(row == k)
             def _():
                 def strip(t, carry):
-                    at = pl.ds(pl.multiple_of(t * 16, 16), 16)
+                    at = pl.ds(pl.multiple_of(lax.rem(t, times // 16) * 16, 16), 16)
+                    cut = pl.ds(pl.multiple_of(t // (times // 16) * sizes[0], sizes[0]), sizes[0])
                     for s in range(row_n):
-                        sorted_[c % 2, s, at, :sizes[c]] = source[c % 2, at, (k + s) % row_n, :sizes[c]]
+                        sorted_[c % 2, s, at, cut] = source[c % 2, at, (k + s) % row_n, cut]
                     return carry
 
-                lax.fori_loop(0, times // 16, strip, 0)
+                lax.fori_loop(0, times // 16 * (sizes[c] // sizes[0]), strip, 0)
         for s in range(row_n):
             out_copy(c, s).start()
 
@@ -324,6 +325,7 @@
         start(head_copy(s))
     split(3)
     split(4)
+    split(5)
     for h in range(2):
         for e in range(1, len(steps)):
             far_copy(h, e).wait_recv()
@@ -560,7 +562,7 @@
 
     flat = samples.reshape(times, groups, local)
     eighth = local // 8
-    sizes = [eighth, 2 * eighth, 2 * eighth, 2 * eighth, eighth] if eighth >= width else [width] * (local // width)
+    sizes = [eighth * n for n in (1, 2, 2, 1, 1, 1)] if eighth >= width else [width] * (local // width)
     starts = [sum(sizes[:c]) for c in range(len(sizes))]
     at = offset + jnp.arange(cols) * width
     have = (me_tm == tm_owner) & (me_col == at // local)

time: 462 us -> 416 us (0.900)
  the two profiles are of different devices: /device:TPU:0 before, /device:TPU:21 now
where the time goes in v5:
time: 416 us; the launch traced here: 410 us
  Pallas kernels  242 us (58%)
  waiting for transfers between devices  109 us (26%)
  starting transfers between devices  38.9 us (9%)
  local copies, waits for them, and re-layouts  15.8 us (4%)
    pallas_call x6, Pallas kernels, final_chunk(): pl.pallas_call(functools.partial(final_body, base, units, per, start), gr...  99.3 us
    pallas_call x3, Pallas kernels, chain_call(): pl.pallas_call(kernel, grid_spec=pltpu.PrefetchScalarGridSpec(num_scalar_...  82.5 us
    ppermute x15, waiting for transfers between devices, on_device(): lax.ppermute(block[s - 1], 'row', [(i, (i + s) % rows) for i in range(row...  75.3 us
    pallas_call x1, Pallas kernels, gather_slab(): pl.pallas_call(functools.partial(gather_kernel, row_n, col_n, tm_n, start...  55.9 us
    ppermute x21, waiting for transfers between devices, hop_gather(): moved.append(lax.ppermute(h, 'col', [(i, i ^ bit) for i in range(cols)]))  33.4 us
    ppermute x21, starting transfers between devices, hop_gather(): moved.append(lax.ppermute(h, 'col', [(i, i ^ bit) for i in range(cols)]))  22.4 us
    ppermute x15, starting transfers between devices, on_device(): lax.ppermute(block[s - 1], 'row', [(i, (i + s) % rows) for i in range(row...  16.4 us
    unnamed x52, local copies, waits for them, and re-layouts  9.73 us
  transfers between devices with their start and end apart: 36, of which 12 were waited for; matrix products, arithmetic and copies ran while one was open for 4% of the time, Pallas kernels for 41%

profile of v5, /device:TPU:21, one launch (start us, length us, event | category | flops | bytes accessed | tf_op | source)
XLA Modules:
  0.0 409.8 jit_solution(7736049684206558346)
XLA Ops:
  1.4 0.6 pad_add_fusion.info
  2.0 4.8 %pick_blocks.1.part = bf16[256,2048]{1,0:T(8,128)(2,1)} custom-call(s32[9]{0:T(128)} %pad_add_fusion.info, bf16[256,4,4096]{2,1,0:T(4,128)(2,1)} %bitcast.19), custom_call_target="tpu_custom_call" | custom-call | bytes 8388608 | tf_op jit(solution)/shard_map/pick_blocks/pallas_call | solution.py:401
  6.8 0.6 broadcast_in_dim.3.ridge
  7.4 55.9 %gather_slab.1 = (bf16[1024,2048]{1,0:T(8,128)(2,1)}, f32[4,8,512]{2,1,0:T(8,128)}, bf16[256,4096]{1,0:T(8,128)(2,1)}, bf16[768,512]{1,0:T(8,128)(2,1)}, bf16[25...) custom-call(bf16[256,2048]{1,0:T(8,128)(2,1)} %pick_blocks.1.part, ...), custom_call_target="tpu_custom_call" | custom-call | flops 40000000000 | bytes 1048576 | tf_op jit(solution)/shard_map/gather_slab/pallas_call | solution.py:354
  63.3 1.8 collective-permute-start.15
  65.1 1.7 collective-permute-start.17
  66.9 2.1 collective-permute-start.10
  69.0 2.5 collective-permute-done.15
  71.5 0.5 collective-permute-start.11
  72.0 1.4 slice.15
  73.4 0.6 fusion
  75.3 0.7 stack.23.info
  76.0 6.5 %collective-permute-done.16 = bf16[256,512]{1,0:T(8,128)(2,1)S(1)} collective-permute-done((bf16[256,512]{1,0:T(8,128)(2,1)}, bf16[256,512]{1,0:T(8,128)(2,1)S(1)}, u32[]{:S(2)}, u32[]{:S(2)}) %collective-permute-start.16) | collective-permute-done | bytes 262176 | tf_op jit(solution)/shard_map/ppermute | solution.py:579
  82.5 6.9 %collective-permute-start.27 = (bf16[256,1024]{1,0:T(8,128)(2,1)}, bf16[256,1024]{1,0:T(8,128)(2,1)S(1)}, u32[]{:S(2)}, u32[]{:S(2)}) collective-permute-start(bf16[256,1024]{1,0:T(8,128)(2,1)} %get-tuple-element.56), channel_id=1, source_target_pairs={{0,8},{8,16},{16,24},{24,0},{1,9},{9,17},{17,25},{25,1},{2,10},{10... | collective-permute-start | bytes 1572872 | tf_op jit(solution)/shard_map/ppermute | solution.py:579
  89.4 9.9 %collective-permute-done.17 = bf16[256,512]{1,0:T(8,128)(2,1)S(1)} collective-permute-done((bf16[256,512]{1,0:T(8,128)(2,1)}, bf16[256,512]{1,0:T(8,128)(2,1)S(1)}, u32[]{:S(2)}, u32[]{:S(2)}) %collective-permute-start.17) | collective-permute-done | bytes 262176 | tf_op jit(solution)/shard_map/ppermute | solution.py:579
  99.4 5.8 %collective-permute-done.9 = bf16[256,512]{1,0:T(8,128)(2,1)S(1)} collective-permute-done((bf16[256,512]{1,0:T(8,128)(2,1)}, bf16[256,512]{1,0:T(8,128)(2,1)S(1)}, u32[]{:S(2)}, u32[]{:S(2)}) %collective-permute-start.9) | collective-permute-done | bytes 262176 | tf_op jit(solution)/shard_map/ppermute | solution.py:579
  105.2 22.3 %collective-permute-done.10 = bf16[256,512]{1,0:T(8,128)(2,1)S(1)} collective-permute-done((bf16[256,512]{1,0:T(8,128)(2,1)}, bf16[256,512]{1,0:T(8,128)(2,1)S(1)}, u32[]{:S(2)}, u32[]{:S(2)}) %collective-permute-start.10) | collective-permute-done | bytes 262176 | tf_op jit(solution)/shard_map/ppermute | solution.py:579
  127.5 6.0 %collective-permute-done.11 = bf16[256,512]{1,0:T(8,128)(2,1)S(1)} collective-permute-done((bf16[256,512]{1,0:T(8,128)(2,1)}, bf16[256,512]{1,0:T(8,128)(2,1)S(1)}, u32[]{:S(2)}, u32[]{:S(2)}) %collective-permute-start.11) | collective-permute-done | bytes 262176 | tf_op jit(solution)/shard_map/ppermute | solution.py:579
  133.5 0.4 collective-permute-start.3
  134.0 0.2 copy-done.10
  134.2 25.2 %shard_map.68.i0_ref = f32[512,512]{1,0:T(8,128)} custom-call(s32[7]{0:T(128)} %stack.23.info, bf16[1024,2048]{1,0:T(8,128)(2,1)} %get-tuple-element.40.s0_ref.s1_ref.sj_ref, f32[1,2048]{1,0:T(1,128)} %bitcast.21), custom_call_target="tpu_custom_call" | custom-call | flops 20000000000 | bytes 8388608 | tf_op jit(solution)/shard_map/pallas_call | solution.py:181
  159.4 13.4 %collective-permute-done.3 = bf16[256,512]{1,0:T(8,128)(2,1)} collective-permute-done((bf16[256,512]{1,0:T(8,128)(2,1)}, bf16[256,512]{1,0:T(8,128)(2,1)}, u32[]{:S(2)}, u32[]{:S(2)}) %collective-permute-start.3) | collective-permute-done | bytes 262176 | tf_op jit(solution)/shard_map/ppermute | solution.py:579
  172.8 0.6 collective-permute-start.33
  173.4 1.2 collective-permute-start.34
  174.6 0.9 collective-permute-start
  175.6 30.6 %shard_map.69 = (bf16[512,512]{1,0:T(8,128)(2,1)}, bf16[512,512]{1,0:T(8,128)(2,1)}, f32[512,512]{1,0:T(8,128)}) custom-call(s32[7]{0:T(128)} %stack.23.info, bf16[1024,2048]{1,0:T(8,128)(2,1)} %get-tuple-element.40.s0_ref.s1_ref.sj_ref, bf16[1024,2048]{1,0:T(8,128)(2,1)} %get-tuple-element.40.s0_ref.s1_ref.sj_ref, ...), custom_call_target="tpu_custom_call" | custom-call | flops 24000000000 | bytes 8388608 | tf_op jit(solution)/shard_map/pallas_call | solution.py:181
  206.2 0.8 constant_dynamic-update-slice_fusion.14
  207.0 1.9 constant_dynamic-update-slice_fusion.11
  208.9 1.9 constant_dynamic-update-slice_fusion.13
  210.8 2.5 collective-permute-start.4
  213.2 0.4 collective-permute-start.5
  213.6 0.8 constant_dynamic-update-slice_fusion.12.refs_4_
  214.4 1.9 constant_dynamic-update-slice_fusion.10
  216.3 1.9 constant_dynamic-update-slice_fusion.9.refs_4_
  218.2 5.7 %collective-permute-done.4 = bf16[256,512]{1,0:T(8,128)(2,1)S(1)} collective-permute-done((bf16[256,512]{1,0:T(8,128)(2,1)S(1)}, bf16[256,512]{1,0:T(8,128)(2,1)S(1)}, u32[]{:S(2)}, u32[]{:S(2)}) %collective-permute-start.4) | collective-permute-done | bytes 262176 | tf_op jit(solution)/shard_map/ppermute | solution.py:579
  223.9 2.5 collective-permute-start.1
  226.5 3.1 collective-permute-done.5
  229.6 0.6 collective-permute-start.30
  230.2 0.9 collective-permute-start.24
  231.0 2.0 collective-permute-start.35
  233.1 3.0 collective-permute-done.refs_1_
  236.0 3.1 collective-permute-start.2
  239.2 26.7 %shard_map.70 = (bf16[1024,1536]{1,0:T(8,128)(2,1)}, f32[1024,1536]{1,0:T(8,128)}) custom-call(s32[7]{0:T(128)} %stack.23.info, bf16[1024,2048]{1,0:T(8,128)(2,1)} %get-tuple-element.40.s0_ref.s1_ref.sj_ref, bf16[1024,2048]{1,0:T(8,128)(2,1)} %get-tuple-element.40.s0_ref.s1_ref.sj_ref, bf16[1024,2048]{1,0:T(8,128)(2,1)} %get-tuple-element.40.s0_ref.s1_ref.sj_ref, ...), custom_call_target="tpu_custom_call" | custom-call | flops 15000000512 | bytes 8388608 | tf_op jit(solution)/shard_map/pallas_call | solution.py:181
  266.0 3.7 collective-permute-done.30.refs_5_
  269.7 3.1 collective-permute-start.32
  272.9 1.0 constant_dynamic-update-slice_fusion.8
  273.9 1.0 constant_dynamic-update-slice_fusion.5
  274.9 1.0 constant_dynamic-update-slice_fusion.2
  276.2 0.7 collective-permute-start.18
  276.8 26.6 %collective-permute-done.24.refs_5_ = bf16[768,1024]{1,0:T(8,128)(2,1)} collective-permute-done((bf16[768,1024]{1,0:T(8,128)(2,1)}, bf16[768,1024]{1,0:T(8,128)(2,1)}, u32[]{:S(2)}, u32[]{:S(2)}) %collective-permute-start.24) | collective-permute-done | bytes 1572896 | tf_op jit(solution)/shard_map/ppermute | solution.py:538
  303.5 3.1 collective-permute-start.25
  306.6 13.1 %final.6 = (f32[16384,512]{1,0:T(8,128)}, bf16[2,16384,512]{2,1,0:T(8,128)(2,1)}) custom-call(s32[7]{0:T(128)S(1)} %copy-done.2, bf16[256,4096]{1,0:T(8,128)(2,1)S(1)} %copy-done, bf16[256,4096]{1,0:T(8,128)(2,1)} %collective-permute-done.refs_1_, bf16[256,4096]{1,0:T(8,128)(2,1)} %collective-permute-done.1.refs_2_, ...), custom_call_target="tpu_custom_call" | custom-call | flops 6442450944 | bytes 12582912 | tf_op jit(solution)/shard_map/final/pallas_call | solution.py:506
  319.8 0.6 collective-permute-start.19
  320.3 0.6 collective-permute-start.12
  320.9 22.9 %final.7 = (f32[16384,512]{1,0:T(8,128)}, bf16[2,16384,512]{2,1,0:T(8,128)(2,1)}) custom-call(s32[7]{0:T(128)S(1)} %copy-done.2, bf16[256,4096]{1,0:T(8,128)(2,1)} %get-tuple-element.36.refs_0_, bf16[256,4096]{1,0:T(8,128)(2,1)} %collective-permute-done.refs_1_, ...), custom_call_target="tpu_custom_call", output_to_operand_aliasing={{0}: (12, {}), {1}: (13, {})} | custom-call | flops 12884901888 | bytes 25165824 | tf_op jit(solution)/shard_map/final/pallas_call | solution.py:506
  343.9 0.4 collective-permute-start.13
  344.3 0.9 collective-permute-start.6
  345.2 0.4 collective-permute-start.20
  345.7 23.0 %final.8 = (f32[16384,512]{1,0:T(8,128)}, bf16[2,16384,512]{2,1,0:T(8,128)(2,1)}) custom-call(s32[7]{0:T(128)S(1)} %copy-done.2, bf16[256,4096]{1,0:T(8,128)(2,1)} %get-tuple-element.36.refs_0_, bf16[256,4096]{1,0:T(8,128)(2,1)} %collective-permute-done.refs_1_, ...), custom_call_target="tpu_custom_call", output_to_operand_aliasing={{0}: (12, {}), {1}: (13, {})} | custom-call | flops 12884901888 | bytes 25165824 | tf_op jit(solution)/shard_map/final/pallas_call | solution.py:506
  368.7 0.5 collective-permute-start.7
  369.2 0.1 collective-permute-start.8
  369.3 13.5 %final.9 = (f32[16384,512]{1,0:T(8,128)}, bf16[2,16384,512]{2,1,0:T(8,128)(2,1)}) custom-call(s32[7]{0:T(128)S(1)} %copy-done.2, bf16[256,4096]{1,0:T(8,128)(2,1)S(1)} %copy-done.1, bf16[256,4096]{1,0:T(8,128)(2,1)} %collective-permute-done.refs_1_, ...), custom_call_target="tpu_custom_call", output_to_operand_aliasing={{0}: (12, {}), {1}: (13, {})} | custom-call | flops 6442450944 | bytes 12582912 | tf_op jit(solution)/shard_map/final/pallas_call | solution.py:506
  382.8 13.3 %final.10 = (f32[16384,512]{1,0:T(8,128)}, bf16[2,16384,512]{2,1,0:T(8,128)(2,1)}) custom-call(s32[7]{0:T(128)S(1)} %copy-done.2, bf16[256,4096]{1,0:T(8,128)(2,1)S(1)} %copy-done.1, bf16[256,4096]{1,0:T(8,128)(2,1)} %collective-permute-done.refs_1_, ...), custom_call_target="tpu_custom_call", output_to_operand_aliasing={{0}: (12, {}), {1}: (13, {})} | custom-call | flops 6442450944 | bytes 12582912 | tf_op jit(solution)/shard_map/final/pallas_call | solution.py:506
  396.2 13.3 %final.11 = (f32[16384,512]{1,0:T(8,128)}, bf16[2,16384,512]{2,1,0:T(8,128)(2,1)}) custom-call(s32[7]{0:T(128)S(1)} %copy-done.2, bf16[256,4096]{1,0:T(8,128)(2,1)S(1)} %copy-done.1, bf16[256,4096]{1,0:T(8,128)(2,1)} %collective-permute-done.refs_1_, ...), custom_call_target="tpu_custom_call", output_to_operand_aliasing={{0}: (12, {}), {1}: (13, {})} | custom-call | flops 6442450944 | bytes 12582912 | tf_op jit(solution)/shard_map/final/pallas_call | solution.py:506
  (84 shorter events, 0.5 us)
Async XLA Ops:
  2.0 4.8 %copy-start.17 = (f32[512]{0:T(512)S(1)}, f32[512]{0:T(512)}, u32[]{:S(2)}) copy-start(f32[512]{0:T(512)} %param.7) | copy-start | bytes 6148
  7.4 66.0 %copy-start.18 = (s32[4]{0:T(128)S(1)}, s32[4]{0:T(128)}, u32[]{:S(2)}) copy-start(s32[4]{0:T(128)} %param.9) | copy-start | bytes 52
  63.3 8.2 %collective-permute-start.15 = (bf16[256,512]{1,0:T(8,128)(2,1)}, bf16[256,512]{1,0:T(8,128)(2,1)}, u32[]{:S(2)}, u32[]{:S(2)}) collective-permute-start(bf16[256,512]{1,0:T(8,128)(2,1)} %get-tuple-element.50), channel_id=1, source_target_pairs={{0,8},{8,16},{16,24},{24,0},{1,9},{9,17},{17,25},{25,1},{2,10},{10... | collective-permute-start | bytes 786440 | tf_op jit(solution)/shard_map/ppermute | solution.py:579
  65.1 17.4 %collective-permute-start.16 = (bf16[256,512]{1,0:T(8,128)(2,1)}, bf16[256,512]{1,0:T(8,128)(2,1)S(1)}, u32[]{:S(2)}, u32[]{:S(2)}) collective-permute-start(bf16[256,512]{1,0:T(8,128)(2,1)} %get-tuple-element.51), channel_id=1, source_target_pairs={{0,16},{8,24},{16,0},{24,8},{1,17},{9,25},{17,1},{25,9},{2,18},{10... | collective-permute-start | bytes 786440 | tf_op jit(solution)/shard_map/ppermute | solution.py:579
  65.1 34.2 %collective-permute-start.17 = (bf16[256,512]{1,0:T(8,128)(2,1)}, bf16[256,512]{1,0:T(8,128)(2,1)S(1)}, u32[]{:S(2)}, u32[]{:S(2)}) collective-permute-start(bf16[256,512]{1,0:T(8,128)(2,1)} %get-tuple-element.52), channel_id=1, source_target_pairs={{0,24},{8,0},{16,8},{24,16},{1,25},{9,1},{17,9},{25,17},{2,26},{10... | collective-permute-start | bytes 786440 | tf_op jit(solution)/shard_map/ppermute | solution.py:579
  66.9 38.3 %collective-permute-start.9 = (bf16[256,512]{1,0:T(8,128)(2,1)}, bf16[256,512]{1,0:T(8,128)(2,1)S(1)}, u32[]{:S(2)}, u32[]{:S(2)}) collective-permute-start(bf16[256,512]{1,0:T(8,128)(2,1)} %get-tuple-element.47), channel_id=1, source_target_pairs={{0,8},{8,16},{16,24},{24,0},{1,9},{9,17},{17,25},{25,1},{2,10},{10... | collective-permute-start | bytes 786440 | tf_op jit(solution)/shard_map/ppermute | solution.py:579
  66.9 60.6 %collective-permute-start.10 = (bf16[256,512]{1,0:T(8,128)(2,1)}, bf16[256,512]{1,0:T(8,128)(2,1)S(1)}, u32[]{:S(2)}, u32[]{:S(2)}) collective-permute-start(bf16[256,512]{1,0:T(8,128)(2,1)} %get-tuple-element.48), channel_id=1, source_target_pairs={{0,16},{8,24},{16,0},{24,8},{1,17},{9,25},{17,1},{25,9},{2,18},{10... | collective-permute-start | bytes 786440 | tf_op jit(solution)/shard_map/ppermute | solution.py:579
  71.5 62.0 %collective-permute-start.11 = (bf16[256,512]{1,0:T(8,128)(2,1)}, bf16[256,512]{1,0:T(8,128)(2,1)S(1)}, u32[]{:S(2)}, u32[]{:S(2)}) collective-permute-start(bf16[256,512]{1,0:T(8,128)(2,1)} %get-tuple-element.49), channel_id=1, source_target_pairs={{0,24},{8,0},{16,8},{24,16},{1,25},{9,1},{17,9},{25,17},{2,26},{10... | collective-permute-start | bytes 786440 | tf_op jit(solution)/shard_map/ppermute | solution.py:579
  82.5 51.5 %copy-start.4 = (bf16[256,512]{1,0:T(8,128)(2,1)}, bf16[256,512]{1,0:T(8,128)(2,1)S(1)}, u32[]{:S(2)}) copy-start(bf16[256,512]{1,0:T(8,128)(2,1)S(1)} %collective-permute-done.16) | copy-start | bytes 786436
  82.5 90.9 %collective-permute-start.27 = (bf16[256,1024]{1,0:T(8,128)(2,1)}, bf16[256,1024]{1,0:T(8,128)(2,1)S(1)}, u32[]{:S(2)}, u32[]{:S(2)}) collective-permute-start(bf16[256,1024]{1,0:T(8,128)(2,1)} %get-tuple-element.56), channel_id=1, source_target_pairs={{0,8},{8,16},{16,24},{24,0},{1,9},{9,17},{17,25},{25,1},{2,10},{10... | collective-permute-start | bytes 1572872 | tf_op jit(solution)/shard_map/ppermute | solution.py:579
  99.4 34.6 %copy-start.6 = (bf16[256,512]{1,0:T(8,128)(2,1)}, bf16[256,512]{1,0:T(8,128)(2,1)S(1)}, u32[]{:S(2)}) copy-start(bf16[256,512]{1,0:T(8,128)(2,1)S(1)} %collective-permute-done.17) | copy-start | bytes 786436
  99.4 75.2 %collective-permute-start.28 = (bf16[256,1024]{1,0:T(8,128)(2,1)}, bf16[256,1024]{1,0:T(8,128)(2,1)}, u32[]{:S(2)}, u32[]{:S(2)}) collective-permute-start(bf16[256,1024]{1,0:T(8,128)(2,1)} %get-tuple-element.57), channel_id=1, source_target_pairs={{0,16},{8,24},{16,0},{24,8},{1,17},{9,25},{17,1},{25,9},{2,18},{10... | collective-permute-start | bytes 1572872 | tf_op jit(solution)/shard_map/ppermute | solution.py:579
  105.2 28.8 %copy-start.12 = (bf16[256,512]{1,0:T(8,128)(2,1)}, bf16[256,512]{1,0:T(8,128)(2,1)S(1)}, u32[]{:S(2)}) copy-start(bf16[256,512]{1,0:T(8,128)(2,1)S(1)} %collective-permute-done.9) | copy-start | bytes 786436
  105.2 70.3 %collective-permute-start.29 = (bf16[256,1024]{1,0:T(8,128)(2,1)}, bf16[256,1024]{1,0:T(8,128)(2,1)S(1)}, u32[]{:S(2)}, u32[]{:S(2)}) collective-permute-start(bf16[256,1024]{1,0:T(8,128)(2,1)} %get-tuple-element.58), channel_id=1, source_target_pairs={{0,24},{8,0},{16,8},{24,16},{1,25},{9,1},{17,9},{25,17},{2,26},{10... | collective-permute-start | bytes 1572872 | tf_op jit(solution)/shard_map/ppermute | solution.py:579
  127.5 6.5 %copy-start.8 = (bf16[256,512]{1,0:T(8,128)(2,1)}, bf16[256,512]{1,0:T(8,128)(2,1)S(1)}, u32[]{:S(2)}) copy-start(bf16[256,512]{1,0:T(8,128)(2,1)S(1)} %collective-permute-done.10) | copy-start | bytes 786436
  127.5 48.0 %collective-permute-start.21 = (bf16[256,1024]{1,0:T(8,128)(2,1)}, bf16[256,1024]{1,0:T(8,128)(2,1)}, u32[]{:S(2)}, u32[]{:S(2)}) collective-permute-start(bf16[256,1024]{1,0:T(8,128)(2,1)} %get-tuple-element.53), channel_id=1, source_target_pairs={{0,8},{8,16},{16,24},{24,0},{1,9},{9,17},{17,25},{25,1},{2,10},{10... | collective-permute-start | bytes 1572872 | tf_op jit(solution)/shard_map/ppermute | solution.py:579
  133.5 0.7 copy-start.10
  133.5 39.3 %collective-permute-start.3 = (bf16[256,512]{1,0:T(8,128)(2,1)}, bf16[256,512]{1,0:T(8,128)(2,1)}, u32[]{:S(2)}, u32[]{:S(2)}) collective-permute-start(bf16[256,512]{1,0:T(8,128)(2,1)} %get-tuple-element.37), channel_id=1, source_target_pairs={{0,8},{8,16},{16,24},{24,0},{1,9},{9,17},{17,25},{25,1},{2,10},{10... | collective-permute-start | bytes 786440 | tf_op jit(solution)/shard_map/ppermute | solution.py:579
  134.2 38.6 %copy-start.3 = (bf16[768,512]{1,0:T(8,128)(2,1)S(1)}, bf16[768,512]{1,0:T(8,128)(2,1)}, u32[]{:S(2)}) copy-start(bf16[768,512]{1,0:T(8,128)(2,1)} %get-tuple-element.59.refs_4_) | copy-start | bytes 2359300
  134.2 40.4 %copy-start = (bf16[256,4096]{1,0:T(8,128)(2,1)S(1)}, bf16[256,4096]{1,0:T(8,128)(2,1)}, u32[]{:S(2)}) copy-start(bf16[256,4096]{1,0:T(8,128)(2,1)} %get-tuple-element.36.refs_0_) | copy-start | bytes 6291460
  172.8 57.3 %collective-permute-start.33 = (bf16[768,512]{1,0:T(8,128)(2,1)S(1)}, bf16[768,512]{1,0:T(8,128)(2,1)}, u32[]{:S(2)}, u32[]{:S(2)}) collective-permute-start(bf16[768,512]{1,0:T(8,128)(2,1)S(1)} %copy-done.3), channel_id=1, source_target_pairs={{0,4},{2,6},{4,0},{6,2},{1,5},{3,7},{5,1},{7,3},{8,12},{10,14},{12... | collective-permute-start | bytes 2359304 | tf_op jit(solution)/shard_map/ppermute | solution.py:538
  173.4 57.6 %collective-permute-start.34 = (bf16[768,512]{1,0:T(8,128)(2,1)S(1)}, bf16[768,512]{1,0:T(8,128)(2,1)}, u32[]{:S(2)}, u32[]{:S(2)}) collective-permute-start(bf16[768,512]{1,0:T(8,128)(2,1)S(1)} %copy-done.3), channel_id=1, source_target_pairs={{0,2},{2,0},{4,6},{6,4},{1,3},{3,1},{5,7},{7,5},{8,10},{10,8},{12,... | collective-permute-start | bytes 2359304 | tf_op jit(solution)/shard_map/ppermute | solution.py:538
  174.6 61.4 %collective-permute-start = (bf16[256,4096]{1,0:T(8,128)(2,1)S(1)}, bf16[256,4096]{1,0:T(8,128)(2,1)}, u32[]{:S(2)}, u32[]{:S(2)}) collective-permute-start(bf16[256,4096]{1,0:T(8,128)(2,1)S(1)} %copy-done), channel_id=1, source_target_pairs={{0,4},{2,6},{4,0},{6,2},{1,5},{3,7},{5,1},{7,3},{8,12},{10,14},{12... | collective-permute-start | bytes 6291464 | tf_op jit(solution)/shard_map/ppermute | solution.py:538
  175.5 35.3 %collective-permute-start.22 = (bf16[256,1024]{1,0:T(8,128)(2,1)}, bf16[256,1024]{1,0:T(8,128)(2,1)}, u32[]{:S(2)}, u32[]{:S(2)}) collective-permute-start(bf16[256,1024]{1,0:T(8,128)(2,1)} %get-tuple-element.54), channel_id=1, source_target_pairs={{0,16},{8,24},{16,0},{24,8},{1,17},{9,25},{17,1},{25,9},{2,18},{10... | collective-permute-start | bytes 1572872 | tf_op jit(solution)/shard_map/ppermute | solution.py:579
  175.5 37.7 %collective-permute-start.23 = (bf16[256,1024]{1,0:T(8,128)(2,1)}, bf16[256,1024]{1,0:T(8,128)(2,1)}, u32[]{:S(2)}, u32[]{:S(2)}) collective-permute-start(bf16[256,1024]{1,0:T(8,128)(2,1)} %get-tuple-element.55), channel_id=1, source_target_pairs={{0,24},{8,0},{16,8},{24,16},{1,25},{9,1},{17,9},{25,17},{2,26},{10... | collective-permute-start | bytes 1572872 | tf_op jit(solution)/shard_map/ppermute | solution.py:579
  206.2 4.6 %copy-start.20 = (bf16[256,512]{1,0:T(8,128)(2,1)S(1)}, bf16[256,512]{1,0:T(8,128)(2,1)}, u32[]{:S(2)}) copy-start(bf16[256,512]{1,0:T(8,128)(2,1)} %get-tuple-element.38) | copy-start | bytes 786436
  206.2 7.0 %copy-start.19 = (bf16[256,512]{1,0:T(8,128)(2,1)S(1)}, bf16[256,512]{1,0:T(8,128)(2,1)}, u32[]{:S(2)}) copy-start(bf16[256,512]{1,0:T(8,128)(2,1)} %get-tuple-element.39) | copy-start | bytes 786436
  210.8 13.2 %collective-permute-start.4 = (bf16[256,512]{1,0:T(8,128)(2,1)S(1)}, bf16[256,512]{1,0:T(8,128)(2,1)S(1)}, u32[]{:S(2)}, u32[]{:S(2)}) collective-permute-start(bf16[256,512]{1,0:T(8,128)(2,1)S(1)} %copy-done.20), channel_id=1, source_target_pairs={{0,16},{8,24},{16,0},{24,8},{1,17},{9,25},{17,1},{25,9},{2,18},{10... | collective-permute-start | bytes 786440 | tf_op jit(solution)/shard_map/ppermute | solution.py:579
  213.2 16.3 %collective-permute-start.5 = (bf16[256,512]{1,0:T(8,128)(2,1)S(1)}, bf16[256,512]{1,0:T(8,128)(2,1)S(1)}, u32[]{:S(2)}, u32[]{:S(2)}) collective-permute-start(bf16[256,512]{1,0:T(8,128)(2,1)S(1)} %copy-done.19), channel_id=1, source_target_pairs={{0,24},{8,0},{16,8},{24,16},{1,25},{9,1},{17,9},{25,17},{2,26},{10... | collective-permute-start | bytes 786440 | tf_op jit(solution)/shard_map/ppermute | solution.py:579
  223.9 12.1 %copy-start.13 = (bf16[256,512]{1,0:T(8,128)(2,1)}, bf16[256,512]{1,0:T(8,128)(2,1)S(1)}, u32[]{:S(2)}) copy-start(bf16[256,512]{1,0:T(8,128)(2,1)S(1)} %collective-permute-done.4) | copy-start | bytes 786436
  223.9 52.2 %collective-permute-start.1 = (bf16[256,4096]{1,0:T(8,128)(2,1)S(1)}, bf16[256,4096]{1,0:T(8,128)(2,1)}, u32[]{:S(2)}, u32[]{:S(2)}) collective-permute-start(bf16[256,4096]{1,0:T(8,128)(2,1)S(1)} %copy-done), channel_id=1, source_target_pairs={{0,2},{2,0},{4,6},{6,4},{1,3},{3,1},{5,7},{7,5},{8,10},{10,8},{12,... | collective-permute-start | bytes 6291464 | tf_op jit(solution)/shard_map/ppermute | solution.py:538
  229.6 9.6 %copy-start.15 = (bf16[256,512]{1,0:T(8,128)(2,1)}, bf16[256,512]{1,0:T(8,128)(2,1)S(1)}, u32[]{:S(2)}) copy-start(bf16[256,512]{1,0:T(8,128)(2,1)S(1)} %collective-permute-done.5) | copy-start | bytes 786436
  229.6 40.2 %collective-permute-start.30 = (bf16[768,1024]{1,0:T(8,128)(2,1)}, bf16[768,1024]{1,0:T(8,128)(2,1)}, u32[]{:S(2)}, u32[]{:S(2)}) collective-permute-start(bf16[768,1024]{1,0:T(8,128)(2,1)} %constant_dynamic-update-slice_fusion.12.refs_4_), channel_id=1, source_target_pairs={{0,4},{2,6},{4,0},{6,2},{1,5},{3,7},{5,1},{7,3},{8,12},{10,14},{12... | collective-permute-start | bytes 4718600 | tf_op jit(solution)/shard_map/ppermute | solution.py:538
  230.2 73.3 %collective-permute-start.24 = (bf16[768,1024]{1,0:T(8,128)(2,1)}, bf16[768,1024]{1,0:T(8,128)(2,1)}, u32[]{:S(2)}, u32[]{:S(2)}) collective-permute-start(bf16[768,1024]{1,0:T(8,128)(2,1)} %constant_dynamic-update-slice_fusion.9.refs_4_), channel_id=1, source_target_pairs={{0,4},{2,6},{4,0},{6,2},{1,5},{3,7},{5,1},{7,3},{8,12},{10,14},{12... | collective-permute-start | bytes 4718600 | tf_op jit(solution)/shard_map/ppermute | solution.py:538
  231.0 34.9 %collective-permute-start.35 = (bf16[768,512]{1,0:T(8,128)(2,1)}, bf16[768,512]{1,0:T(8,128)(2,1)}, u32[]{:S(2)}, u32[]{:S(2)}) collective-permute-start(bf16[768,512]{1,0:T(8,128)(2,1)} %collective-permute-done.33.refs_5_), channel_id=1, source_target_pairs={{0,2},{2,0},{4,6},{6,4},{1,3},{3,1},{5,7},{7,5},{8,10},{10,8},{12,... | collective-permute-start | bytes 2359304 | tf_op jit(solution)/shard_map/ppermute | solution.py:538
  236.0 70.6 %collective-permute-start.2 = (bf16[256,4096]{1,0:T(8,128)(2,1)}, bf16[256,4096]{1,0:T(8,128)(2,1)}, u32[]{:S(2)}, u32[]{:S(2)}) collective-permute-start(bf16[256,4096]{1,0:T(8,128)(2,1)} %collective-permute-done.refs_1_), channel_id=1, source_target_pairs={{0,2},{2,0},{4,6},{6,4},{1,3},{3,1},{5,7},{7,5},{8,10},{10,8},{12,... | collective-permute-start | bytes 6291464 | tf_op jit(solution)/shard_map/ppermute | solution.py:538
  265.9 10.0 %copy-start.5 = (bf16[256,512]{1,0:T(8,128)(2,1)S(1)}, bf16[256,512]{1,0:T(8,128)(2,1)}, u32[]{:S(2)}) copy-start(bf16[256,512]{1,0:T(8,128)(2,1)} %copy-done.4) | copy-start | bytes 786436
  265.9 10.0 %copy-start.7 = (bf16[256,512]{1,0:T(8,128)(2,1)S(1)}, bf16[256,512]{1,0:T(8,128)(2,1)}, u32[]{:S(2)}) copy-start(bf16[256,512]{1,0:T(8,128)(2,1)} %copy-done.6) | copy-start | bytes 786436
  265.9 10.1 %copy-start.9 = (bf16[256,512]{1,0:T(8,128)(2,1)S(1)}, bf16[256,512]{1,0:T(8,128)(2,1)}, u32[]{:S(2)}) copy-start(bf16[256,512]{1,0:T(8,128)(2,1)} %copy-done.8) | copy-start | bytes 786436
  265.9 10.1 %copy-start.11 = (bf16[256,512]{1,0:T(8,128)(2,1)S(1)}, bf16[256,512]{1,0:T(8,128)(2,1)}, u32[]{:S(2)}) copy-start(bf16[256,512]{1,0:T(8,128)(2,1)} %copy-done.10) | copy-start | bytes 786436
  266.0 53.8 %collective-permute-start.31 = (bf16[768,1024]{1,0:T(8,128)(2,1)}, bf16[768,1024]{1,0:T(8,128)(2,1)S(1)}, u32[]{:S(2)}, u32[]{:S(2)}) collective-permute-start(bf16[768,1024]{1,0:T(8,128)(2,1)} %constant_dynamic-update-slice_fusion.12.refs_4_), channel_id=1, source_target_pairs={{0,2},{2,0},{4,6},{6,4},{1,3},{3,1},{5,7},{7,5},{8,10},{10,8},{12,... | collective-permute-start | bytes 4718600 | tf_op jit(solution)/shard_map/ppermute | solution.py:538
  269.7 50.6 %collective-permute-start.32 = (bf16[768,1024]{1,0:T(8,128)(2,1)}, bf16[768,1024]{1,0:T(8,128)(2,1)}, u32[]{:S(2)}, u32[]{:S(2)}) collective-permute-start(bf16[768,1024]{1,0:T(8,128)(2,1)} %collective-permute-done.30.refs_5_), channel_id=1, source_target_pairs={{0,2},{2,0},{4,6},{6,4},{1,3},{3,1},{5,7},{7,5},{8,10},{10,8},{12,... | collective-permute-start | bytes 4718600 | tf_op jit(solution)/shard_map/ppermute | solution.py:538
  273.9 2.2 copy-start.14
  274.9 1.2 copy-start.16
  275.9 30.7 %copy-start.2 = (s32[7]{0:T(128)S(1)}, s32[7]{0:T(128)}, u32[]{:S(2)}) copy-start(s32[7]{0:T(128)} %stack.23.info) | copy-start | bytes 88
  276.2 67.7 %collective-permute-start.18 = (bf16[768,512]{1,0:T(8,128)(2,1)S(1)}, bf16[768,512]{1,0:T(8,128)(2,1)S(1)}, u32[]{:S(2)}, u32[]{:S(2)}) collective-permute-start(bf16[768,512]{1,0:T(8,128)(2,1)S(1)} %constant_dynamic-update-slice_fusion.6.refs_4_), channel_id=1, source_target_pairs={{0,4},{2,6},{4,0},{6,2},{1,5},{3,7},{5,1},{7,3},{8,12},{10,14},{12... | collective-permute-start | bytes 2359304 | tf_op jit(solution)/shard_map/ppermute | solution.py:538
  303.5 41.7 %collective-permute-start.25 = (bf16[768,1024]{1,0:T(8,128)(2,1)}, bf16[768,1024]{1,0:T(8,128)(2,1)S(1)}, u32[]{:S(2)}, u32[]{:S(2)}) collective-permute-start(bf16[768,1024]{1,0:T(8,128)(2,1)} %constant_dynamic-update-slice_fusion.9.refs_4_), channel_id=1, source_target_pairs={{0,2},{2,0},{4,6},{6,4},{1,3},{3,1},{5,7},{7,5},{8,10},{10,8},{12,... | collective-permute-start | bytes 4718600 | tf_op jit(solution)/shard_map/ppermute | solution.py:538
  306.6 39.0 %collective-permute-start.26 = (bf16[768,1024]{1,0:T(8,128)(2,1)}, bf16[768,1024]{1,0:T(8,128)(2,1)}, u32[]{:S(2)}, u32[]{:S(2)}) collective-permute-start(bf16[768,1024]{1,0:T(8,128)(2,1)} %collective-permute-done.24.refs_5_), channel_id=1, source_target_pairs={{0,2},{2,0},{4,6},{6,4},{1,3},{3,1},{5,7},{7,5},{8,10},{10,8},{12,... | collective-permute-start | bytes 4718600 | tf_op jit(solution)/shard_map/ppermute | solution.py:538
  319.8 48.9 %collective-permute-start.19 = (bf16[768,512]{1,0:T(8,128)(2,1)S(1)}, bf16[768,512]{1,0:T(8,128)(2,1)S(1)}, u32[]{:S(2)}, u32[]{:S(2)}) collective-permute-start(bf16[768,512]{1,0:T(8,128)(2,1)S(1)} %constant_dynamic-update-slice_fusion.6.refs_4_), channel_id=1, source_target_pairs={{0,2},{2,0},{4,6},{6,4},{1,3},{3,1},{5,7},{7,5},{8,10},{10,8},{12,... | collective-permute-start | bytes 2359304 | tf_op jit(solution)/shard_map/ppermute | solution.py:538
  320.3 24.0 %collective-permute-start.12 = (bf16[768,512]{1,0:T(8,128)(2,1)S(1)}, bf16[768,512]{1,0:T(8,128)(2,1)S(1)}, u32[]{:S(2)}, u32[]{:S(2)}) collective-permute-start(bf16[768,512]{1,0:T(8,128)(2,1)S(1)} %constant_dynamic-update-slice_fusion.3.refs_4_), channel_id=1, source_target_pairs={{0,4},{2,6},{4,0},{6,2},{1,5},{3,7},{5,1},{7,3},{8,12},{10,14},{12... | collective-permute-start | bytes 2359304 | tf_op jit(solution)/shard_map/ppermute | solution.py:538
  343.9 38.9 %collective-permute-start.13 = (bf16[768,512]{1,0:T(8,128)(2,1)S(1)}, bf16[768,512]{1,0:T(8,128)(2,1)S(1)}, u32[]{:S(2)}, u32[]{:S(2)}) collective-permute-start(bf16[768,512]{1,0:T(8,128)(2,1)S(1)} %constant_dynamic-update-slice_fusion.3.refs_4_), channel_id=1, source_target_pairs={{0,2},{2,0},{4,6},{6,4},{1,3},{3,1},{5,7},{7,5},{8,10},{10,8},{12,... | collective-permute-start | bytes 2359304 | tf_op jit(solution)/shard_map/ppermute | solution.py:538
  344.3 24.9 %collective-permute-start.6 = (bf16[768,512]{1,0:T(8,128)(2,1)S(1)}, bf16[768,512]{1,0:T(8,128)(2,1)S(1)}, u32[]{:S(2)}, u32[]{:S(2)}) collective-permute-start(bf16[768,512]{1,0:T(8,128)(2,1)S(1)} %constant_dynamic-update-slice_fusion.refs_4_), channel_id=1, source_target_pairs={{0,4},{2,6},{4,0},{6,2},{1,5},{3,7},{5,1},{7,3},{8,12},{10,14},{12... | collective-permute-start | bytes 2359304 | tf_op jit(solution)/shard_map/ppermute | solution.py:538
  345.2 24.1 %collective-permute-start.20 = (bf16[768,512]{1,0:T(8,128)(2,1)S(1)}, bf16[768,512]{1,0:T(8,128)(2,1)S(1)}, u32[]{:S(2)}, u32[]{:S(2)}) collective-permute-start(bf16[768,512]{1,0:T(8,128)(2,1)S(1)} %collective-permute-done.18.refs_5_), channel_id=1, source_target_pairs={{0,2},{2,0},{4,6},{6,4},{1,3},{3,1},{5,7},{7,5},{8,10},{10,8},{12,... | collective-permute-start | bytes 2359304 | tf_op jit(solution)/shard_map/ppermute | solution.py:538
  345.6 37.2 %collective-permute-start.14 = (bf16[768,512]{1,0:T(8,128)(2,1)S(1)}, bf16[768,512]{1,0:T(8,128)(2,1)S(1)}, u32[]{:S(2)}, u32[]{:S(2)}) collective-permute-start(bf16[768,512]{1,0:T(8,128)(2,1)S(1)} %collective-permute-done.12.refs_5_), channel_id=1, source_target_pairs={{0,2},{2,0},{4,6},{6,4},{1,3},{3,1},{5,7},{7,5},{8,10},{10,8},{12,... | collective-permute-start | bytes 2359304 | tf_op jit(solution)/shard_map/ppermute | solution.py:538
  345.7 23.6 %copy-start.1 = (bf16[256,4096]{1,0:T(8,128)(2,1)S(1)}, bf16[256,4096]{1,0:T(8,128)(2,1)}, u32[]{:S(2)}) copy-start(bf16[256,4096]{1,0:T(8,128)(2,1)} %get-tuple-element.36.refs_0_) | copy-start | bytes 6291460
  368.7 27.5 %collective-permute-start.7 = (bf16[768,512]{1,0:T(8,128)(2,1)S(1)}, bf16[768,512]{1,0:T(8,128)(2,1)S(1)}, u32[]{:S(2)}, u32[]{:S(2)}) collective-permute-start(bf16[768,512]{1,0:T(8,128)(2,1)S(1)} %constant_dynamic-update-slice_fusion.refs_4_), channel_id=1, source_target_pairs={{0,2},{2,0},{4,6},{6,4},{1,3},{3,1},{5,7},{7,5},{8,10},{10,8},{12,... | collective-permute-start | bytes 2359304 | tf_op jit(solution)/shard_map/ppermute | solution.py:538
  369.2 27.0 %collective-permute-start.8 = (bf16[768,512]{1,0:T(8,128)(2,1)S(1)}, bf16[768,512]{1,0:T(8,128)(2,1)S(1)}, u32[]{:S(2)}, u32[]{:S(2)}) collective-permute-start(bf16[768,512]{1,0:T(8,128)(2,1)S(1)} %collective-permute-done.6.refs_5_), channel_id=1, source_target_pairs={{0,2},{2,0},{4,6},{6,4},{1,3},{3,1},{5,7},{7,5},{8,10},{10,8},{12,... | collective-permute-start | bytes 2359304 | tf_op jit(solution)/shard_map/ppermute | solution.py:538
